TPU v7x, 512 devices: a whole 4x8x8 slice. The times are simulated.
512 devices in a mesh: ma: 64 (over x, y, core), freq: 8 (over z).
Axes of the slice: x: 4, y: 8, z: 8, core: 2. Of those that a mesh axis runs over, the one named last changes fastest.
Arguments:
- timestream: bfloat16 [32, 128, 8, 2048], P('freq', 'ma'), may hold values from -6 to 6
- beam_transfer: bfloat16 [64, 2048, 896], P('ma'), may hold values from -0.1875 to 0.1875
- chromatic_gain: float32 [32, 896], P('freq'), may hold values from 0.5 to 2
- noise_weight: float32 [32, 64, 2048], P('freq', 'ma'), may hold values from 0.25 to 4.5
- prior_diagonal: float32 [32, 896], P('freq'), may hold values from 0.3 to 3
- prior_modes: float32 [32, 2, 896], P('freq'), may hold values from -3 to 3
Outputs:
- sky_estimate: float32 [32, 64, 8, 896], P('freq', 'ma')
All inputs are finite; a program needn't handle non-finite values.
Results may differ from a plain program's by a relative error of at most 0.015.
Values may be sent and summed in bfloat16 or wider, within the bound.
A program may use at most 64 MiB of HBM per device.

v0:
```python
import jax
import jax.numpy as jnp
from jax import lax
from jax.sharding import PartitionSpec as P

ITERS = 2


def hartley_table(rows, cols):
    index_m = jnp.arange(rows, dtype=jnp.int32)[:, None]
    index_t = jnp.arange(cols, dtype=jnp.int32)[None, :]
    phase = (index_m * index_t % cols).astype(jnp.float32)
    angle = 2.0 * jnp.pi * phase / cols
    return (jnp.cos(angle) + jnp.sin(angle)) / jnp.sqrt(jnp.float32(cols))


def inner(left, right):
    return jnp.sum(left * right, axis=(0, 1, 3))


def shards(timestream, beam_transfer, chromatic_gain, noise_weight, prior_diagonal, prior_modes):
    spectral_channels = timestream.shape[0]
    device_time_samples = timestream.shape[1]
    noise_realizations = timestream.shape[2]
    antenna_pairs = timestream.shape[3]
    timestream_rows = timestream.reshape(
        spectral_channels, device_time_samples, noise_realizations * antenna_pairs
    )
    gathered = lax.all_to_all(timestream_rows, "ma", split_axis=2, concat_axis=1, tiled=True)
    all_times = gathered.shape[1]
    hartley = hartley_table(all_times // 2, all_times)
    hartley_high = hartley.astype(jnp.bfloat16)
    hartley_low = (hartley - hartley_high.astype(jnp.float32)).astype(jnp.bfloat16)
    mode_high = jnp.einsum(
        "mt,ftc->fmc", hartley_high, gathered, preferred_element_type=jnp.float32
    )
    mode_low = jnp.einsum("mt,ftc->fmc", hartley_low, gathered, preferred_element_type=jnp.float32)
    mode_rows = (mode_high + mode_low).astype(jnp.bfloat16)
    device_mode_count = lax.all_to_all(mode_rows, "ma", split_axis=1, concat_axis=2, tiled=True)
    resident_modes = device_mode_count.shape[1]
    measured_visibility = device_mode_count.reshape(
        spectral_channels, resident_modes, noise_realizations, antenna_pairs
    )
    chroma = chromatic_gain[:, None, None, :]
    diagonal = prior_diagonal[:, None, None, :]
    weighted = (noise_weight[:, :, None, :] * measured_visibility.astype(jnp.float32)).astype(
        jnp.bfloat16
    )
    rhs = chroma * jnp.einsum(
        "fmkb,mbs->fmks", weighted, beam_transfer, preferred_element_type=jnp.float32
    )

    def squared_norm(vector):
        return lax.psum(inner(vector, vector), ("ma", "freq"))

    estimate = jnp.zeros(rhs.shape, jnp.float32)
    residual = rhs
    direction = rhs
    norm_now = squared_norm(residual)
    for turn_index in range(ITERS):
        low = (chroma * direction).astype(jnp.bfloat16)
        seen = jnp.einsum("fmks,mbs->fmkb", low, beam_transfer, preferred_element_type=jnp.float32)
        heard = (noise_weight[:, :, None, :] * seen).astype(jnp.bfloat16)
        back = jnp.einsum(
            "fmkb,mbs->fmks", heard, beam_transfer, preferred_element_type=jnp.float32
        )
        partial_sum = jnp.einsum(
            "frs,fmks->rmks", prior_modes, direction, precision=lax.Precision.HIGHEST
        )
        projection = lax.psum(partial_sum.astype(jnp.bfloat16), "freq").astype(jnp.float32)
        image = (
            chroma * back
            + diagonal * direction
            + jnp.einsum("frs,rmks->fmks", prior_modes, projection, precision=lax.Precision.HIGHEST)
        )
        curve = lax.psum(inner(direction, image), ("ma", "freq"))
        step_size = norm_now / curve
        estimate = estimate + step_size[None, None, :, None] * direction
        if turn_index + 1 < ITERS:
            residual = residual - step_size[None, None, :, None] * image
            norm_next = squared_norm(residual)
            direction = residual + (norm_next / norm_now)[None, None, :, None] * direction
            norm_now = norm_next
    return estimate


def solution(mesh):
    in_specs = (
        P("freq", "ma", None, None),
        P("ma", None, None),
        P("freq", None),
        P("freq", "ma", None),
        P("freq", None),
        P("freq", None, None),
    )
    out_specs = P("freq", "ma", None, None)
    return jax.shard_map(shards, mesh=mesh, in_specs=in_specs, out_specs=out_specs, check_vma=False)
```

profile of v0, /device:TPU:1, one launch (start us, length us, event | category | flops | bytes accessed | tf_op | source)
XLA Modules:
  0.0 502.7 jit_solution(1187688553828649920)
XLA Ops:
  0.0 10.9 %copy.41 = bf16[4,2,8,2048]{0,1,3,2:T(2,128)(2,1)} copy(bf16[4,2,8,2048]{3,2,1,0:T(8,128)(2,1)} %param.6) | data formatting | bytes 524288 | tf_op args[0]
  10.9 16.2 %reshape.94 = bf16[64,2,1024]{2,1,0:T(2,128)(2,1)S(1)} reshape(bf16[16384,2,4]{2,1,0:T(2,128)(2,1)} %bitcast.259) | data formatting | bytes 524288
  27.1 23.4 %all_to_all.27 = bf16[64,2,1024]{2,1,0:T(2,128)(2,1)S(1)} all-to-all(bf16[64,2,1024]{2,1,0:T(2,128)(2,1)S(1)} %reshape.94), channel_id=1, replica_groups=mesh['ma'=64,'freq'=8] {'ma'}, dimensions={0} | all-to-all | bytes 524288 | tf_op jit(solution)/shard_map/all_to_all | solution.py:29
  50.5 19.0 %reshape.95 = bf16[16384,2,4]{2,1,0:T(2,128)(2,1)} reshape(bf16[64,2,1024]{2,1,0:T(2,128)(2,1)S(1)} %all_to_all.27) | data formatting | bytes 524288
  69.5 0.0 copy-start.2
  69.5 0.0 copy-start.3
  69.5 16.9 %copy.42 = bf16[4,2,64,256]{3,1,2,0:T(2,128)(2,1)S(1)} copy(bf16[4,2,64,256]{0,1,3,2:T(2,128)(2,1)} %bitcast.258) | data formatting | bytes 524288 | tf_op jit(solution)/shard_map/all_to_all | solution.py:29
  86.4 0.0 copy-start
  86.4 0.1 all_to_all.23
  86.5 0.3 fusion.118
  86.8 0.3 fusion.41
  87.1 0.7 copy.43
  87.9 6.0 %all-to-all-start.1 = ((bf16[4,64,256]{2,0,1:T(4,128)(2,1)}), bf16[4,64,256]{2,0,1:T(4,128)(2,1)S(1)}, u32[]{:S(2)}, u32[]{:S(2)}) async-start(bf16[4,64,256]{2,0,1:T(4,128)(2,1)} %copy.43), calls=%async_computation.1 | async-start | bytes 262144 | tf_op jit(solution)/shard_map/all_to_all | solution.py:39
  93.9 0.0 copy-done.2
  94.1 0.0 copy-done.3
  94.1 0.9 copy.46
  95.0 9.3 %all-to-all-done.1 = bf16[4,64,256]{2,0,1:T(4,128)(2,1)S(1)} async-done(((bf16[4,64,256]{2,0,1:T(4,128)(2,1)}), bf16[4,64,256]{2,0,1:T(4,128)(2,1)S(1)}, u32[]{:S(2)}, u32[]{:S(2)}) %all-to-all-start.1) | async-done | bytes 131104 | tf_op jit(solution)/shard_map/all_to_all | solution.py:39
  104.3 0.1 convert_element_type.80
  104.4 0.0 copy-done
  104.4 2.7 fusion.90
  107.1 1.2 copy.45
  108.3 6.3 %fusion.38 = bf16[2,8,896]{1,0,2:T(2,128)(2,1)S(1)} fusion(f32[4,8,896]{1,0,2:T(4,128)S(1)} %copy.45, f32[4,2,896]{0,1,2:T(2,128)S(1)} %copy.46), kind=kOutput, calls=%fused_computation.20 | convolution fusion | flops 702464 | bytes 172032 | tf_op jit(solution)/shard_map/frs,fmks->rmks/dot_general | solution.py:67
  114.6 0.0 copy-start.1
  114.6 35.3 %psum.43 = bf16[2,8,896]{1,0,2:T(2,128)(2,1)} all-reduce(bf16[2,8,896]{1,0,2:T(2,128)(2,1)S(1)} %fusion.38), channel_id=1, replica_groups=mesh['ma'=64,'freq'=8] {'freq'}, use_global_device_ids=true, to_apply=%region_2.3 | all-reduce | flops 14336 | bytes 57344 | tf_op jit(solution)/shard_map/psum | solution.py:70
  149.9 4.9 fusion.138
  154.8 1.1 copy.48
  155.9 0.0 copy-done.1
  155.9 5.0 multiply_reduce_fusion.1
  160.9 99.6 %all-reduce = (f32[8]{0:T(128)S(1)}, f32[8]{0:T(128)S(1)}) all-reduce(f32[8]{0:T(128)S(1)} %get-tuple-element.6, f32[8]{0:T(128)S(1)} %get-tuple-element.5), channel_id=1, replica_groups=mesh['ma'=64,'freq'=8] {'ma','freq'}, use_global_device_ids=true, to_apply=%region_1.2 | all-reduce | flops 16 | bytes 128 | tf_op jit(solution)/shard_map/psum | solution.py:54
  260.5 0.2 multiply_reduce_fusion
  260.7 95.0 %psum.45 = f32[8]{0:T(128)S(1)} all-reduce(f32[8]{0:T(128)S(1)} %multiply_reduce_fusion), channel_id=1, replica_groups=mesh['ma'=64,'freq'=8] {'ma','freq'}, use_global_device_ids=true, to_apply=%region_6.7 | all-reduce | flops 8 | bytes 64 | tf_op jit(solution)/shard_map/psum | solution.py:54
  355.8 0.1 fusion.133
  355.9 1.2 copy.49
  357.1 7.1 %fusion.39 = bf16[2,8,896]{1,0,2:T(2,128)(2,1)} fusion(f32[4,8,896]{1,0,2:T(4,128)S(1)} %copy.49, f32[4,2,896]{0,1,2:T(2,128)S(1)} %copy.46), kind=kOutput, calls=%fused_computation.21 | convolution fusion | flops 702464 | bytes 172032 | tf_op jit(solution)/shard_map/frs,fmks->rmks/dot_general | solution.py:67
  364.2 28.2 %psum.46 = bf16[2,8,896]{1,0,2:T(2,128)(2,1)S(1)} all-reduce(bf16[2,8,896]{1,0,2:T(2,128)(2,1)} %fusion.39), channel_id=1, replica_groups=mesh['ma'=64,'freq'=8] {'freq'}, use_global_device_ids=true, to_apply=%region_7.8 | all-reduce | flops 14336 | bytes 57344 | tf_op jit(solution)/shard_map/psum | solution.py:70
  392.3 3.7 fusion.139
  396.1 1.1 copy.52
  397.2 5.0 fusion.93
  402.2 99.8 %psum.47 = f32[8]{0:T(128)S(1)} all-reduce(f32[8]{0:T(128)S(1)} %fusion.93), channel_id=1, replica_groups=mesh['ma'=64,'freq'=8] {'ma','freq'}, use_global_device_ids=true, to_apply=%region_9.10 | all-reduce | flops 8 | bytes 64 | tf_op jit(solution)/shard_map/psum | solution.py:76
  502.0 0.8 add_bitcast_fusion
  (7 shorter events, 0.1 us)
Async XLA Ops:
  69.5 24.4 %copy-start.2 = (f32[4,1,2048]{2,1,0:T(1,128)S(1)}, f32[4,1,2048]{2,1,0:T(1,128)}, u32[]{:S(2)}) copy-start(f32[4,1,2048]{2,1,0:T(1,128)} %param.9) | copy-start | bytes 98308
  69.5 24.5 %copy-start.3 = (f32[4,2,896]{2,1,0:T(2,128)S(1)}, f32[4,2,896]{2,1,0:T(2,128)}, u32[]{:S(2)}) copy-start(f32[4,2,896]{2,1,0:T(2,128)} %param.11) | copy-start | bytes 86020
  86.4 18.0 %copy-start = (f32[4,896]{1,0:T(4,128)S(1)}, f32[4,896]{1,0:T(4,128)}, u32[]{:S(2)}) copy-start(f32[4,896]{1,0:T(4,128)} %param.8) | copy-start | bytes 43012
  87.9 16.4 %all-to-all-start.1 = ((bf16[4,64,256]{2,0,1:T(4,128)(2,1)}), bf16[4,64,256]{2,0,1:T(4,128)(2,1)S(1)}, u32[]{:S(2)}, u32[]{:S(2)}) async-start(bf16[4,64,256]{2,0,1:T(4,128)(2,1)} %copy.43), calls=%async_computation.1 | async-start | bytes 262144 | tf_op jit(solution)/shard_map/all_to_all | solution.py:39
  114.6 41.3 %copy-start.1 = (f32[4,896]{1,0:T(4,128)S(1)}, f32[4,896]{1,0:T(4,128)}, u32[]{:S(2)}) copy-start(f32[4,896]{1,0:T(4,128)} %param.10) | copy-start | bytes 43012
where the time goes:
time: 504 us; the launch traced here: 503 us
  blocking collectives  381 us (76%)
  local copies, waits for them, and re-layouts  69.5 us (14%)
  matrix products  35.2 us (7%)
  waiting for transfers between devices  9.29 us (2%)
  starting transfers between devices  6.04 us (1%)
    psum x2, blocking collectives, squared_norm(): return lax.psum(inner(vector, vector), ('ma', 'freq'))  195 us
    psum x1, blocking collectives, shards(): curve = lax.psum(inner(direction, image), ('ma', 'freq'))  99.8 us
    psum x2, blocking collectives, shards(): lax.psum(partial_sum.astype(jnp.bfloat16), 'freq').astype(jnp.float32)  63.4 us
    unnamed x13, local copies, waits for them, and re-layouts  47.1 us
    all_to_all x1, blocking collectives, shards(): lax.all_to_all(timestream_rows, 'ma', split_axis=2, concat_axis=1, tiled=...  23.4 us
    all_to_all x2, local copies, waits for them, and re-layouts, shards(): lax.all_to_all(timestream_rows, 'ma', split_axis=2, concat_axis=1, tiled=...  17 us
    dot_general x2, matrix products, shards(): jnp.einsum('frs,fmks->rmks', prior_modes, direction, precision=lax.Precis...  13.4 us
  transfers between devices with their start and end apart: 1, of which 1 were waited for; matrix products, arithmetic and copies ran while one was open for 0% of the time, Pallas kernels for 0%

commit v1 on v0

v1 whole, which is shorter than its diff:
```python
import functools

import jax
import jax.numpy as jnp
from jax import lax
from jax.experimental import pallas as pl
from jax.experimental.pallas import tpu as pltpu
from jax.sharding import PartitionSpec as P

ITERS = 2
MESH = pl.DeviceIdType.MESH


def hartley_table(rows, cols):
    index_m = jnp.arange(rows, dtype=jnp.int32)[:, None]
    index_t = jnp.arange(cols, dtype=jnp.int32)[None, :]
    phase = (index_m * index_t % cols).astype(jnp.float32)
    angle = 2.0 * jnp.pi * phase / cols
    return (jnp.cos(angle) + jnp.sin(angle)) / jnp.sqrt(jnp.float32(cols))


def inner(left, right):
    return jnp.sum(left * right, axis=(0, 1, 3))


def reduce_kernel(axis_names, stages, x_ref, o_ref, cur, recv, send_sem, recv_sem):
    me = {name: lax.axis_index(name) for name in axis_names}

    def device(axis, coord):
        return tuple(coord if name == axis else me[name] for name in axis_names)

    plan = []
    base = 0
    for axis, stride, size in stages:
        own = (me[axis] // stride) % size
        root = me[axis] - own * stride
        peers = []
        for step in range(1, size):
            other = lax.rem(own + step, size)
            peers.append((other, device(axis, root + other * stride)))
        plan.append((base, own, size, peers))
        base += size

    barrier = pltpu.get_barrier_semaphore()
    for _, _, _, peers in plan:
        for _, peer in peers:
            pl.semaphore_signal(barrier, 1, device_id=peer, device_id_type=MESH)
    pl.semaphore_wait(barrier, sum(len(peers) for _, _, _, peers in plan))

    acc = x_ref[...].astype(jnp.float32)
    for index, (base, own, size, peers) in enumerate(plan):
        cur[index] = acc.astype(cur.dtype)
        copies = []
        for other, peer in peers:
            copy = pltpu.make_async_remote_copy(
                src_ref=cur.at[index],
                dst_ref=recv.at[base + own],
                send_sem=send_sem.at[base + other],
                recv_sem=recv_sem.at[base + own],
                device_id=peer,
                device_id_type=MESH,
            )
            copy.start()
            copies.append(copy)
        recv[base + own] = acc.astype(recv.dtype)
        for other, peer in peers:
            pltpu.make_async_remote_copy(
                src_ref=cur.at[index],
                dst_ref=recv.at[base + other],
                send_sem=send_sem.at[base + other],
                recv_sem=recv_sem.at[base + other],
                device_id=peer,
                device_id_type=MESH,
            ).wait_recv()
        for copy in copies:
            copy.wait_send()
        total = recv[base].astype(jnp.float32)
        for slot in range(1, size):
            total = total + recv[base + slot].astype(jnp.float32)
        acc = total
    o_ref[...] = acc.astype(o_ref.dtype)


def group_sum(x, axis_names, stages, wire_dtype, collective_id):
    slots = sum(size for _, _, size in stages)
    return pl.pallas_call(
        functools.partial(reduce_kernel, axis_names, stages),
        out_shape=jax.ShapeDtypeStruct(x.shape, jnp.float32),
        in_specs=[pl.BlockSpec(memory_space=pltpu.VMEM)],
        out_specs=pl.BlockSpec(memory_space=pltpu.VMEM),
        scratch_shapes=[
            pltpu.VMEM((len(stages),) + x.shape, wire_dtype),
            pltpu.VMEM((slots,) + x.shape, wire_dtype),
            pltpu.SemaphoreType.DMA((slots,)),
            pltpu.SemaphoreType.DMA((slots,)),
        ],
        compiler_params=pltpu.CompilerParams(collective_id=collective_id, has_side_effects=True),
    )(x)


def make_shards(mesh):
    axis_names = tuple(mesh.axis_names)
    mode_devices = mesh.shape["ma"]
    freq_devices = mesh.shape["freq"]
    if mode_devices % 16 == 0:
        mode_stages = [("ma", 1, 2), ("ma", 2, 8), ("ma", 16, mode_devices // 16)]
    else:
        mode_stages = [("ma", 1, mode_devices)]
    global_stages = mode_stages + [("freq", 1, freq_devices)]
    freq_stages = [("freq", 1, freq_devices)]

    def scalar_sum(*vectors):
        rows = jnp.stack(vectors)
        padded = jnp.pad(rows, ((0, 8 - rows.shape[0]), (0, 128 - rows.shape[1])))
        summed = group_sum(padded, axis_names, global_stages, jnp.float32, 2)
        return [summed[index, : rows.shape[1]] for index in range(len(vectors))]

    def freq_sum(partial_sum):
        shape = partial_sum.shape
        flat = partial_sum.reshape(-1, shape[-1])
        summed = group_sum(flat, axis_names, freq_stages, jnp.bfloat16, 1)
        return summed.reshape(shape)

    def shards(timestream, beam_transfer, chromatic_gain, noise_weight, prior_diagonal, prior_modes):
        spectral_channels = timestream.shape[0]
        device_time_samples = timestream.shape[1]
        noise_realizations = timestream.shape[2]
        antenna_pairs = timestream.shape[3]
        timestream_rows = timestream.reshape(
            spectral_channels, device_time_samples, noise_realizations * antenna_pairs
        )
        gathered = lax.all_to_all(timestream_rows, "ma", split_axis=2, concat_axis=1, tiled=True)
        all_times = gathered.shape[1]
        hartley = hartley_table(all_times // 2, all_times)
        hartley_high = hartley.astype(jnp.bfloat16)
        hartley_low = (hartley - hartley_high.astype(jnp.float32)).astype(jnp.bfloat16)
        mode_high = jnp.einsum(
            "mt,ftc->fmc", hartley_high, gathered, preferred_element_type=jnp.float32
        )
        mode_low = jnp.einsum("mt,ftc->fmc", hartley_low, gathered, preferred_element_type=jnp.float32)
        mode_rows = (mode_high + mode_low).astype(jnp.bfloat16)
        device_mode_count = lax.all_to_all(mode_rows, "ma", split_axis=1, concat_axis=2, tiled=True)
        resident_modes = device_mode_count.shape[1]
        measured_visibility = device_mode_count.reshape(
            spectral_channels, resident_modes, noise_realizations, antenna_pairs
        )
        chroma = chromatic_gain[:, None, None, :]
        diagonal = prior_diagonal[:, None, None, :]
        weighted = (noise_weight[:, :, None, :] * measured_visibility.astype(jnp.float32)).astype(
            jnp.bfloat16
        )
        rhs = chroma * jnp.einsum(
            "fmkb,mbs->fmks", weighted, beam_transfer, preferred_element_type=jnp.float32
        )

        estimate = jnp.zeros(rhs.shape, jnp.float32)
        residual = rhs
        direction = rhs
        norm_now = None
        for turn_index in range(ITERS):
            low = (chroma * direction).astype(jnp.bfloat16)
            seen = jnp.einsum("fmks,mbs->fmkb", low, beam_transfer, preferred_element_type=jnp.float32)
            heard = (noise_weight[:, :, None, :] * seen).astype(jnp.bfloat16)
            back = jnp.einsum(
                "fmkb,mbs->fmks", heard, beam_transfer, preferred_element_type=jnp.float32
            )
            partial_sum = jnp.einsum(
                "frs,fmks->rmks", prior_modes, direction, precision=lax.Precision.HIGHEST
            )
            projection = freq_sum(partial_sum)
            image = (
                chroma * back
                + diagonal * direction
                + jnp.einsum("frs,rmks->fmks", prior_modes, projection, precision=lax.Precision.HIGHEST)
            )
            if norm_now is None:
                norm_now, curve = scalar_sum(inner(residual, residual), inner(direction, image))
            else:
                (curve,) = scalar_sum(inner(direction, image))
            step_size = norm_now / curve
            estimate = estimate + step_size[None, None, :, None] * direction
            if turn_index + 1 < ITERS:
                residual = residual - step_size[None, None, :, None] * image
                (norm_next,) = scalar_sum(inner(residual, residual))
                direction = residual + (norm_next / norm_now)[None, None, :, None] * direction
                norm_now = norm_next
        return estimate

    return shards


def solution(mesh):
    in_specs = (
        P("freq", "ma", None, None),
        P("ma", None, None),
        P("freq", None),
        P("freq", "ma", None),
        P("freq", None),
        P("freq", None, None),
    )
    out_specs = P("freq", "ma", None, None)
    return jax.shard_map(make_shards(mesh), mesh=mesh, in_specs=in_specs, out_specs=out_specs, check_vma=False)
```

time: 504 us -> 256 us (0.51)
  blocking collectives: 381 us -> 23.4 us
  Pallas kernels: 0 us -> 87.4 us
  matrix products: 35.2 us -> 44.9 us
  local copies, waits for them, and re-layouts: 69.5 us -> 78.6 us
    psum x5 -> x0, blocking collectives: 358 us -> none  [the longest x2 195 us: squared_norm(): return lax.psum(inner(vector, vector), ('ma', 'freq'))]
    pallas_call x0 -> x5, Pallas kernels: none -> 87.4 us  [group_sum(): pl.pallas_call(functools.partial(reduce_kernel, axis_names, stages), out_...]
    dot_general x2, matrix products: 8.61 us -> 17.1 us  [shards(): jnp.einsum('frs,rmks->fmks', prior_modes, projection, precision=lax.Preci...]
where the time goes in v1:
time: 256 us; the launch traced here: 254 us
  Pallas kernels  87.4 us (34%)
  local copies, waits for them, and re-layouts  78.6 us (31%)
  matrix products  44.9 us (18%)
  blocking collectives  23.4 us (9%)
  waiting for transfers between devices  9.29 us (4%)
  starting transfers between devices  6.04 us (2%)
  other arithmetic  3.84 us (2%)
    pallas_call x5, Pallas kernels, group_sum(): pl.pallas_call(functools.partial(reduce_kernel, axis_names, stages), out_...  87.4 us
    unnamed x13, local copies, waits for them, and re-layouts  47.1 us
    all_to_all x1, blocking collectives, shards(): lax.all_to_all(timestream_rows, 'ma', split_axis=2, concat_axis=1, tiled=...  23.4 us
    dot_general x2, matrix products, shards(): jnp.einsum('frs,rmks->fmks', prior_modes, projection, precision=lax.Preci...  17.1 us
    all_to_all x2, local copies, waits for them, and re-layouts, shards(): lax.all_to_all(timestream_rows, 'ma', split_axis=2, concat_axis=1, tiled=...  17 us
    dot_general x2, matrix products, shards(): jnp.einsum('frs,fmks->rmks', prior_modes, direction, precision=lax.Precis...  14.6 us
    dot_general x2, matrix products, shards(): jnp.einsum('fmkb,mbs->fmks', heard, beam_transfer, preferred_element_type...  9.99 us
    all_to_all x1, waiting for transfers between devices, shards(): lax.all_to_all(mode_rows, 'ma', split_axis=1, concat_axis=2, tiled=True)  9.29 us
  transfers between devices with their start and end apart: 1, of which 1 were waited for; matrix products, arithmetic and copies ran while one was open for 0% of the time, Pallas kernels for 0%

profile of v1, /device:TPU:1, one launch (start us, length us, event | category | flops | bytes accessed | tf_op | source)
XLA Modules:
  0.0 253.8 jit_solution(15700989188380397150)
XLA Ops:
  0.0 10.9 %copy.53 = bf16[4,2,8,2048]{0,1,3,2:T(2,128)(2,1)} copy(bf16[4,2,8,2048]{3,2,1,0:T(8,128)(2,1)} %param.6) | data formatting | bytes 524288 | tf_op args[0]
  10.9 16.2 %reshape.131 = bf16[64,2,1024]{2,1,0:T(2,128)(2,1)S(1)} reshape(bf16[16384,2,4]{2,1,0:T(2,128)(2,1)} %bitcast.269) | data formatting | bytes 524288
  27.1 23.4 %all_to_all.27 = bf16[64,2,1024]{2,1,0:T(2,128)(2,1)S(1)} all-to-all(bf16[64,2,1024]{2,1,0:T(2,128)(2,1)S(1)} %reshape.131), channel_id=1, replica_groups=mesh['ma'=64,'freq'=8] {'ma'}, dimensions={0} | all-to-all | bytes 524288 | tf_op jit(solution)/shard_map/all_to_all | solution.py:132
  50.5 19.0 %reshape.132 = bf16[16384,2,4]{2,1,0:T(2,128)(2,1)} reshape(bf16[64,2,1024]{2,1,0:T(2,128)(2,1)S(1)} %all_to_all.27) | data formatting | bytes 524288
  69.5 0.0 copy-start.2
  69.5 0.0 copy-start.3
  69.5 16.9 %copy.54 = bf16[4,2,64,256]{3,1,2,0:T(2,128)(2,1)S(1)} copy(bf16[4,2,64,256]{0,1,3,2:T(2,128)(2,1)} %bitcast.268) | data formatting | bytes 524288 | tf_op jit(solution)/shard_map/all_to_all | solution.py:132
  86.4 0.0 copy-start
  86.4 0.1 all_to_all.23
  86.5 0.3 fusion.116
  86.8 0.3 fusion.39
  87.1 0.7 copy.55
  87.9 6.0 %all-to-all-start.1 = ((bf16[4,64,256]{2,0,1:T(4,128)(2,1)}), bf16[4,64,256]{2,0,1:T(4,128)(2,1)S(1)}, u32[]{:S(2)}, u32[]{:S(2)}) async-start(bf16[4,64,256]{2,0,1:T(4,128)(2,1)} %copy.55), calls=%async_computation.1 | async-start | bytes 262144 | tf_op jit(solution)/shard_map/all_to_all | solution.py:142
  93.9 0.0 copy-done.2
  94.1 0.0 copy-done.3
  94.1 0.9 copy.58
  95.0 9.3 %all-to-all-done.1 = bf16[4,64,256]{2,0,1:T(4,128)(2,1)S(1)} async-done(((bf16[4,64,256]{2,0,1:T(4,128)(2,1)}), bf16[4,64,256]{2,0,1:T(4,128)(2,1)S(1)}, u32[]{:S(2)}, u32[]{:S(2)}) %all-to-all-start.1) | async-done | bytes 131104 | tf_op jit(solution)/shard_map/all_to_all | solution.py:142
  104.3 0.1 convert_element_type.65
  104.4 0.0 copy-done
  104.4 2.7 %fusion.88 = f32[4,1,8,896]{3,2,0,1:T(8,128)S(1)} fusion(bf16[4,8,2048]{2,1,0:T(8,128)(2,1)S(1)} %convert_element_type.65, bf16[1,2048,896]{2,1,0:T(8,128)(2,1)} %param.7, f32[4,896]{1,0:T(4,128)S(1)} %copy-done), kind=kOutput, calls=%fused_computation.33 | convolution fusion | flops 117469184 | bytes 3930112 | tf_op jit(solution)/shard_map/fmkb,mbs->fmks/dot_general | solution.py:152
  107.1 1.2 copy.57
  108.3 7.2 %convolution_bitcast_fusion.1 = f32[2,1,8,896]{2,0,3,1:T(2,128)} fusion(f32[4,8,896]{1,0,2:T(4,128)S(1)} %copy.57, f32[4,2,896]{0,1,2:T(2,128)S(1)} %copy.58), kind=kOutput, calls=%fused_computation.19 | convolution fusion | flops 688128 | bytes 200704 | tf_op jit(solution)/shard_map/frs,fmks->rmks/dot_general | solution.py:167
  115.5 0.0 copy-start.1
  115.5 2.0 copy.59
  117.5 16.8 %shard_map.64 = f32[16,896]{1,0:T(8,128)} custom-call(f32[16,896]{1,0:T(8,128)} %bitcast.275), custom_call_target="tpu_custom_call" | custom-call | tf_op jit(solution)/shard_map/pallas_call | solution.py:86
  134.3 1.9 copy.60
  136.3 8.5 %fusion.138 = f32[896,8,4]{1,2,0:T(4,128)S(1)} fusion(f32[2,8,896]{1,0,2:T(2,128)} %copy.60, f32[4,2,896]{0,1,2:T(2,128)S(1)} %copy.58), kind=kOutput, calls=%fused_computation.85 | convolution fusion | flops 688128 | bytes 200704 | tf_op jit(solution)/shard_map/frs,rmks->fmks/dot_general | solution.py:174
  144.8 1.1 copy.62
  145.9 0.0 copy-done.1
  146.0 5.0 %multiply_reduce_fusion.2 = (f32[8]{0:T(128)S(1)}, f32[8]{0:T(128)S(1)}, f32[4,1,8,896]{3,2,0,1:T(8,128)S(1)}) fusion(f32[4,1,8,896]{3,2,0,1:T(8,128)S(1)} %fusion.88, f32[896,8,4]{0,1,2:T(8,128)S(1)} %copy.62, f32[4,896]{1,0:T(4,128)S(1)} %copy-done.1, bf16[1,2048,896]{2,1,0:T(8,128)(2,1)} %param.7, f32[4,2048]{1,0:T(4,128)S(1)} %bitcast.273, ...), kind=kOutput, calls=%fused_computation.45 | convolution fusion | flops 235298816 | bytes 4075584 | tf_op jit(solution)/shard_map/fmkb,mbs->fmks/dot_general | solution.py:164
  151.0 0.6 select_maximum_fusion.x_ref
  151.6 19.7 %shard_map.65 = f32[8,128]{1,0:T(8,128)} custom-call(f32[8,128]{1,0:T(8,128)} %select_maximum_fusion.x_ref), custom_call_target="tpu_custom_call" | custom-call | tf_op jit(solution)/shard_map/pallas_call | solution.py:86
  171.3 0.8 fusion.121
  172.1 0.2 multiply_reduce_fusion
  172.3 0.6 pad.12.x_ref
  172.9 19.0 %shard_map.66 = f32[8,128]{1,0:T(8,128)} custom-call(f32[8,128]{1,0:T(8,128)} %pad.12.x_ref), custom_call_target="tpu_custom_call" | custom-call | tf_op jit(solution)/shard_map/pallas_call | solution.py:86
  191.9 0.7 divide_bitcast_fusion
  192.6 0.1 fusion.133
  192.7 1.2 copy.63
  193.9 7.4 %convolution_bitcast_fusion = f32[2,1,8,896]{2,0,3,1:T(2,128)} fusion(f32[4,8,896]{1,0,2:T(4,128)S(1)} %copy.63, f32[4,2,896]{0,1,2:T(2,128)S(1)} %copy.58), kind=kOutput, calls=%fused_computation.18 | convolution fusion | flops 688128 | bytes 200704 | tf_op jit(solution)/shard_map/frs,fmks->rmks/dot_general | solution.py:167
  201.3 2.0 copy.65
  203.3 10.7 %shard_map.67 = f32[16,896]{1,0:T(8,128)} custom-call(f32[16,896]{1,0:T(8,128)} %bitcast.277), custom_call_target="tpu_custom_call" | custom-call | tf_op jit(solution)/shard_map/pallas_call | solution.py:86
  214.1 1.9 copy.66
  216.0 8.5 %fusion.139 = f32[896,8,4]{1,2,0:T(4,128)S(1)} fusion(f32[2,8,896]{1,0,2:T(2,128)} %copy.66, f32[4,2,896]{0,1,2:T(2,128)S(1)} %copy.58), kind=kOutput, calls=%fused_computation.86 | convolution fusion | flops 688128 | bytes 200704 | tf_op jit(solution)/shard_map/frs,rmks->fmks/dot_general | solution.py:174
  224.6 1.1 copy.68
  225.7 5.0 %fusion.91 = f32[8]{0:T(128)S(1)} fusion(bf16[1,2048,896]{2,1,0:T(8,128)(2,1)} %param.7, f32[4,2048]{1,0:T(4,128)S(1)} %bitcast.274, f32[896,8,4]{0,1,2:T(8,128)S(1)} %copy.68, f32[4,896]{1,0:T(4,128)S(1)} %copy-done.1, f32[4,896]{1,0:T(4,128)S(1)} %copy-done, f32[4,1,8,896]{3,2,0,1:T(8,128)S(1)} %fusion.88, f32[8]{0:T(128)S(1)} %divide_bitcast_fusion, ...), kind=kOutput, calls=%fused_computation.34 | convolution fusion | flops 235470848 | bytes 4075616 | tf_op jit(solution)/shard_map/fmkb,mbs->fmks/dot_general | solution.py:164
  230.7 0.6 pad.13.x_ref
  231.3 21.1 %shard_map.68 = f32[8,128]{1,0:T(8,128)} custom-call(f32[8,128]{1,0:T(8,128)} %pad.13.x_ref), custom_call_target="tpu_custom_call" | custom-call | tf_op jit(solution)/shard_map/pallas_call | solution.py:86
  252.4 0.7 fusion.122
  253.1 0.7 add_bitcast_fusion
  (4 shorter events, 0.1 us)
Async XLA Ops:
  69.5 24.4 %copy-start.2 = (f32[4,1,2048]{2,1,0:T(1,128)S(1)}, f32[4,1,2048]{2,1,0:T(1,128)}, u32[]{:S(2)}) copy-start(f32[4,1,2048]{2,1,0:T(1,128)} %param.9) | copy-start | bytes 98308
  69.5 24.5 %copy-start.3 = (f32[4,2,896]{2,1,0:T(2,128)S(1)}, f32[4,2,896]{2,1,0:T(2,128)}, u32[]{:S(2)}) copy-start(f32[4,2,896]{2,1,0:T(2,128)} %param.11) | copy-start | bytes 86020
  86.4 18.0 %copy-start = (f32[4,896]{1,0:T(4,128)S(1)}, f32[4,896]{1,0:T(4,128)}, u32[]{:S(2)}) copy-start(f32[4,896]{1,0:T(4,128)} %param.8) | copy-start | bytes 43012
  87.9 16.4 %all-to-all-start.1 = ((bf16[4,64,256]{2,0,1:T(4,128)(2,1)}), bf16[4,64,256]{2,0,1:T(4,128)(2,1)S(1)}, u32[]{:S(2)}, u32[]{:S(2)}) async-start(bf16[4,64,256]{2,0,1:T(4,128)(2,1)} %copy.55), calls=%async_computation.1 | async-start | bytes 262144 | tf_op jit(solution)/shard_map/all_to_all | solution.py:142
  115.5 30.5 %copy-start.1 = (f32[4,896]{1,0:T(4,128)S(1)}, f32[4,896]{1,0:T(4,128)}, u32[]{:S(2)}) copy-start(f32[4,896]{1,0:T(4,128)} %param.10) | copy-start | bytes 43012

commit v2 on v1

--- a/solution.py
+++ b/solution.py
@@ -126,22 +126,33 @@
         device_time_samples = timestream.shape[1]
         noise_realizations = timestream.shape[2]
         antenna_pairs = timestream.shape[3]
-        timestream_rows = timestream.reshape(
-            spectral_channels, device_time_samples, noise_realizations * antenna_pairs
-        )
-        gathered = lax.all_to_all(timestream_rows, "ma", split_axis=2, concat_axis=1, tiled=True)
-        all_times = gathered.shape[1]
+        mode_devices_here = mode_devices
+        columns = noise_realizations * antenna_pairs // mode_devices_here
+        blocks = antenna_pairs // columns
+        halves = columns // 128
+        send = timestream.reshape(
+            spectral_channels, device_time_samples, noise_realizations, blocks, halves, 128
+        ).transpose(2, 3, 0, 1, 4, 5)
+        send = send.reshape(mode_devices_here, spectral_channels * device_time_samples * halves, 128)
+        received = lax.all_to_all(send, "ma", 0, 0, tiled=True)
+        received = received.reshape(mode_devices_here, spectral_channels, device_time_samples, columns)
+        all_times = mode_devices_here * device_time_samples
         hartley = hartley_table(all_times // 2, all_times)
         hartley_high = hartley.astype(jnp.bfloat16)
         hartley_low = (hartley - hartley_high.astype(jnp.float32)).astype(jnp.bfloat16)
+        hartley_high = hartley_high.reshape(all_times // 2, mode_devices_here, device_time_samples)
+        hartley_low = hartley_low.reshape(all_times // 2, mode_devices_here, device_time_samples)
         mode_high = jnp.einsum(
-            "mt,ftc->fmc", hartley_high, gathered, preferred_element_type=jnp.float32
-        )
-        mode_low = jnp.einsum("mt,ftc->fmc", hartley_low, gathered, preferred_element_type=jnp.float32)
+            "mit,iftc->mfc", hartley_high, received, preferred_element_type=jnp.float32
+        )
+        mode_low = jnp.einsum("mit,iftc->mfc", hartley_low, received, preferred_element_type=jnp.float32)
         mode_rows = (mode_high + mode_low).astype(jnp.bfloat16)
-        device_mode_count = lax.all_to_all(mode_rows, "ma", split_axis=1, concat_axis=2, tiled=True)
-        resident_modes = device_mode_count.shape[1]
-        measured_visibility = device_mode_count.reshape(
+        back_rows = lax.all_to_all(mode_rows, "ma", 0, 0, tiled=True)
+        resident_modes = back_rows.shape[0] // mode_devices_here
+        back_rows = back_rows.reshape(
+            noise_realizations, blocks, resident_modes, spectral_channels, columns
+        )
+        measured_visibility = back_rows.transpose(3, 2, 0, 1, 4).reshape(
             spectral_channels, resident_modes, noise_realizations, antenna_pairs
         )
         chroma = chromatic_gain[:, None, None, :]
@@ -164,14 +175,12 @@
             back = jnp.einsum(
                 "fmkb,mbs->fmks", heard, beam_transfer, preferred_element_type=jnp.float32
             )
-            partial_sum = jnp.einsum(
-                "frs,fmks->rmks", prior_modes, direction, precision=lax.Precision.HIGHEST
-            )
+            partial_sum = jnp.sum(prior_modes[:, :, None, None, :] * direction[:, None], axis=0)
             projection = freq_sum(partial_sum)
             image = (
                 chroma * back
                 + diagonal * direction
-                + jnp.einsum("frs,rmks->fmks", prior_modes, projection, precision=lax.Precision.HIGHEST)
+                + jnp.sum(prior_modes[:, :, None, None, :] * projection[None], axis=1)
             )
             if norm_now is None:
                 norm_now, curve = scalar_sum(inner(residual, residual), inner(direction, image))

time: 256 us -> 154 us (0.60)
  local copies, waits for them, and re-layouts: 78.6 us -> 4.27 us
  matrix products: 44.9 us -> 13.6 us
  blocking collectives: 23.4 us -> 0 us
  waiting for transfers between devices: 9.29 us -> 22.2 us
  starting transfers between devices: 6.04 us -> 17.8 us
  other arithmetic: 3.84 us -> 6.95 us
    unnamed x13 -> x9, local copies, waits for them, and re-layouts: 47.1 us -> 0.03 us
    dot_general x6 -> x2, matrix products: 32.3 us -> 0.95 us  [the longest x1 0.48 us: shards(): jnp.einsum('mit,iftc->mfc', hartley_high, received, preferred_element_typ...]
    all_to_all x1 -> x0, blocking collectives: 23.4 us -> none  [shards(): lax.all_to_all(timestream_rows, 'ma', split_axis=2, concat_axis=1, tiled=...]
    all_to_all x2 -> x0, local copies, waits for them, and re-layouts: 17 us -> none  [shards(): lax.all_to_all(timestream_rows, 'ma', split_axis=2, concat_axis=1, tiled=...]
    all_to_all x1 -> x2, waiting for transfers between devices: 9.29 us -> 22.2 us  [the longest x1 12 us: shards(): received = lax.all_to_all(send, 'ma', 0, 0, tiled=True)]
    all_to_all x1 -> x2, starting transfers between devices: 6.04 us -> 17.8 us  [the longest x1 11.6 us: shards(): received = lax.all_to_all(send, 'ma', 0, 0, tiled=True)]
    another operation x4 -> x0, local copies, waits for them, and re-layouts: 6.3 us -> none
    transpose x2 -> x1, local copies, waits for them, and re-layouts: 4 us -> 0.05 us  [shards(): send = timestream.reshape(spectral_channels, device_time_samples, noise_r...]
  transfers between devices with their start and end apart: 1 -> 2, of which waited for: 1 -> 2; matrix products, arithmetic and copies ran while one was open for 0% -> 0% of each run, Pallas kernels for 0% -> 0%
where the time goes in v2:
time: 154 us; the launch traced here: 152 us
  Pallas kernels  87.4 us (57%)
  waiting for transfers between devices  22.2 us (14%)
  starting transfers between devices  17.8 us (12%)
  matrix products  13.6 us (9%)
  other arithmetic  6.95 us (5%)
  local copies, waits for them, and re-layouts  4.27 us (3%)
    pallas_call x5, Pallas kernels, group_sum(): pl.pallas_call(functools.partial(reduce_kernel, axis_names, stages), out_...  87.4 us
    all_to_all x1, waiting for transfers between devices, shards(): received = lax.all_to_all(send, 'ma', 0, 0, tiled=True)  12 us
    all_to_all x1, starting transfers between devices, shards(): received = lax.all_to_all(send, 'ma', 0, 0, tiled=True)  11.6 us
    all_to_all x1, waiting for transfers between devices, shards(): back_rows = lax.all_to_all(mode_rows, 'ma', 0, 0, tiled=True)  10.2 us
    dot_general x2, matrix products, shards(): jnp.einsum('fmkb,mbs->fmks', heard, beam_transfer, preferred_element_type...  10 us
    all_to_all x1, starting transfers between devices, shards(): back_rows = lax.all_to_all(mode_rows, 'ma', 0, 0, tiled=True)  6.16 us
  transfers between devices with their start and end apart: 2, of which 2 were waited for; matrix products, arithmetic and copies ran while one was open for 0% of the time, Pallas kernels for 0%

profile of v2, /device:TPU:1, one launch (start us, length us, event | category | flops | bytes accessed | tf_op | source)
XLA Modules:
  0.0 152.4 jit_solution(987457338034716223)
XLA Ops:
  0.0 0.0 copy-start.1
  0.0 0.0 copy-start.2
  0.0 1.1 reshape.240
  1.2 0.9 copy.27
  2.0 11.6 %all-to-all-start = ((bf16[64,16,128]{2,1,0:T(8,128)(2,1)}), bf16[64,16,128]{2,1,0:T(8,128)(2,1)S(1)}, u32[]{:S(2)}, u32[]{:S(2)}) async-start(bf16[64,16,128]{2,1,0:T(8,128)(2,1)} %copy.27), calls=%async_computation | async-start | bytes 524288 | tf_op jit(solution)/shard_map/all_to_all | solution.py:137
  13.7 12.0 %all-to-all-done = bf16[64,16,128]{2,1,0:T(8,128)(2,1)S(1)} async-done(((bf16[64,16,128]{2,1,0:T(8,128)(2,1)}), bf16[64,16,128]{2,1,0:T(8,128)(2,1)S(1)}, u32[]{:S(2)}, u32[]{:S(2)}) %all-to-all-start) | async-done | bytes 262176 | tf_op jit(solution)/shard_map/all_to_all | solution.py:137
  25.7 0.2 reshape.242
  25.9 0.5 convolution_bitcast_fusion
  26.3 0.5 fusion.39
  26.8 0.0 copy-start
  26.8 0.7 copy.30
  27.6 0.0 copy-start.3
  27.6 6.2 %all-to-all-start.1 = ((bf16[64,4,256]{2,1,0:T(4,128)(2,1)}), bf16[64,4,256]{2,1,0:T(4,128)(2,1)S(1)}, u32[]{:S(2)}, u32[]{:S(2)}) async-start(bf16[64,4,256]{2,1,0:T(4,128)(2,1)} %copy.30), calls=%async_computation.1 | async-start | bytes 262144 | tf_op jit(solution)/shard_map/all_to_all | solution.py:150
  33.7 0.0 copy-done.1
  33.7 0.1 reduce.4
  33.8 10.2 %all-to-all-done.1 = bf16[64,4,256]{2,1,0:T(4,128)(2,1)S(1)} async-done(((bf16[64,4,256]{2,1,0:T(4,128)(2,1)}), bf16[64,4,256]{2,1,0:T(4,128)(2,1)S(1)}, u32[]{:S(2)}, u32[]{:S(2)}) %all-to-all-start.1) | async-done | bytes 131104 | tf_op jit(solution)/shard_map/all_to_all | solution.py:150
  44.1 0.1 fusion.97
  44.1 0.1 copy.31
  44.2 0.0 copy-done.2
  44.2 2.7 %fusion.88 = f32[4,1,8,896]{3,2,0,1:T(8,128)S(1)} fusion(bf16[4,8,2048]{2,1,0:T(8,128)(2,1)S(1)} %bitcast.268, bf16[1,2048,896]{2,1,0:T(8,128)(2,1)} %param.7, f32[4,896]{1,0:T(4,128)S(1)} %copy-done.2), kind=kOutput, calls=%fused_computation.32 | convolution fusion | flops 117469184 | bytes 3930112 | tf_op jit(solution)/shard_map/fmkb,mbs->fmks/dot_general | solution.py:163
  46.9 0.0 copy-done
  46.9 0.6 multiply_reduce_fusion.3
  47.6 16.8 %shard_map.64 = f32[16,896]{1,0:T(8,128)} custom-call(f32[16,896]{1,0:T(8,128)} %bitcast.275), custom_call_target="tpu_custom_call" | custom-call | tf_op jit(solution)/shard_map/pallas_call | solution.py:86
  64.4 0.8 multiply_reduce_fusion.2
  65.3 0.0 copy-done.3
  65.3 5.0 %multiply_reduce_fusion.6 = (f32[8]{0:T(128)S(1)}, f32[8]{0:T(128)S(1)}, f32[4,1,8,896]{3,2,0,1:T(8,128)S(1)}) fusion(f32[4,1,8,896]{3,2,0,1:T(8,128)S(1)} %fusion.88, f32[4,8,896]{2,1,0:T(8,128)S(1)} %multiply_reduce_fusion.2, f32[4,896]{1,0:T(4,128)S(1)} %copy-done.3, bf16[1,2048,896]{2,1,0:T(8,128)(2,1)} %param.7, f32[4,2048]{1,0:T(4,128)S(1)} %bitcast.270, ...), kind=kOutput, calls=%fused_computation.52 | convolution fusion | flops 235298816 | bytes 4075584 | tf_op jit(solution)/shard_map/fmkb,mbs->fmks/dot_general | solution.py:175
  70.3 0.6 select_maximum_fusion.x_ref
  70.9 19.7 %shard_map.65 = f32[8,128]{1,0:T(8,128)} custom-call(f32[8,128]{1,0:T(8,128)} %select_maximum_fusion.x_ref), custom_call_target="tpu_custom_call" | custom-call | tf_op jit(solution)/shard_map/pallas_call | solution.py:86
  90.7 0.8 fusion.124
  91.4 0.2 multiply_reduce_fusion.4
  91.6 0.6 pad.12.x_ref
  92.3 19.0 %shard_map.66 = f32[8,128]{1,0:T(8,128)} custom-call(f32[8,128]{1,0:T(8,128)} %pad.12.x_ref), custom_call_target="tpu_custom_call" | custom-call | tf_op jit(solution)/shard_map/pallas_call | solution.py:86
  111.3 0.7 divide_bitcast_fusion
  112.0 0.1 fusion.136
  112.1 0.6 multiply_reduce_fusion.1
  112.7 10.7 %shard_map.67 = f32[16,896]{1,0:T(8,128)} custom-call(f32[16,896]{1,0:T(8,128)} %bitcast.273), custom_call_target="tpu_custom_call" | custom-call | tf_op jit(solution)/shard_map/pallas_call | solution.py:86
  123.5 0.9 multiply_reduce_fusion
  124.3 5.0 %fusion.91 = f32[8]{0:T(128)S(1)} fusion(bf16[1,2048,896]{2,1,0:T(8,128)(2,1)} %param.7, f32[4,2048]{1,0:T(4,128)S(1)} %bitcast.271, f32[4,8,896]{2,1,0:T(8,128)S(1)} %multiply_reduce_fusion, f32[4,896]{1,0:T(4,128)S(1)} %copy-done.3, f32[4,896]{1,0:T(4,128)S(1)} %copy-done.2, f32[4,1,8,896]{3,2,0,1:T(8,128)S(1)} %fusion.88, f32[8]{0:T(128)S(1)} %divide_bitcast_fusion, ...), kind=kOutput, calls=%fused_computation.33 | convolution fusion | flops 235470848 | bytes 4075616 | tf_op jit(solution)/shard_map/fmkb,mbs->fmks/dot_general | solution.py:175
  129.3 0.6 pad.13.x_ref
  129.9 21.0 %shard_map.68 = f32[8,128]{1,0:T(8,128)} custom-call(f32[8,128]{1,0:T(8,128)} %pad.13.x_ref), custom_call_target="tpu_custom_call" | custom-call | tf_op jit(solution)/shard_map/pallas_call | solution.py:86
  151.0 0.7 fusion.125
  151.7 0.7 add_bitcast_fusion
  (3 shorter events, 0.1 us)
Async XLA Ops:
  0.0 33.7 %copy-start.1 = (f32[4,1,2048]{2,1,0:T(1,128)S(1)}, f32[4,1,2048]{2,1,0:T(1,128)}, u32[]{:S(2)}) copy-start(f32[4,1,2048]{2,1,0:T(1,128)} %param.9) | copy-start | bytes 98308
  0.0 44.2 %copy-start.2 = (f32[4,896]{1,0:T(4,128)S(1)}, f32[4,896]{1,0:T(4,128)}, u32[]{:S(2)}) copy-start(f32[4,896]{1,0:T(4,128)} %param.8) | copy-start | bytes 43012
  2.0 23.6 %all-to-all-start = ((bf16[64,16,128]{2,1,0:T(8,128)(2,1)}), bf16[64,16,128]{2,1,0:T(8,128)(2,1)S(1)}, u32[]{:S(2)}, u32[]{:S(2)}) async-start(bf16[64,16,128]{2,1,0:T(8,128)(2,1)} %copy.27), calls=%async_computation | async-start | bytes 524288 | tf_op jit(solution)/shard_map/all_to_all | solution.py:137
  26.8 20.1 %copy-start = (f32[4,2,896]{2,1,0:T(2,128)S(1)}, f32[4,2,896]{2,1,0:T(2,128)}, u32[]{:S(2)}) copy-start(f32[4,2,896]{2,1,0:T(2,128)} %param.11) | copy-start | bytes 86020
  27.6 37.7 %copy-start.3 = (f32[4,896]{1,0:T(4,128)S(1)}, f32[4,896]{1,0:T(4,128)}, u32[]{:S(2)}) copy-start(f32[4,896]{1,0:T(4,128)} %param.10) | copy-start | bytes 43012
  27.6 16.5 %all-to-all-start.1 = ((bf16[64,4,256]{2,1,0:T(4,128)(2,1)}), bf16[64,4,256]{2,1,0:T(4,128)(2,1)S(1)}, u32[]{:S(2)}, u32[]{:S(2)}) async-start(bf16[64,4,256]{2,1,0:T(4,128)(2,1)} %copy.30), calls=%async_computation.1 | async-start | bytes 262144 | tf_op jit(solution)/shard_map/all_to_all | solution.py:150

commit v3 on v2

--- a/solution.py
+++ b/solution.py
@@ -98,6 +98,159 @@
     )(x)
 
 
+def column_sum(x):
+    return jnp.sum(jnp.sum(x, axis=0), axis=1, keepdims=True)
+
+
+def to_row(columns):
+    count = columns[0].shape[0]
+    sub = lax.broadcasted_iota(jnp.int32, (count, 128), 0)
+    lane = lax.broadcasted_iota(jnp.int32, (count, 128), 1)
+    acc = jnp.zeros((count, 128), jnp.float32)
+    for index, column in enumerate(columns):
+        acc = acc + jnp.where(lane == sub + count * index, jnp.broadcast_to(column, (count, 128)), 0.0)
+    return jnp.sum(acc, axis=0, keepdims=True)
+
+
+def from_row(row, index, count):
+    sub = lax.broadcasted_iota(jnp.int32, (count, 128), 0)
+    lane = lax.broadcasted_iota(jnp.int32, (count, 128), 1)
+    picked = jnp.where(lane == sub + count * index, jnp.broadcast_to(row, (count, 128)), 0.0)
+    return jnp.sum(picked, axis=1, keepdims=True)
+
+
+def cg_kernel(first, axis_names, sizes, *refs):
+    if first:
+        (d_ref, cb_ref, diag_ref, pm_ref, est_ref, next_ref, norm_ref,
+         part, rows, recv_p, recv_rows, p_send, p_recv, r_send, r_recv) = refs
+    else:
+        (d_ref, cb_ref, diag_ref, pm_ref, est_in_ref, norm_in_ref, est_ref,
+         part, rows, recv_p, recv_rows, p_send, p_recv, r_send, r_recv) = refs
+    me = {name: lax.axis_index(name) for name in axis_names}
+
+    def device(axis, coord):
+        return tuple(coord if name == axis else me[name] for name in axis_names)
+
+    barrier = pltpu.get_barrier_semaphore()
+    for axis in axis_names:
+        size = sizes[axis]
+
+        def greet(step, carry, axis=axis, size=size):
+            other = lax.rem(me[axis] + step, size)
+            pl.semaphore_signal(barrier, 1, device_id=device(axis, other), device_id_type=MESH)
+            return carry
+
+        lax.fori_loop(1, size, greet, 0)
+    pl.semaphore_wait(barrier, sum(sizes[axis] - 1 for axis in axis_names))
+
+    def exchange(axis, src, recv, base, send_sems, recv_sems):
+        size = sizes[axis]
+        own = me[axis]
+
+        def copy_to(other, slot):
+            return pltpu.make_async_remote_copy(
+                src_ref=src,
+                dst_ref=recv.at[base + slot],
+                send_sem=send_sems.at[base + other],
+                recv_sem=recv_sems.at[base + slot],
+                device_id=device(axis, other),
+                device_id_type=MESH,
+            )
+
+        def start(step, carry):
+            copy_to(lax.rem(own + step, size), own).start()
+            return carry
+
+        lax.fori_loop(1, size, start, 0)
+        recv[base + own] = src[...]
+
+        def arrive(step, carry):
+            other = lax.rem(own + step, size)
+            copy_to(other, other).wait_recv()
+            return carry
+
+        lax.fori_loop(1, size, arrive, 0)
+
+        def drain(step, carry):
+            copy_to(lax.rem(own + step, size), own).wait_send()
+            return carry
+
+        lax.fori_loop(1, size, drain, 0)
+
+        def add(slot, acc):
+            return acc + recv[base + slot]
+
+        return lax.fori_loop(1, size, add, recv[base])
+
+    fz, fm = "freq", "ma"
+    nz, nm = sizes[fz], sizes[fm]
+    d = d_ref[...]
+    cb = cb_ref[...]
+    diag = diag_ref[...]
+    pm = pm_ref[...]
+    count = d.shape[1]
+    for rank in range(pm.shape[1]):
+        part[rank] = jnp.sum(pm[:, rank] * d, axis=0)
+    if first:
+        rows[0] = to_row([column_sum(d * (cb + diag * d)), column_sum(d * d)])
+    else:
+        rows[0] = to_row([column_sum(d * (cb + diag * d))])
+    projection = exchange(fz, part, recv_p, 0, p_send, p_recv)
+    zrow = exchange(fz, rows.at[0], recv_rows, 0, r_send, r_recv)
+    rows[1] = zrow + to_row([column_sum(projection * projection)])
+    total = exchange(fm, rows.at[1], recv_rows, nz, r_send, r_recv)
+    curve = from_row(total, 0, count)
+    if first:
+        norm_now = from_row(total, 1, count)
+        step_size = (norm_now / curve)[None]
+        est_ref[...] = step_size * d
+        spread = pm[:, 0] * projection[0][None]
+        for rank in range(1, pm.shape[1]):
+            spread = spread + pm[:, rank] * projection[rank][None]
+        image = cb + diag * d + spread
+        residual = d - step_size * image
+        rows[2] = to_row([column_sum(residual * residual)])
+        zrow = exchange(fz, rows.at[2], recv_rows, nz + nm, r_send, r_recv)
+        rows[3] = zrow
+        total = exchange(fm, rows.at[3], recv_rows, 2 * nz + nm, r_send, r_recv)
+        norm_next = from_row(total, 0, count)
+        next_ref[...] = residual + (norm_next / norm_now)[None] * d
+        norm_ref[...] = total
+    else:
+        norm_now = from_row(norm_in_ref[...], 0, count)
+        est_ref[...] = est_in_ref[...] + (norm_now / curve)[None] * d
+
+
+def cg_step(first, axis_names, sizes, d, cb, diag, pm, *extra):
+    rounds = 4 if first else 2
+    slots = (rounds // 2) * (sizes["ma"] + sizes["freq"])
+    nz = sizes["freq"]
+    vector = jax.ShapeDtypeStruct(d.shape, jnp.float32)
+    row = jax.ShapeDtypeStruct((1, 128), jnp.float32)
+    out_shape = (vector, vector, row) if first else vector
+    vmem = pl.BlockSpec(memory_space=pltpu.VMEM)
+    part_shape = (pm.shape[1],) + d.shape[1:]
+    return pl.pallas_call(
+        functools.partial(cg_kernel, first, axis_names, sizes),
+        out_shape=out_shape,
+        in_specs=[vmem] * (4 + len(extra)),
+        out_specs=(vmem, vmem, vmem) if first else vmem,
+        scratch_shapes=[
+            pltpu.VMEM(part_shape, jnp.float32),
+            pltpu.VMEM((rounds, 1, 128), jnp.float32),
+            pltpu.VMEM((nz,) + part_shape, jnp.float32),
+            pltpu.VMEM((slots, 1, 128), jnp.float32),
+            pltpu.SemaphoreType.DMA((nz,)),
+            pltpu.SemaphoreType.DMA((nz,)),
+            pltpu.SemaphoreType.DMA((slots,)),
+            pltpu.SemaphoreType.DMA((slots,)),
+        ],
+        compiler_params=pltpu.CompilerParams(
+            collective_id=1 if first else 2, has_side_effects=True
+        ),
+    )(d, cb, diag, pm, *extra)
+
+
 def make_shards(mesh):
     axis_names = tuple(mesh.axis_names)
     mode_devices = mesh.shape["ma"]
@@ -164,35 +317,29 @@
             "fmkb,mbs->fmks", weighted, beam_transfer, preferred_element_type=jnp.float32
         )
 
-        estimate = jnp.zeros(rhs.shape, jnp.float32)
-        residual = rhs
-        direction = rhs
-        norm_now = None
-        for turn_index in range(ITERS):
+        assert resident_modes == 1
+        sizes = {name: mesh.shape[name] for name in axis_names}
+        diag_rows = prior_diagonal[:, None, :]
+        mode_rows4 = prior_modes[:, :, None, :]
+
+        def beam_back(direction):
             low = (chroma * direction).astype(jnp.bfloat16)
             seen = jnp.einsum("fmks,mbs->fmkb", low, beam_transfer, preferred_element_type=jnp.float32)
             heard = (noise_weight[:, :, None, :] * seen).astype(jnp.bfloat16)
             back = jnp.einsum(
                 "fmkb,mbs->fmks", heard, beam_transfer, preferred_element_type=jnp.float32
             )
-            partial_sum = jnp.sum(prior_modes[:, :, None, None, :] * direction[:, None], axis=0)
-            projection = freq_sum(partial_sum)
-            image = (
-                chroma * back
-                + diagonal * direction
-                + jnp.sum(prior_modes[:, :, None, None, :] * projection[None], axis=1)
-            )
-            if norm_now is None:
-                norm_now, curve = scalar_sum(inner(residual, residual), inner(direction, image))
-            else:
-                (curve,) = scalar_sum(inner(direction, image))
-            step_size = norm_now / curve
-            estimate = estimate + step_size[None, None, :, None] * direction
-            if turn_index + 1 < ITERS:
-                residual = residual - step_size[None, None, :, None] * image
-                (norm_next,) = scalar_sum(inner(residual, residual))
-                direction = residual + (norm_next / norm_now)[None, None, :, None] * direction
-                norm_now = norm_next
+            return (chroma * back)[:, 0]
+
+        direction = rhs[:, 0]
+        estimate, direction, norm_row = cg_step(
+            True, axis_names, sizes, direction, beam_back(direction[:, None]), diag_rows, mode_rows4
+        )
+        estimate = cg_step(
+            False, axis_names, sizes, direction, beam_back(direction[:, None]), diag_rows, mode_rows4,
+            estimate, norm_row,
+        )
+        estimate = estimate[:, None]
         return estimate
 
     return shards

time: 154 us -> 146 us (0.948)
  other arithmetic: 6.95 us -> 0.15 us
  local copies, waits for them, and re-layouts: 4.27 us -> 5.91 us
    reduce_sum x5 -> x0, other arithmetic: 3.2 us -> none  [the longest x2 1.7 us: shards(): jnp.sum(prior_modes[:, :, None, None, :] * projection[None], axis=1)]
    div x3 -> x0, other arithmetic: 2.14 us -> none  [the longest x2 1.45 us: shards(): step_size = norm_now / curve]
    unnamed x9 -> x12, local copies, waits for them, and re-layouts: 0.03 us -> 1.59 us
    pallas_call x5 -> x2, Pallas kernels: 87.4 us -> 86.4 us  [cg_step(): pl.pallas_call(functools.partial(cg_kernel, first, axis_names, sizes), ou...]
  transfers between devices with their start and end apart: 2 -> 2, of which waited for: 2 -> 2; matrix products, arithmetic and copies ran while one was open for 0% -> 1% of each run, Pallas kernels for 0% -> 0%
where the time goes in v3:
time: 146 us
  Pallas kernels  86.4 us (59%)
  waiting for transfers between devices  21 us (14%)
  starting transfers between devices  17.6 us (12%)
  matrix products  14.7 us (10%)
  local copies, waits for them, and re-layouts  5.91 us (4%)
    pallas_call x2, Pallas kernels, cg_step(): pl.pallas_call(functools.partial(cg_kernel, first, axis_names, sizes), ou...  86.4 us
    all_to_all x1, waiting for transfers between devices, shards(): received = lax.all_to_all(send, 'ma', 0, 0, tiled=True)  12 us
    all_to_all x1, starting transfers between devices, shards(): received = lax.all_to_all(send, 'ma', 0, 0, tiled=True)  11.6 us
    dot_general x2, matrix products, beam_back(): jnp.einsum('fmkb,mbs->fmks', heard, beam_transfer, preferred_element_type...  11.1 us
    all_to_all x1, waiting for transfers between devices, shards(): back_rows = lax.all_to_all(mode_rows, 'ma', 0, 0, tiled=True)  8.99 us
    all_to_all x1, starting transfers between devices, shards(): back_rows = lax.all_to_all(mode_rows, 'ma', 0, 0, tiled=True)  6.03 us
  transfers between devices with their start and end apart: 2, of which 2 were waited for; matrix products, arithmetic and copies ran while one was open for 1% of the time, Pallas kernels for 0%

profile of v3, /device:TPU:1, one launch (start us, length us, event | category | flops | bytes accessed | tf_op | source)
XLA Modules:
  0.0 145.9 jit_solution(16514245280097576732)
XLA Ops:
  0.0 0.0 copy-start.1
  0.0 0.0 copy-start.3
  0.0 0.0 copy-start.4
  0.0 0.0 copy-start.2
  0.0 1.2 reshape.159
  1.2 0.9 copy.19
  2.1 11.6 %all-to-all-start = ((bf16[64,16,128]{2,1,0:T(8,128)(2,1)}), bf16[64,16,128]{2,1,0:T(8,128)(2,1)S(1)}, u32[]{:S(2)}, u32[]{:S(2)}) async-start(bf16[64,16,128]{2,1,0:T(8,128)(2,1)} %copy.19), calls=%async_computation | async-start | bytes 524288 | tf_op jit(solution)/shard_map/all_to_all | solution.py:290
  13.7 12.0 %all-to-all-done = bf16[64,16,128]{2,1,0:T(8,128)(2,1)S(1)} async-done(((bf16[64,16,128]{2,1,0:T(8,128)(2,1)}), bf16[64,16,128]{2,1,0:T(8,128)(2,1)S(1)}, u32[]{:S(2)}, u32[]{:S(2)}) %all-to-all-start) | async-done | bytes 262176 | tf_op jit(solution)/shard_map/all_to_all | solution.py:290
  25.7 0.2 reshape.161
  25.9 0.5 convolution_bitcast_fusion
  26.4 0.5 fusion.39
  26.9 0.8 copy.22
  27.6 6.0 %all-to-all-start.1 = ((bf16[64,4,256]{2,1,0:T(4,128)(2,1)}), bf16[64,4,256]{2,1,0:T(4,128)(2,1)S(1)}, u32[]{:S(2)}, u32[]{:S(2)}) async-start(bf16[64,4,256]{2,1,0:T(4,128)(2,1)} %copy.22), calls=%async_computation.1 | async-start | bytes 262144 | tf_op jit(solution)/shard_map/all_to_all | solution.py:303
  33.7 0.0 copy-done.1
  33.7 0.1 reduce
  33.8 0.0 copy-done.3
  33.8 0.6 broadcast_in_dim.7.refs_3_
  34.4 0.0 copy-done.4
  34.4 0.6 broadcast_in_dim.6.refs_2_
  35.0 9.0 %all-to-all-done.1 = bf16[64,4,256]{2,1,0:T(4,128)(2,1)S(1)} async-done(((bf16[64,4,256]{2,1,0:T(4,128)(2,1)}), bf16[64,4,256]{2,1,0:T(4,128)(2,1)S(1)}, u32[]{:S(2)}, u32[]{:S(2)}) %all-to-all-start.1) | async-done | bytes 131104 | tf_op jit(solution)/shard_map/all_to_all | solution.py:303
  44.0 0.1 fusion.77
  44.1 0.1 copy.23
  44.2 0.0 copy-done.2
  44.2 2.7 %fusion.73 = f32[4,1,8,896]{3,2,0,1:T(8,128)S(1)} fusion(bf16[4,8,2048]{2,1,0:T(8,128)(2,1)S(1)} %bitcast.199, bf16[1,2048,896]{2,1,0:T(8,128)(2,1)} %param.7, f32[4,896]{1,0:T(4,128)S(1)} %copy-done.2), kind=kOutput, calls=%fused_computation.29 | convolution fusion | flops 117469184 | bytes 3930112 | tf_op jit(solution)/shard_map/fmkb,mbs->fmks/dot_general | solution.py:316
  46.9 0.0 copy-start
  46.9 5.5 %fusion.68.refs_1_ = f32[4,8,896]{2,1,0:T(8,128)} fusion(bf16[1,2048,896]{2,1,0:T(8,128)(2,1)} %param.7, f32[4,2048]{1,0:T(4,128)S(1)} %bitcast.202, f32[4,1,8,896]{3,2,0,1:T(8,128)S(1)} %fusion.73, f32[4,896]{1,0:T(4,128)S(1)} %copy-done.2), kind=kOutput, calls=%fused_computation.28 | convolution fusion | flops 235098112 | bytes 3946496 | tf_op jit(solution)/shard_map/fmkb,mbs->fmks/dot_general | solution.py:329
  52.4 0.0 copy-done
  52.4 52.2 %shard_map.64 = (f32[4,8,896]{2,1,0:T(8,128)}, f32[4,8,896]{2,1,0:T(8,128)}, f32[1,128]{1,0:T(1,128)}) custom-call(f32[4,8,896]{2,1,0:T(8,128)} %bitcast.198, f32[4,8,896]{2,1,0:T(8,128)} %fusion.68.refs_1_, f32[4,1,896]{2,1,0:T(1,128)} %broadcast_in_dim.6.refs_2_, f32[4,2,1,896]{3,2,1,0:T(1,128)} %broadcast_in_dim.7.refs_3_), custom_call_target="tpu_custom_call" | custom-call | tf_op jit(solution)/shard_map/pallas_call | solution.py:233
  104.6 5.5 %fusion.58.refs_1_ = f32[4,8,896]{2,1,0:T(8,128)} fusion(bf16[1,2048,896]{2,1,0:T(8,128)(2,1)} %param.7, f32[4,2048]{1,0:T(4,128)S(1)} %bitcast.203, f32[4,8,896]{2,1,0:T(8,128)} %get-tuple-element.8.refs_0_, f32[4,896]{1,0:T(4,128)S(1)} %copy-done.2), kind=kOutput, calls=%fused_computation.26 | convolution fusion | flops 235098112 | bytes 3946496 | tf_op jit(solution)/shard_map/fmkb,mbs->fmks/dot_general | solution.py:329
  110.1 34.2 %shard_map.65 = f32[4,8,896]{2,1,0:T(8,128)} custom-call(f32[4,8,896]{2,1,0:T(8,128)} %get-tuple-element.8.refs_0_, f32[4,8,896]{2,1,0:T(8,128)} %fusion.58.refs_1_, f32[4,1,896]{2,1,0:T(1,128)} %broadcast_in_dim.6.refs_2_, f32[4,2,1,896]{3,2,1,0:T(1,128)} %broadcast_in_dim.7.refs_3_, f32[4,8,896]{2,1,0:T(8,128)} %get-tuple-element.9.refs_4_, ...), custom_call_target="tpu_custom_call" | custom-call | tf_op jit(solution)/shard_map/pallas_call | solution.py:233
  144.3 1.6 %copy.35 = f32[4,1,8,896]{3,2,1,0:T(8,128)} copy(f32[4,1,8,896]{3,2,1,0:T(8,128)} %bitcast.201) | data formatting | bytes 229376
  (3 shorter events, 0.1 us)
Async XLA Ops:
  0.0 33.7 %copy-start.1 = (f32[4,1,2048]{2,1,0:T(1,128)S(1)}, f32[4,1,2048]{2,1,0:T(1,128)}, u32[]{:S(2)}) copy-start(f32[4,1,2048]{2,1,0:T(1,128)} %param.9) | copy-start | bytes 98308
  0.0 33.8 %copy-start.3 = (f32[4,2,896]{2,1,0:T(2,128)S(1)}, f32[4,2,896]{2,1,0:T(2,128)}, u32[]{:S(2)}) copy-start(f32[4,2,896]{2,1,0:T(2,128)} %param.11) | copy-start | bytes 86020
  0.0 34.4 %copy-start.4 = (f32[4,896]{1,0:T(4,128)S(1)}, f32[4,896]{1,0:T(4,128)}, u32[]{:S(2)}) copy-start(f32[4,896]{1,0:T(4,128)} %param.10) | copy-start | bytes 43012
  0.0 44.2 %copy-start.2 = (f32[4,896]{1,0:T(4,128)S(1)}, f32[4,896]{1,0:T(4,128)}, u32[]{:S(2)}) copy-start(f32[4,896]{1,0:T(4,128)} %param.8) | copy-start | bytes 43012
  2.1 23.6 %all-to-all-start = ((bf16[64,16,128]{2,1,0:T(8,128)(2,1)}), bf16[64,16,128]{2,1,0:T(8,128)(2,1)S(1)}, u32[]{:S(2)}, u32[]{:S(2)}) async-start(bf16[64,16,128]{2,1,0:T(8,128)(2,1)} %copy.19), calls=%async_computation | async-start | bytes 524288 | tf_op jit(solution)/shard_map/all_to_all | solution.py:290
  27.6 16.4 %all-to-all-start.1 = ((bf16[64,4,256]{2,1,0:T(4,128)(2,1)}), bf16[64,4,256]{2,1,0:T(4,128)(2,1)S(1)}, u32[]{:S(2)}, u32[]{:S(2)}) async-start(bf16[64,4,256]{2,1,0:T(4,128)(2,1)} %copy.22), calls=%async_computation.1 | async-start | bytes 262144 | tf_op jit(solution)/shard_map/all_to_all | solution.py:303
  46.9 5.5 %copy-start = (f32[4,1,8,896]{3,2,0,1:T(8,128)}, f32[4,1,8,896]{3,2,0,1:T(8,128)S(1)}, u32[]{:S(2)}) copy-start(f32[4,1,8,896]{3,2,0,1:T(8,128)S(1)} %fusion.73) | copy-start | bytes 344068

commit v4 on v3

--- a/solution.py
+++ b/solution.py
@@ -119,7 +119,7 @@
     return jnp.sum(picked, axis=1, keepdims=True)
 
 
-def cg_kernel(first, axis_names, sizes, *refs):
+def cg_kernel(first, axis_names, stages, *refs):
     if first:
         (d_ref, cb_ref, diag_ref, pm_ref, est_ref, next_ref, norm_ref,
          part, rows, recv_p, recv_rows, p_send, p_recv, r_send, r_recv) = refs
@@ -128,24 +128,27 @@
          part, rows, recv_p, recv_rows, p_send, p_recv, r_send, r_recv) = refs
     me = {name: lax.axis_index(name) for name in axis_names}
 
-    def device(axis, coord):
-        return tuple(coord if name == axis else me[name] for name in axis_names)
+    def place(stage):
+        axis, stride, size = stage
+        own = lax.rem(me[axis] // stride, size)
+        root = me[axis] - own * stride
+
+        def device(other):
+            return tuple(root + other * stride if name == axis else me[name] for name in axis_names)
+
+        return own, device
 
     barrier = pltpu.get_barrier_semaphore()
-    for axis in axis_names:
-        size = sizes[axis]
-
-        def greet(step, carry, axis=axis, size=size):
-            other = lax.rem(me[axis] + step, size)
-            pl.semaphore_signal(barrier, 1, device_id=device(axis, other), device_id_type=MESH)
-            return carry
-
-        lax.fori_loop(1, size, greet, 0)
-    pl.semaphore_wait(barrier, sum(sizes[axis] - 1 for axis in axis_names))
-
-    def exchange(axis, src, recv, base, send_sems, recv_sems):
-        size = sizes[axis]
-        own = me[axis]
+    for stage in stages:
+        own, device = place(stage)
+        for step in range(1, stage[2]):
+            other = lax.rem(own + step, stage[2])
+            pl.semaphore_signal(barrier, 1, device_id=device(other), device_id_type=MESH)
+    pl.semaphore_wait(barrier, sum(size - 1 for _, _, size in stages))
+
+    def exchange_start(stage, src, recv, base, send_sems, recv_sems):
+        own, device = place(stage)
+        size = stage[2]
 
         def copy_to(other, slot):
             return pltpu.make_async_remote_copy(
@@ -153,37 +156,45 @@
                 dst_ref=recv.at[base + slot],
                 send_sem=send_sems.at[base + other],
                 recv_sem=recv_sems.at[base + slot],
-                device_id=device(axis, other),
+                device_id=device(other),
                 device_id_type=MESH,
             )
 
-        def start(step, carry):
+        for step in range(1, size):
             copy_to(lax.rem(own + step, size), own).start()
-            return carry
-
-        lax.fori_loop(1, size, start, 0)
         recv[base + own] = src[...]
-
-        def arrive(step, carry):
+        return own, size, base, recv, copy_to
+
+    def exchange_finish(state):
+        own, size, base, recv, copy_to = state
+        for step in range(1, size):
             other = lax.rem(own + step, size)
             copy_to(other, other).wait_recv()
-            return carry
-
-        lax.fori_loop(1, size, arrive, 0)
-
-        def drain(step, carry):
+        for step in range(1, size):
             copy_to(lax.rem(own + step, size), own).wait_send()
-            return carry
-
-        lax.fori_loop(1, size, drain, 0)
-
-        def add(slot, acc):
-            return acc + recv[base + slot]
-
-        return lax.fori_loop(1, size, add, recv[base])
-
-    fz, fm = "freq", "ma"
-    nz, nm = sizes[fz], sizes[fm]
+        total = recv[base]
+        for slot in range(1, size):
+            total = total + recv[base + slot]
+        return total
+
+    counter = {"row": 0, "slot": 0}
+
+    def next_row(value):
+        index = counter["row"]
+        counter["row"] += 1
+        rows[index] = value
+        return rows.at[index]
+
+    def row_stage(stage, src):
+        base = counter["slot"]
+        counter["slot"] += stage[2]
+        return exchange_start(stage, src, recv_rows, base, r_send, r_recv)
+
+    def reduce_rest(value):
+        for stage in stages[1:]:
+            value = exchange_finish(row_stage(stage, next_row(value)))
+        return value
+
     d = d_ref[...]
     cb = cb_ref[...]
     diag = diag_ref[...]
@@ -192,13 +203,14 @@
     for rank in range(pm.shape[1]):
         part[rank] = jnp.sum(pm[:, rank] * d, axis=0)
     if first:
-        rows[0] = to_row([column_sum(d * (cb + diag * d)), column_sum(d * d)])
+        row = to_row([column_sum(d * (cb + diag * d)), column_sum(d * d)])
     else:
-        rows[0] = to_row([column_sum(d * (cb + diag * d))])
-    projection = exchange(fz, part, recv_p, 0, p_send, p_recv)
-    zrow = exchange(fz, rows.at[0], recv_rows, 0, r_send, r_recv)
-    rows[1] = zrow + to_row([column_sum(projection * projection)])
-    total = exchange(fm, rows.at[1], recv_rows, nz, r_send, r_recv)
+        row = to_row([column_sum(d * (cb + diag * d))])
+    p_state = exchange_start(stages[0], part, recv_p, 0, p_send, p_recv)
+    z_state = row_stage(stages[0], next_row(row))
+    projection = exchange_finish(p_state)
+    zrow = exchange_finish(z_state)
+    total = reduce_rest(zrow + to_row([column_sum(projection * projection)]))
     curve = from_row(total, 0, count)
     if first:
         norm_now = from_row(total, 1, count)
@@ -209,10 +221,9 @@
             spread = spread + pm[:, rank] * projection[rank][None]
         image = cb + diag * d + spread
         residual = d - step_size * image
-        rows[2] = to_row([column_sum(residual * residual)])
-        zrow = exchange(fz, rows.at[2], recv_rows, nz + nm, r_send, r_recv)
-        rows[3] = zrow
-        total = exchange(fm, rows.at[3], recv_rows, 2 * nz + nm, r_send, r_recv)
+        row = to_row([column_sum(residual * residual)])
+        zrow = exchange_finish(row_stage(stages[0], next_row(row)))
+        total = reduce_rest(zrow)
         norm_next = from_row(total, 0, count)
         next_ref[...] = residual + (norm_next / norm_now)[None] * d
         norm_ref[...] = total
@@ -221,17 +232,18 @@
         est_ref[...] = est_in_ref[...] + (norm_now / curve)[None] * d
 
 
-def cg_step(first, axis_names, sizes, d, cb, diag, pm, *extra):
-    rounds = 4 if first else 2
-    slots = (rounds // 2) * (sizes["ma"] + sizes["freq"])
-    nz = sizes["freq"]
+def cg_step(first, axis_names, stages, d, cb, diag, pm, *extra):
+    reductions = 2 if first else 1
+    slots = reductions * sum(size for _, _, size in stages)
+    rounds = reductions * len(stages)
+    nz = stages[0][2]
     vector = jax.ShapeDtypeStruct(d.shape, jnp.float32)
     row = jax.ShapeDtypeStruct((1, 128), jnp.float32)
     out_shape = (vector, vector, row) if first else vector
     vmem = pl.BlockSpec(memory_space=pltpu.VMEM)
     part_shape = (pm.shape[1],) + d.shape[1:]
     return pl.pallas_call(
-        functools.partial(cg_kernel, first, axis_names, sizes),
+        functools.partial(cg_kernel, first, axis_names, stages),
         out_shape=out_shape,
         in_specs=[vmem] * (4 + len(extra)),
         out_specs=(vmem, vmem, vmem) if first else vmem,
@@ -318,7 +330,7 @@
         )
 
         assert resident_modes == 1
-        sizes = {name: mesh.shape[name] for name in axis_names}
+        cg_stages = [("freq", 1, freq_devices)] + mode_stages
         diag_rows = prior_diagonal[:, None, :]
         mode_rows4 = prior_modes[:, :, None, :]
 
@@ -333,10 +345,10 @@
 
         direction = rhs[:, 0]
         estimate, direction, norm_row = cg_step(
-            True, axis_names, sizes, direction, beam_back(direction[:, None]), diag_rows, mode_rows4
+            True, axis_names, cg_stages, direction, beam_back(direction[:, None]), diag_rows, mode_rows4
         )
         estimate = cg_step(
-            False, axis_names, sizes, direction, beam_back(direction[:, None]), diag_rows, mode_rows4,
+            False, axis_names, cg_stages, direction, beam_back(direction[:, None]), diag_rows, mode_rows4,
             estimate, norm_row,
         )
         estimate = estimate[:, None]

time: 146 us -> 134 us (0.918)
  Pallas kernels: 86.4 us -> 73.7 us
    pallas_call x2, Pallas kernels: 86.4 us -> 73.7 us  [cg_step(): pl.pallas_call(functools.partial(cg_kernel, first, axis_names, stages), o...]
where the time goes in v4:
time: 134 us; the launch traced here: 133 us
  Pallas kernels  73.7 us (55%)
  waiting for transfers between devices  21 us (16%)
  starting transfers between devices  17.6 us (13%)
  matrix products  14.7 us (11%)
  local copies, waits for them, and re-layouts  5.91 us (4%)
    pallas_call x2, Pallas kernels, cg_step(): pl.pallas_call(functools.partial(cg_kernel, first, axis_names, stages), o...  73.7 us
    all_to_all x1, waiting for transfers between devices, shards(): received = lax.all_to_all(send, 'ma', 0, 0, tiled=True)  12 us
    all_to_all x1, starting transfers between devices, shards(): received = lax.all_to_all(send, 'ma', 0, 0, tiled=True)  11.6 us
    dot_general x2, matrix products, beam_back(): jnp.einsum('fmkb,mbs->fmks', heard, beam_transfer, preferred_element_type...  11.1 us
    all_to_all x1, waiting for transfers between devices, shards(): back_rows = lax.all_to_all(mode_rows, 'ma', 0, 0, tiled=True)  8.99 us
    all_to_all x1, starting transfers between devices, shards(): back_rows = lax.all_to_all(mode_rows, 'ma', 0, 0, tiled=True)  6.03 us
    dot_general x1, matrix products, shards(): jnp.einsum('fmkb,mbs->fmks', weighted, beam_transfer, preferred_element_t...  2.68 us
  transfers between devices with their start and end apart: 2, of which 2 were waited for; matrix products, arithmetic and copies ran while one was open for 1% of the time, Pallas kernels for 0%

profile of v4, /device:TPU:1, one launch (start us, length us, event | category | flops | bytes accessed | tf_op | source)
XLA Modules:
  0.0 133.2 jit_solution(15622915762719859372)
XLA Ops:
  0.0 0.0 copy-start.1
  0.0 0.0 copy-start.3
  0.0 0.0 copy-start.4
  0.0 0.0 copy-start.2
  0.0 1.2 reshape.159
  1.2 0.9 copy.19
  2.1 11.6 %all-to-all-start = ((bf16[64,16,128]{2,1,0:T(8,128)(2,1)}), bf16[64,16,128]{2,1,0:T(8,128)(2,1)S(1)}, u32[]{:S(2)}, u32[]{:S(2)}) async-start(bf16[64,16,128]{2,1,0:T(8,128)(2,1)} %copy.19), calls=%async_computation | async-start | bytes 524288 | tf_op jit(solution)/shard_map/all_to_all | solution.py:302
  13.7 12.0 %all-to-all-done = bf16[64,16,128]{2,1,0:T(8,128)(2,1)S(1)} async-done(((bf16[64,16,128]{2,1,0:T(8,128)(2,1)}), bf16[64,16,128]{2,1,0:T(8,128)(2,1)S(1)}, u32[]{:S(2)}, u32[]{:S(2)}) %all-to-all-start) | async-done | bytes 262176 | tf_op jit(solution)/shard_map/all_to_all | solution.py:302
  25.7 0.2 reshape.161
  25.9 0.5 convolution_bitcast_fusion
  26.4 0.5 fusion.39
  26.9 0.8 copy.22
  27.6 6.0 %all-to-all-start.1 = ((bf16[64,4,256]{2,1,0:T(4,128)(2,1)}), bf16[64,4,256]{2,1,0:T(4,128)(2,1)S(1)}, u32[]{:S(2)}, u32[]{:S(2)}) async-start(bf16[64,4,256]{2,1,0:T(4,128)(2,1)} %copy.22), calls=%async_computation.1 | async-start | bytes 262144 | tf_op jit(solution)/shard_map/all_to_all | solution.py:315
  33.7 0.0 copy-done.1
  33.7 0.1 reduce
  33.8 0.0 copy-done.3
  33.8 0.6 broadcast_in_dim.7.refs_3_
  34.4 0.0 copy-done.4
  34.4 0.6 broadcast_in_dim.6.refs_2_
  35.0 9.0 %all-to-all-done.1 = bf16[64,4,256]{2,1,0:T(4,128)(2,1)S(1)} async-done(((bf16[64,4,256]{2,1,0:T(4,128)(2,1)}), bf16[64,4,256]{2,1,0:T(4,128)(2,1)S(1)}, u32[]{:S(2)}, u32[]{:S(2)}) %all-to-all-start.1) | async-done | bytes 131104 | tf_op jit(solution)/shard_map/all_to_all | solution.py:315
  44.0 0.1 fusion.77
  44.1 0.1 copy.23
  44.2 0.0 copy-done.2
  44.2 2.7 %fusion.73 = f32[4,1,8,896]{3,2,0,1:T(8,128)S(1)} fusion(bf16[4,8,2048]{2,1,0:T(8,128)(2,1)S(1)} %bitcast.199, bf16[1,2048,896]{2,1,0:T(8,128)(2,1)} %param.7, f32[4,896]{1,0:T(4,128)S(1)} %copy-done.2), kind=kOutput, calls=%fused_computation.29 | convolution fusion | flops 117469184 | bytes 3930112 | tf_op jit(solution)/shard_map/fmkb,mbs->fmks/dot_general | solution.py:328
  46.9 0.0 copy-start
  46.9 5.5 %fusion.68.refs_1_ = f32[4,8,896]{2,1,0:T(8,128)} fusion(bf16[1,2048,896]{2,1,0:T(8,128)(2,1)} %param.7, f32[4,2048]{1,0:T(4,128)S(1)} %bitcast.202, f32[4,1,8,896]{3,2,0,1:T(8,128)S(1)} %fusion.73, f32[4,896]{1,0:T(4,128)S(1)} %copy-done.2), kind=kOutput, calls=%fused_computation.28 | convolution fusion | flops 235098112 | bytes 3946496 | tf_op jit(solution)/shard_map/fmkb,mbs->fmks/dot_general | solution.py:341
  52.4 0.0 copy-done
  52.4 46.5 %shard_map.64 = (f32[4,8,896]{2,1,0:T(8,128)}, f32[4,8,896]{2,1,0:T(8,128)}, f32[1,128]{1,0:T(1,128)}) custom-call(f32[4,8,896]{2,1,0:T(8,128)} %bitcast.198, f32[4,8,896]{2,1,0:T(8,128)} %fusion.68.refs_1_, f32[4,1,896]{2,1,0:T(1,128)} %broadcast_in_dim.6.refs_2_, f32[4,2,1,896]{3,2,1,0:T(1,128)} %broadcast_in_dim.7.refs_3_), custom_call_target="tpu_custom_call" | custom-call | tf_op jit(solution)/shard_map/pallas_call | solution.py:245
  99.0 5.5 %fusion.58.refs_1_ = f32[4,8,896]{2,1,0:T(8,128)} fusion(bf16[1,2048,896]{2,1,0:T(8,128)(2,1)} %param.7, f32[4,2048]{1,0:T(4,128)S(1)} %bitcast.203, f32[4,8,896]{2,1,0:T(8,128)} %get-tuple-element.8.refs_0_, f32[4,896]{1,0:T(4,128)S(1)} %copy-done.2), kind=kOutput, calls=%fused_computation.26 | convolution fusion | flops 235098112 | bytes 3946496 | tf_op jit(solution)/shard_map/fmkb,mbs->fmks/dot_general | solution.py:341
  104.5 27.1 %shard_map.65 = f32[4,8,896]{2,1,0:T(8,128)} custom-call(f32[4,8,896]{2,1,0:T(8,128)} %get-tuple-element.8.refs_0_, f32[4,8,896]{2,1,0:T(8,128)} %fusion.58.refs_1_, f32[4,1,896]{2,1,0:T(1,128)} %broadcast_in_dim.6.refs_2_, f32[4,2,1,896]{3,2,1,0:T(1,128)} %broadcast_in_dim.7.refs_3_, f32[4,8,896]{2,1,0:T(8,128)} %get-tuple-element.9.refs_4_, ...), custom_call_target="tpu_custom_call" | custom-call | tf_op jit(solution)/shard_map/pallas_call | solution.py:245
  131.6 1.6 %copy.35 = f32[4,1,8,896]{3,2,1,0:T(8,128)} copy(f32[4,1,8,896]{3,2,1,0:T(8,128)} %bitcast.201) | data formatting | bytes 229376
  (3 shorter events, 0.1 us)
Async XLA Ops:
  0.0 33.7 %copy-start.1 = (f32[4,1,2048]{2,1,0:T(1,128)S(1)}, f32[4,1,2048]{2,1,0:T(1,128)}, u32[]{:S(2)}) copy-start(f32[4,1,2048]{2,1,0:T(1,128)} %param.9) | copy-start | bytes 98308
  0.0 33.8 %copy-start.3 = (f32[4,2,896]{2,1,0:T(2,128)S(1)}, f32[4,2,896]{2,1,0:T(2,128)}, u32[]{:S(2)}) copy-start(f32[4,2,896]{2,1,0:T(2,128)} %param.11) | copy-start | bytes 86020
  0.0 34.4 %copy-start.4 = (f32[4,896]{1,0:T(4,128)S(1)}, f32[4,896]{1,0:T(4,128)}, u32[]{:S(2)}) copy-start(f32[4,896]{1,0:T(4,128)} %param.10) | copy-start | bytes 43012
  0.0 44.2 %copy-start.2 = (f32[4,896]{1,0:T(4,128)S(1)}, f32[4,896]{1,0:T(4,128)}, u32[]{:S(2)}) copy-start(f32[4,896]{1,0:T(4,128)} %param.8) | copy-start | bytes 43012
  2.1 23.6 %all-to-all-start = ((bf16[64,16,128]{2,1,0:T(8,128)(2,1)}), bf16[64,16,128]{2,1,0:T(8,128)(2,1)S(1)}, u32[]{:S(2)}, u32[]{:S(2)}) async-start(bf16[64,16,128]{2,1,0:T(8,128)(2,1)} %copy.19), calls=%async_computation | async-start | bytes 524288 | tf_op jit(solution)/shard_map/all_to_all | solution.py:302
  27.6 16.4 %all-to-all-start.1 = ((bf16[64,4,256]{2,1,0:T(4,128)(2,1)}), bf16[64,4,256]{2,1,0:T(4,128)(2,1)S(1)}, u32[]{:S(2)}, u32[]{:S(2)}) async-start(bf16[64,4,256]{2,1,0:T(4,128)(2,1)} %copy.22), calls=%async_computation.1 | async-start | bytes 262144 | tf_op jit(solution)/shard_map/all_to_all | solution.py:315
  46.9 5.5 %copy-start = (f32[4,1,8,896]{3,2,0,1:T(8,128)}, f32[4,1,8,896]{3,2,0,1:T(8,128)S(1)}, u32[]{:S(2)}) copy-start(f32[4,1,8,896]{3,2,0,1:T(8,128)S(1)} %fusion.73) | copy-start | bytes 344068

commit v5 on v4

--- a/solution.py
+++ b/solution.py
@@ -165,13 +165,14 @@
         recv[base + own] = src[...]
         return own, size, base, recv, copy_to
 
+    sent = []
+
     def exchange_finish(state):
         own, size, base, recv, copy_to = state
         for step in range(1, size):
             other = lax.rem(own + step, size)
             copy_to(other, other).wait_recv()
-        for step in range(1, size):
-            copy_to(lax.rem(own + step, size), own).wait_send()
+        sent.append(state)
         total = recv[base]
         for slot in range(1, size):
             total = total + recv[base + slot]
@@ -230,6 +231,9 @@
     else:
         norm_now = from_row(norm_in_ref[...], 0, count)
         est_ref[...] = est_in_ref[...] + (norm_now / curve)[None] * d
+    for own, size, _, _, copy_to in sent:
+        for step in range(1, size):
+            copy_to(lax.rem(own + step, size), own).wait_send()
 
 
 def cg_step(first, axis_names, stages, d, cb, diag, pm, *extra):

time: 134 us -> 133 us (level)
  no operation moved by 1% of the time
where the time goes in v5:
time: 133 us
  Pallas kernels  73.1 us (55%)
  waiting for transfers between devices  21 us (16%)
  starting transfers between devices  17.6 us (13%)
  matrix products  14.7 us (11%)
  local copies, waits for them, and re-layouts  5.91 us (4%)
    pallas_call x2, Pallas kernels, cg_step(): pl.pallas_call(functools.partial(cg_kernel, first, axis_names, stages), o...  73.1 us
    all_to_all x1, waiting for transfers between devices, shards(): received = lax.all_to_all(send, 'ma', 0, 0, tiled=True)  12 us
    all_to_all x1, starting transfers between devices, shards(): received = lax.all_to_all(send, 'ma', 0, 0, tiled=True)  11.6 us
    dot_general x2, matrix products, beam_back(): jnp.einsum('fmkb,mbs->fmks', heard, beam_transfer, preferred_element_type...  11.1 us
    all_to_all x1, waiting for transfers between devices, shards(): back_rows = lax.all_to_all(mode_rows, 'ma', 0, 0, tiled=True)  8.99 us
    all_to_all x1, starting transfers between devices, shards(): back_rows = lax.all_to_all(mode_rows, 'ma', 0, 0, tiled=True)  6.03 us
    dot_general x1, matrix products, shards(): jnp.einsum('fmkb,mbs->fmks', weighted, beam_transfer, preferred_element_t...  2.68 us
  transfers between devices with their start and end apart: 2, of which 2 were waited for; matrix products, arithmetic and copies ran while one was open for 1% of the time, Pallas kernels for 0%

profile of v5, /device:TPU:1, one launch (start us, length us, event | category | flops | bytes accessed | tf_op | source)
XLA Modules:
  0.0 132.6 jit_solution(10005842208011449222)
XLA Ops:
  0.0 0.0 copy-start.1
  0.0 0.0 copy-start.3
  0.0 0.0 copy-start.4
  0.0 0.0 copy-start.2
  0.0 1.2 reshape.159
  1.2 0.9 copy.19
  2.1 11.6 %all-to-all-start = ((bf16[64,16,128]{2,1,0:T(8,128)(2,1)}), bf16[64,16,128]{2,1,0:T(8,128)(2,1)S(1)}, u32[]{:S(2)}, u32[]{:S(2)}) async-start(bf16[64,16,128]{2,1,0:T(8,128)(2,1)} %copy.19), calls=%async_computation | async-start | bytes 524288 | tf_op jit(solution)/shard_map/all_to_all | solution.py:306
  13.7 12.0 %all-to-all-done = bf16[64,16,128]{2,1,0:T(8,128)(2,1)S(1)} async-done(((bf16[64,16,128]{2,1,0:T(8,128)(2,1)}), bf16[64,16,128]{2,1,0:T(8,128)(2,1)S(1)}, u32[]{:S(2)}, u32[]{:S(2)}) %all-to-all-start) | async-done | bytes 262176 | tf_op jit(solution)/shard_map/all_to_all | solution.py:306
  25.7 0.2 reshape.161
  25.9 0.5 convolution_bitcast_fusion
  26.4 0.5 fusion.39
  26.9 0.8 copy.22
  27.6 6.0 %all-to-all-start.1 = ((bf16[64,4,256]{2,1,0:T(4,128)(2,1)}), bf16[64,4,256]{2,1,0:T(4,128)(2,1)S(1)}, u32[]{:S(2)}, u32[]{:S(2)}) async-start(bf16[64,4,256]{2,1,0:T(4,128)(2,1)} %copy.22), calls=%async_computation.1 | async-start | bytes 262144 | tf_op jit(solution)/shard_map/all_to_all | solution.py:319
  33.7 0.0 copy-done.1
  33.7 0.1 reduce
  33.8 0.0 copy-done.3
  33.8 0.6 broadcast_in_dim.7.refs_3_
  34.4 0.0 copy-done.4
  34.4 0.6 broadcast_in_dim.6.refs_2_
  35.0 9.0 %all-to-all-done.1 = bf16[64,4,256]{2,1,0:T(4,128)(2,1)S(1)} async-done(((bf16[64,4,256]{2,1,0:T(4,128)(2,1)}), bf16[64,4,256]{2,1,0:T(4,128)(2,1)S(1)}, u32[]{:S(2)}, u32[]{:S(2)}) %all-to-all-start.1) | async-done | bytes 131104 | tf_op jit(solution)/shard_map/all_to_all | solution.py:319
  44.0 0.1 fusion.77
  44.1 0.1 copy.23
  44.2 0.0 copy-done.2
  44.2 2.7 %fusion.73 = f32[4,1,8,896]{3,2,0,1:T(8,128)S(1)} fusion(bf16[4,8,2048]{2,1,0:T(8,128)(2,1)S(1)} %bitcast.199, bf16[1,2048,896]{2,1,0:T(8,128)(2,1)} %param.7, f32[4,896]{1,0:T(4,128)S(1)} %copy-done.2), kind=kOutput, calls=%fused_computation.29 | convolution fusion | flops 117469184 | bytes 3930112 | tf_op jit(solution)/shard_map/fmkb,mbs->fmks/dot_general | solution.py:332
  46.9 0.0 copy-start
  46.9 5.5 %fusion.68.refs_1_ = f32[4,8,896]{2,1,0:T(8,128)} fusion(bf16[1,2048,896]{2,1,0:T(8,128)(2,1)} %param.7, f32[4,2048]{1,0:T(4,128)S(1)} %bitcast.202, f32[4,1,8,896]{3,2,0,1:T(8,128)S(1)} %fusion.73, f32[4,896]{1,0:T(4,128)S(1)} %copy-done.2), kind=kOutput, calls=%fused_computation.28 | convolution fusion | flops 235098112 | bytes 3946496 | tf_op jit(solution)/shard_map/fmkb,mbs->fmks/dot_general | solution.py:345
  52.4 0.0 copy-done
  52.4 45.9 %shard_map.64 = (f32[4,8,896]{2,1,0:T(8,128)}, f32[4,8,896]{2,1,0:T(8,128)}, f32[1,128]{1,0:T(1,128)}) custom-call(f32[4,8,896]{2,1,0:T(8,128)} %bitcast.198, f32[4,8,896]{2,1,0:T(8,128)} %fusion.68.refs_1_, f32[4,1,896]{2,1,0:T(1,128)} %broadcast_in_dim.6.refs_2_, f32[4,2,1,896]{3,2,1,0:T(1,128)} %broadcast_in_dim.7.refs_3_), custom_call_target="tpu_custom_call" | custom-call | tf_op jit(solution)/shard_map/pallas_call | solution.py:249
  98.4 5.5 %fusion.58.refs_1_ = f32[4,8,896]{2,1,0:T(8,128)} fusion(bf16[1,2048,896]{2,1,0:T(8,128)(2,1)} %param.7, f32[4,2048]{1,0:T(4,128)S(1)} %bitcast.203, f32[4,8,896]{2,1,0:T(8,128)} %get-tuple-element.8.refs_0_, f32[4,896]{1,0:T(4,128)S(1)} %copy-done.2), kind=kOutput, calls=%fused_computation.26 | convolution fusion | flops 235098112 | bytes 3946496 | tf_op jit(solution)/shard_map/fmkb,mbs->fmks/dot_general | solution.py:345
  103.9 27.1 %shard_map.65 = f32[4,8,896]{2,1,0:T(8,128)} custom-call(f32[4,8,896]{2,1,0:T(8,128)} %get-tuple-element.8.refs_0_, f32[4,8,896]{2,1,0:T(8,128)} %fusion.58.refs_1_, f32[4,1,896]{2,1,0:T(1,128)} %broadcast_in_dim.6.refs_2_, f32[4,2,1,896]{3,2,1,0:T(1,128)} %broadcast_in_dim.7.refs_3_, f32[4,8,896]{2,1,0:T(8,128)} %get-tuple-element.9.refs_4_, ...), custom_call_target="tpu_custom_call" | custom-call | tf_op jit(solution)/shard_map/pallas_call | solution.py:249
  131.0 1.6 %copy.35 = f32[4,1,8,896]{3,2,1,0:T(8,128)} copy(f32[4,1,8,896]{3,2,1,0:T(8,128)} %bitcast.201) | data formatting | bytes 229376
  (3 shorter events, 0.1 us)
Async XLA Ops:
  0.0 33.7 %copy-start.1 = (f32[4,1,2048]{2,1,0:T(1,128)S(1)}, f32[4,1,2048]{2,1,0:T(1,128)}, u32[]{:S(2)}) copy-start(f32[4,1,2048]{2,1,0:T(1,128)} %param.9) | copy-start | bytes 98308
  0.0 33.8 %copy-start.3 = (f32[4,2,896]{2,1,0:T(2,128)S(1)}, f32[4,2,896]{2,1,0:T(2,128)}, u32[]{:S(2)}) copy-start(f32[4,2,896]{2,1,0:T(2,128)} %param.11) | copy-start | bytes 86020
  0.0 34.4 %copy-start.4 = (f32[4,896]{1,0:T(4,128)S(1)}, f32[4,896]{1,0:T(4,128)}, u32[]{:S(2)}) copy-start(f32[4,896]{1,0:T(4,128)} %param.10) | copy-start | bytes 43012
  0.0 44.2 %copy-start.2 = (f32[4,896]{1,0:T(4,128)S(1)}, f32[4,896]{1,0:T(4,128)}, u32[]{:S(2)}) copy-start(f32[4,896]{1,0:T(4,128)} %param.8) | copy-start | bytes 43012
  2.1 23.6 %all-to-all-start = ((bf16[64,16,128]{2,1,0:T(8,128)(2,1)}), bf16[64,16,128]{2,1,0:T(8,128)(2,1)S(1)}, u32[]{:S(2)}, u32[]{:S(2)}) async-start(bf16[64,16,128]{2,1,0:T(8,128)(2,1)} %copy.19), calls=%async_computation | async-start | bytes 524288 | tf_op jit(solution)/shard_map/all_to_all | solution.py:306
  27.6 16.4 %all-to-all-start.1 = ((bf16[64,4,256]{2,1,0:T(4,128)(2,1)}), bf16[64,4,256]{2,1,0:T(4,128)(2,1)S(1)}, u32[]{:S(2)}, u32[]{:S(2)}) async-start(bf16[64,4,256]{2,1,0:T(4,128)(2,1)} %copy.22), calls=%async_computation.1 | async-start | bytes 262144 | tf_op jit(solution)/shard_map/all_to_all | solution.py:319
  46.9 5.5 %copy-start = (f32[4,1,8,896]{3,2,0,1:T(8,128)}, f32[4,1,8,896]{3,2,0,1:T(8,128)S(1)}, u32[]{:S(2)}) copy-start(f32[4,1,8,896]{3,2,0,1:T(8,128)S(1)} %fusion.73) | copy-start | bytes 344068

commit v6 on v5

--- a/solution.py
+++ b/solution.py
@@ -119,6 +119,13 @@
     return jnp.sum(picked, axis=1, keepdims=True)
 
 
+def group_size(stage):
+    size = 1
+    for _, extent in stage[1]:
+        size *= extent
+    return size
+
+
 def cg_kernel(first, axis_names, stages, *refs):
     if first:
         (d_ref, cb_ref, diag_ref, pm_ref, est_ref, next_ref, norm_ref,
@@ -129,26 +136,37 @@
     me = {name: lax.axis_index(name) for name in axis_names}
 
     def place(stage):
-        axis, stride, size = stage
-        own = lax.rem(me[axis] // stride, size)
-        root = me[axis] - own * stride
+        axis, dims = stage
+        own = 0
+        root = me[axis]
+        scale = 1
+        for stride, size in dims:
+            digit = lax.rem(me[axis] // stride, size)
+            own = own + digit * scale
+            root = root - digit * stride
+            scale *= size
 
         def device(other):
-            return tuple(root + other * stride if name == axis else me[name] for name in axis_names)
+            coord = root
+            scale = 1
+            for stride, size in dims:
+                coord = coord + lax.rem(other // scale, size) * stride
+                scale *= size
+            return tuple(coord if name == axis else me[name] for name in axis_names)
 
         return own, device
 
     barrier = pltpu.get_barrier_semaphore()
     for stage in stages:
         own, device = place(stage)
-        for step in range(1, stage[2]):
-            other = lax.rem(own + step, stage[2])
+        for step in range(1, group_size(stage)):
+            other = lax.rem(own + step, group_size(stage))
             pl.semaphore_signal(barrier, 1, device_id=device(other), device_id_type=MESH)
-    pl.semaphore_wait(barrier, sum(size - 1 for _, _, size in stages))
+    pl.semaphore_wait(barrier, sum(group_size(stage) - 1 for stage in stages))
 
     def exchange_start(stage, src, recv, base, send_sems, recv_sems):
         own, device = place(stage)
-        size = stage[2]
+        size = group_size(stage)
 
         def copy_to(other, slot):
             return pltpu.make_async_remote_copy(
@@ -188,7 +206,7 @@
 
     def row_stage(stage, src):
         base = counter["slot"]
-        counter["slot"] += stage[2]
+        counter["slot"] += group_size(stage)
         return exchange_start(stage, src, recv_rows, base, r_send, r_recv)
 
     def reduce_rest(value):
@@ -238,9 +256,9 @@
 
 def cg_step(first, axis_names, stages, d, cb, diag, pm, *extra):
     reductions = 2 if first else 1
-    slots = reductions * sum(size for _, _, size in stages)
+    slots = reductions * sum(group_size(stage) for stage in stages)
     rounds = reductions * len(stages)
-    nz = stages[0][2]
+    nz = group_size(stages[0])
     vector = jax.ShapeDtypeStruct(d.shape, jnp.float32)
     row = jax.ShapeDtypeStruct((1, 128), jnp.float32)
     out_shape = (vector, vector, row) if first else vector
@@ -334,7 +352,14 @@
         )
 
         assert resident_modes == 1
-        cg_stages = [("freq", 1, freq_devices)] + mode_stages
+        if mode_devices % 16 == 0:
+            cg_stages = [
+                ("freq", [(1, freq_devices)]),
+                ("ma", [(1, 2), (16, mode_devices // 16)]),
+                ("ma", [(2, 8)]),
+            ]
+        else:
+            cg_stages = [("freq", [(1, freq_devices)]), ("ma", [(1, mode_devices)])]
         diag_rows = prior_diagonal[:, None, :]
         mode_rows4 = prior_modes[:, :, None, :]
 

time: 133 us -> 132 us (level)
  no operation moved by 1% of the time
where the time goes in v6:
time: 132 us
  Pallas kernels  72.3 us (55%)
  waiting for transfers between devices  21 us (16%)
  starting transfers between devices  17.6 us (13%)
  matrix products  14.7 us (11%)
  local copies, waits for them, and re-layouts  5.91 us (4%)
    pallas_call x2, Pallas kernels, cg_step(): pl.pallas_call(functools.partial(cg_kernel, first, axis_names, stages), o...  72.3 us
    all_to_all x1, waiting for transfers between devices, shards(): received = lax.all_to_all(send, 'ma', 0, 0, tiled=True)  12 us
    all_to_all x1, starting transfers between devices, shards(): received = lax.all_to_all(send, 'ma', 0, 0, tiled=True)  11.6 us
    dot_general x2, matrix products, beam_back(): jnp.einsum('fmkb,mbs->fmks', heard, beam_transfer, preferred_element_type...  11.1 us
    all_to_all x1, waiting for transfers between devices, shards(): back_rows = lax.all_to_all(mode_rows, 'ma', 0, 0, tiled=True)  8.99 us
    all_to_all x1, starting transfers between devices, shards(): back_rows = lax.all_to_all(mode_rows, 'ma', 0, 0, tiled=True)  6.03 us
    dot_general x1, matrix products, shards(): jnp.einsum('fmkb,mbs->fmks', weighted, beam_transfer, preferred_element_t...  2.68 us
  transfers between devices with their start and end apart: 2, of which 2 were waited for; matrix products, arithmetic and copies ran while one was open for 1% of the time, Pallas kernels for 0%

profile of v6, /device:TPU:1, one launch (start us, length us, event | category | flops | bytes accessed | tf_op | source)
XLA Modules:
  0.0 131.8 jit_solution(14896292959296466517)
XLA Ops:
  0.0 0.0 copy-start.1
  0.0 0.0 copy-start.3
  0.0 0.0 copy-start.4
  0.0 0.0 copy-start.2
  0.0 1.2 reshape.159
  1.2 0.9 copy.19
  2.1 11.6 %all-to-all-start = ((bf16[64,16,128]{2,1,0:T(8,128)(2,1)}), bf16[64,16,128]{2,1,0:T(8,128)(2,1)S(1)}, u32[]{:S(2)}, u32[]{:S(2)}) async-start(bf16[64,16,128]{2,1,0:T(8,128)(2,1)} %copy.19), calls=%async_computation | async-start | bytes 524288 | tf_op jit(solution)/shard_map/all_to_all | solution.py:324
  13.7 12.0 %all-to-all-done = bf16[64,16,128]{2,1,0:T(8,128)(2,1)S(1)} async-done(((bf16[64,16,128]{2,1,0:T(8,128)(2,1)}), bf16[64,16,128]{2,1,0:T(8,128)(2,1)S(1)}, u32[]{:S(2)}, u32[]{:S(2)}) %all-to-all-start) | async-done | bytes 262176 | tf_op jit(solution)/shard_map/all_to_all | solution.py:324
  25.7 0.2 reshape.161
  25.9 0.5 convolution_bitcast_fusion
  26.4 0.5 fusion.39
  26.9 0.8 copy.22
  27.6 6.0 %all-to-all-start.1 = ((bf16[64,4,256]{2,1,0:T(4,128)(2,1)}), bf16[64,4,256]{2,1,0:T(4,128)(2,1)S(1)}, u32[]{:S(2)}, u32[]{:S(2)}) async-start(bf16[64,4,256]{2,1,0:T(4,128)(2,1)} %copy.22), calls=%async_computation.1 | async-start | bytes 262144 | tf_op jit(solution)/shard_map/all_to_all | solution.py:337
  33.7 0.0 copy-done.1
  33.7 0.1 reduce
  33.8 0.0 copy-done.3
  33.8 0.6 broadcast_in_dim.7.refs_3_
  34.4 0.0 copy-done.4
  34.4 0.6 broadcast_in_dim.6.refs_2_
  35.0 9.0 %all-to-all-done.1 = bf16[64,4,256]{2,1,0:T(4,128)(2,1)S(1)} async-done(((bf16[64,4,256]{2,1,0:T(4,128)(2,1)}), bf16[64,4,256]{2,1,0:T(4,128)(2,1)S(1)}, u32[]{:S(2)}, u32[]{:S(2)}) %all-to-all-start.1) | async-done | bytes 131104 | tf_op jit(solution)/shard_map/all_to_all | solution.py:337
  44.0 0.1 fusion.77
  44.1 0.1 copy.23
  44.2 0.0 copy-done.2
  44.2 2.7 %fusion.73 = f32[4,1,8,896]{3,2,0,1:T(8,128)S(1)} fusion(bf16[4,8,2048]{2,1,0:T(8,128)(2,1)S(1)} %bitcast.199, bf16[1,2048,896]{2,1,0:T(8,128)(2,1)} %param.7, f32[4,896]{1,0:T(4,128)S(1)} %copy-done.2), kind=kOutput, calls=%fused_computation.29 | convolution fusion | flops 117469184 | bytes 3930112 | tf_op jit(solution)/shard_map/fmkb,mbs->fmks/dot_general | solution.py:350
  46.9 0.0 copy-start
  46.9 5.5 %fusion.68.refs_1_ = f32[4,8,896]{2,1,0:T(8,128)} fusion(bf16[1,2048,896]{2,1,0:T(8,128)(2,1)} %param.7, f32[4,2048]{1,0:T(4,128)S(1)} %bitcast.202, f32[4,1,8,896]{3,2,0,1:T(8,128)S(1)} %fusion.73, f32[4,896]{1,0:T(4,128)S(1)} %copy-done.2), kind=kOutput, calls=%fused_computation.28 | convolution fusion | flops 235098112 | bytes 3946496 | tf_op jit(solution)/shard_map/fmkb,mbs->fmks/dot_general | solution.py:370
  52.4 0.0 copy-done
  52.4 45.5 %shard_map.64 = (f32[4,8,896]{2,1,0:T(8,128)}, f32[4,8,896]{2,1,0:T(8,128)}, f32[1,128]{1,0:T(1,128)}) custom-call(f32[4,8,896]{2,1,0:T(8,128)} %bitcast.198, f32[4,8,896]{2,1,0:T(8,128)} %fusion.68.refs_1_, f32[4,1,896]{2,1,0:T(1,128)} %broadcast_in_dim.6.refs_2_, f32[4,2,1,896]{3,2,1,0:T(1,128)} %broadcast_in_dim.7.refs_3_), custom_call_target="tpu_custom_call" | custom-call | tf_op jit(solution)/shard_map/pallas_call | solution.py:267
  97.9 5.5 %fusion.58.refs_1_ = f32[4,8,896]{2,1,0:T(8,128)} fusion(bf16[1,2048,896]{2,1,0:T(8,128)(2,1)} %param.7, f32[4,2048]{1,0:T(4,128)S(1)} %bitcast.203, f32[4,8,896]{2,1,0:T(8,128)} %get-tuple-element.8.refs_0_, f32[4,896]{1,0:T(4,128)S(1)} %copy-done.2), kind=kOutput, calls=%fused_computation.26 | convolution fusion | flops 235098112 | bytes 3946496 | tf_op jit(solution)/shard_map/fmkb,mbs->fmks/dot_general | solution.py:370
  103.4 26.8 %shard_map.65 = f32[4,8,896]{2,1,0:T(8,128)} custom-call(f32[4,8,896]{2,1,0:T(8,128)} %get-tuple-element.8.refs_0_, f32[4,8,896]{2,1,0:T(8,128)} %fusion.58.refs_1_, f32[4,1,896]{2,1,0:T(1,128)} %broadcast_in_dim.6.refs_2_, f32[4,2,1,896]{3,2,1,0:T(1,128)} %broadcast_in_dim.7.refs_3_, f32[4,8,896]{2,1,0:T(8,128)} %get-tuple-element.9.refs_4_, ...), custom_call_target="tpu_custom_call" | custom-call | tf_op jit(solution)/shard_map/pallas_call | solution.py:267
  130.2 1.6 %copy.35 = f32[4,1,8,896]{3,2,1,0:T(8,128)} copy(f32[4,1,8,896]{3,2,1,0:T(8,128)} %bitcast.201) | data formatting | bytes 229376
  (3 shorter events, 0.1 us)
Async XLA Ops:
  0.0 33.7 %copy-start.1 = (f32[4,1,2048]{2,1,0:T(1,128)S(1)}, f32[4,1,2048]{2,1,0:T(1,128)}, u32[]{:S(2)}) copy-start(f32[4,1,2048]{2,1,0:T(1,128)} %param.9) | copy-start | bytes 98308
  0.0 33.8 %copy-start.3 = (f32[4,2,896]{2,1,0:T(2,128)S(1)}, f32[4,2,896]{2,1,0:T(2,128)}, u32[]{:S(2)}) copy-start(f32[4,2,896]{2,1,0:T(2,128)} %param.11) | copy-start | bytes 86020
  0.0 34.4 %copy-start.4 = (f32[4,896]{1,0:T(4,128)S(1)}, f32[4,896]{1,0:T(4,128)}, u32[]{:S(2)}) copy-start(f32[4,896]{1,0:T(4,128)} %param.10) | copy-start | bytes 43012
  0.0 44.2 %copy-start.2 = (f32[4,896]{1,0:T(4,128)S(1)}, f32[4,896]{1,0:T(4,128)}, u32[]{:S(2)}) copy-start(f32[4,896]{1,0:T(4,128)} %param.8) | copy-start | bytes 43012
  2.1 23.6 %all-to-all-start = ((bf16[64,16,128]{2,1,0:T(8,128)(2,1)}), bf16[64,16,128]{2,1,0:T(8,128)(2,1)S(1)}, u32[]{:S(2)}, u32[]{:S(2)}) async-start(bf16[64,16,128]{2,1,0:T(8,128)(2,1)} %copy.19), calls=%async_computation | async-start | bytes 524288 | tf_op jit(solution)/shard_map/all_to_all | solution.py:324
  27.6 16.4 %all-to-all-start.1 = ((bf16[64,4,256]{2,1,0:T(4,128)(2,1)}), bf16[64,4,256]{2,1,0:T(4,128)(2,1)S(1)}, u32[]{:S(2)}, u32[]{:S(2)}) async-start(bf16[64,4,256]{2,1,0:T(4,128)(2,1)} %copy.22), calls=%async_computation.1 | async-start | bytes 262144 | tf_op jit(solution)/shard_map/all_to_all | solution.py:337
  46.9 5.5 %copy-start = (f32[4,1,8,896]{3,2,0,1:T(8,128)}, f32[4,1,8,896]{3,2,0,1:T(8,128)S(1)}, u32[]{:S(2)}) copy-start(f32[4,1,8,896]{3,2,0,1:T(8,128)S(1)} %fusion.73) | copy-start | bytes 344068

commit v7 on v6

--- a/solution.py
+++ b/solution.py
@@ -191,9 +191,9 @@
             other = lax.rem(own + step, size)
             copy_to(other, other).wait_recv()
         sent.append(state)
-        total = recv[base]
+        total = recv[base].astype(jnp.float32)
         for slot in range(1, size):
-            total = total + recv[base + slot]
+            total = total + recv[base + slot].astype(jnp.float32)
         return total
 
     counter = {"row": 0, "slot": 0}
@@ -220,7 +220,7 @@
     pm = pm_ref[...]
     count = d.shape[1]
     for rank in range(pm.shape[1]):
-        part[rank] = jnp.sum(pm[:, rank] * d, axis=0)
+        part[rank] = jnp.sum(pm[:, rank] * d, axis=0).astype(part.dtype)
     if first:
         row = to_row([column_sum(d * (cb + diag * d)), column_sum(d * d)])
     else:
@@ -270,9 +270,9 @@
         in_specs=[vmem] * (4 + len(extra)),
         out_specs=(vmem, vmem, vmem) if first else vmem,
         scratch_shapes=[
-            pltpu.VMEM(part_shape, jnp.float32),
+            pltpu.VMEM(part_shape, jnp.bfloat16),
             pltpu.VMEM((rounds, 1, 128), jnp.float32),
-            pltpu.VMEM((nz,) + part_shape, jnp.float32),
+            pltpu.VMEM((nz,) + part_shape, jnp.bfloat16),
             pltpu.VMEM((slots, 1, 128), jnp.float32),
             pltpu.SemaphoreType.DMA((nz,)),
             pltpu.SemaphoreType.DMA((nz,)),

time: 132 us -> 122 us (0.924)
  Pallas kernels: 72.3 us -> 62.4 us
    pallas_call x2, Pallas kernels: 72.3 us -> 62.4 us  [cg_step(): pl.pallas_call(functools.partial(cg_kernel, first, axis_names, stages), o...]
where the time goes in v7:
time: 122 us
  Pallas kernels  62.4 us (51%)
  waiting for transfers between devices  21 us (17%)
  starting transfers between devices  17.6 us (14%)
  matrix products  14.7 us (12%)
  local copies, waits for them, and re-layouts  5.91 us (5%)
    pallas_call x2, Pallas kernels, cg_step(): pl.pallas_call(functools.partial(cg_kernel, first, axis_names, stages), o...  62.4 us
    all_to_all x1, waiting for transfers between devices, shards(): received = lax.all_to_all(send, 'ma', 0, 0, tiled=True)  12 us
    all_to_all x1, starting transfers between devices, shards(): received = lax.all_to_all(send, 'ma', 0, 0, tiled=True)  11.6 us
    dot_general x2, matrix products, beam_back(): jnp.einsum('fmkb,mbs->fmks', heard, beam_transfer, preferred_element_type...  11.1 us
    all_to_all x1, waiting for transfers between devices, shards(): back_rows = lax.all_to_all(mode_rows, 'ma', 0, 0, tiled=True)  8.99 us
    all_to_all x1, starting transfers between devices, shards(): back_rows = lax.all_to_all(mode_rows, 'ma', 0, 0, tiled=True)  6.03 us
    dot_general x1, matrix products, shards(): jnp.einsum('fmkb,mbs->fmks', weighted, beam_transfer, preferred_element_t...  2.68 us
  transfers between devices with their start and end apart: 2, of which 2 were waited for; matrix products, arithmetic and copies ran while one was open for 1% of the time, Pallas kernels for 0%

profile of v7, /device:TPU:1, one launch (start us, length us, event | category | flops | bytes accessed | tf_op | source)
XLA Modules:
  0.0 121.9 jit_solution(12402112590282673022)
XLA Ops:
  0.0 0.0 copy-start.1
  0.0 0.0 copy-start.3
  0.0 0.0 copy-start.4
  0.0 0.0 copy-start.2
  0.0 1.2 reshape.159
  1.2 0.9 copy.19
  2.1 11.6 %all-to-all-start = ((bf16[64,16,128]{2,1,0:T(8,128)(2,1)}), bf16[64,16,128]{2,1,0:T(8,128)(2,1)S(1)}, u32[]{:S(2)}, u32[]{:S(2)}) async-start(bf16[64,16,128]{2,1,0:T(8,128)(2,1)} %copy.19), calls=%async_computation | async-start | bytes 524288 | tf_op jit(solution)/shard_map/all_to_all | solution.py:324
  13.7 12.0 %all-to-all-done = bf16[64,16,128]{2,1,0:T(8,128)(2,1)S(1)} async-done(((bf16[64,16,128]{2,1,0:T(8,128)(2,1)}), bf16[64,16,128]{2,1,0:T(8,128)(2,1)S(1)}, u32[]{:S(2)}, u32[]{:S(2)}) %all-to-all-start) | async-done | bytes 262176 | tf_op jit(solution)/shard_map/all_to_all | solution.py:324
  25.7 0.2 reshape.161
  25.9 0.5 convolution_bitcast_fusion
  26.4 0.5 fusion.39
  26.9 0.8 copy.22
  27.6 6.0 %all-to-all-start.1 = ((bf16[64,4,256]{2,1,0:T(4,128)(2,1)}), bf16[64,4,256]{2,1,0:T(4,128)(2,1)S(1)}, u32[]{:S(2)}, u32[]{:S(2)}) async-start(bf16[64,4,256]{2,1,0:T(4,128)(2,1)} %copy.22), calls=%async_computation.1 | async-start | bytes 262144 | tf_op jit(solution)/shard_map/all_to_all | solution.py:337
  33.7 0.0 copy-done.1
  33.7 0.1 reduce
  33.8 0.0 copy-done.3
  33.8 0.6 broadcast_in_dim.7.refs_3_
  34.4 0.0 copy-done.4
  34.4 0.6 broadcast_in_dim.6.refs_2_
  35.0 9.0 %all-to-all-done.1 = bf16[64,4,256]{2,1,0:T(4,128)(2,1)S(1)} async-done(((bf16[64,4,256]{2,1,0:T(4,128)(2,1)}), bf16[64,4,256]{2,1,0:T(4,128)(2,1)S(1)}, u32[]{:S(2)}, u32[]{:S(2)}) %all-to-all-start.1) | async-done | bytes 131104 | tf_op jit(solution)/shard_map/all_to_all | solution.py:337
  44.0 0.1 fusion.77
  44.1 0.1 copy.23
  44.2 0.0 copy-done.2
  44.2 2.7 %fusion.73 = f32[4,1,8,896]{3,2,0,1:T(8,128)S(1)} fusion(bf16[4,8,2048]{2,1,0:T(8,128)(2,1)S(1)} %bitcast.199, bf16[1,2048,896]{2,1,0:T(8,128)(2,1)} %param.7, f32[4,896]{1,0:T(4,128)S(1)} %copy-done.2), kind=kOutput, calls=%fused_computation.29 | convolution fusion | flops 117469184 | bytes 3930112 | tf_op jit(solution)/shard_map/fmkb,mbs->fmks/dot_general | solution.py:350
  46.9 0.0 copy-start
  46.9 5.5 %fusion.68.refs_1_ = f32[4,8,896]{2,1,0:T(8,128)} fusion(bf16[1,2048,896]{2,1,0:T(8,128)(2,1)} %param.7, f32[4,2048]{1,0:T(4,128)S(1)} %bitcast.202, f32[4,1,8,896]{3,2,0,1:T(8,128)S(1)} %fusion.73, f32[4,896]{1,0:T(4,128)S(1)} %copy-done.2), kind=kOutput, calls=%fused_computation.28 | convolution fusion | flops 235098112 | bytes 3946496 | tf_op jit(solution)/shard_map/fmkb,mbs->fmks/dot_general | solution.py:370
  52.4 0.0 copy-done
  52.4 40.6 %shard_map.64 = (f32[4,8,896]{2,1,0:T(8,128)}, f32[4,8,896]{2,1,0:T(8,128)}, f32[1,128]{1,0:T(1,128)}) custom-call(f32[4,8,896]{2,1,0:T(8,128)} %bitcast.198, f32[4,8,896]{2,1,0:T(8,128)} %fusion.68.refs_1_, f32[4,1,896]{2,1,0:T(1,128)} %broadcast_in_dim.6.refs_2_, f32[4,2,1,896]{3,2,1,0:T(1,128)} %broadcast_in_dim.7.refs_3_), custom_call_target="tpu_custom_call" | custom-call | tf_op jit(solution)/shard_map/pallas_call | solution.py:267
  93.0 5.5 %fusion.58.refs_1_ = f32[4,8,896]{2,1,0:T(8,128)} fusion(bf16[1,2048,896]{2,1,0:T(8,128)(2,1)} %param.7, f32[4,2048]{1,0:T(4,128)S(1)} %bitcast.203, f32[4,8,896]{2,1,0:T(8,128)} %get-tuple-element.8.refs_0_, f32[4,896]{1,0:T(4,128)S(1)} %copy-done.2), kind=kOutput, calls=%fused_computation.26 | convolution fusion | flops 235098112 | bytes 3946496 | tf_op jit(solution)/shard_map/fmkb,mbs->fmks/dot_general | solution.py:370
  98.5 21.8 %shard_map.65 = f32[4,8,896]{2,1,0:T(8,128)} custom-call(f32[4,8,896]{2,1,0:T(8,128)} %get-tuple-element.8.refs_0_, f32[4,8,896]{2,1,0:T(8,128)} %fusion.58.refs_1_, f32[4,1,896]{2,1,0:T(1,128)} %broadcast_in_dim.6.refs_2_, f32[4,2,1,896]{3,2,1,0:T(1,128)} %broadcast_in_dim.7.refs_3_, f32[4,8,896]{2,1,0:T(8,128)} %get-tuple-element.9.refs_4_, ...), custom_call_target="tpu_custom_call" | custom-call | tf_op jit(solution)/shard_map/pallas_call | solution.py:267
  120.3 1.6 %copy.35 = f32[4,1,8,896]{3,2,1,0:T(8,128)} copy(f32[4,1,8,896]{3,2,1,0:T(8,128)} %bitcast.201) | data formatting | bytes 229376
  (3 shorter events, 0.1 us)
Async XLA Ops:
  0.0 33.7 %copy-start.1 = (f32[4,1,2048]{2,1,0:T(1,128)S(1)}, f32[4,1,2048]{2,1,0:T(1,128)}, u32[]{:S(2)}) copy-start(f32[4,1,2048]{2,1,0:T(1,128)} %param.9) | copy-start | bytes 98308
  0.0 33.8 %copy-start.3 = (f32[4,2,896]{2,1,0:T(2,128)S(1)}, f32[4,2,896]{2,1,0:T(2,128)}, u32[]{:S(2)}) copy-start(f32[4,2,896]{2,1,0:T(2,128)} %param.11) | copy-start | bytes 86020
  0.0 34.4 %copy-start.4 = (f32[4,896]{1,0:T(4,128)S(1)}, f32[4,896]{1,0:T(4,128)}, u32[]{:S(2)}) copy-start(f32[4,896]{1,0:T(4,128)} %param.10) | copy-start | bytes 43012
  0.0 44.2 %copy-start.2 = (f32[4,896]{1,0:T(4,128)S(1)}, f32[4,896]{1,0:T(4,128)}, u32[]{:S(2)}) copy-start(f32[4,896]{1,0:T(4,128)} %param.8) | copy-start | bytes 43012
  2.1 23.6 %all-to-all-start = ((bf16[64,16,128]{2,1,0:T(8,128)(2,1)}), bf16[64,16,128]{2,1,0:T(8,128)(2,1)S(1)}, u32[]{:S(2)}, u32[]{:S(2)}) async-start(bf16[64,16,128]{2,1,0:T(8,128)(2,1)} %copy.19), calls=%async_computation | async-start | bytes 524288 | tf_op jit(solution)/shard_map/all_to_all | solution.py:324
  27.6 16.4 %all-to-all-start.1 = ((bf16[64,4,256]{2,1,0:T(4,128)(2,1)}), bf16[64,4,256]{2,1,0:T(4,128)(2,1)S(1)}, u32[]{:S(2)}, u32[]{:S(2)}) async-start(bf16[64,4,256]{2,1,0:T(4,128)(2,1)} %copy.22), calls=%async_computation.1 | async-start | bytes 262144 | tf_op jit(solution)/shard_map/all_to_all | solution.py:337
  46.9 5.5 %copy-start = (f32[4,1,8,896]{3,2,0,1:T(8,128)}, f32[4,1,8,896]{3,2,0,1:T(8,128)S(1)}, u32[]{:S(2)}) copy-start(f32[4,1,8,896]{3,2,0,1:T(8,128)S(1)} %fusion.73) | copy-start | bytes 344068

commit v8 on v7

--- a/solution.py
+++ b/solution.py
@@ -128,10 +128,10 @@
 
 def cg_kernel(first, axis_names, stages, *refs):
     if first:
-        (d_ref, cb_ref, diag_ref, pm_ref, est_ref, next_ref, norm_ref,
+        (d_ref, beam_ref, chroma_ref, weight_ref, diag_ref, pm_ref, est_ref, next_ref, norm_ref,
          part, rows, recv_p, recv_rows, p_send, p_recv, r_send, r_recv) = refs
     else:
-        (d_ref, cb_ref, diag_ref, pm_ref, est_in_ref, norm_in_ref, est_ref,
+        (d_ref, beam_ref, chroma_ref, weight_ref, diag_ref, pm_ref, est_in_ref, norm_in_ref, est_ref,
          part, rows, recv_p, recv_rows, p_send, p_recv, r_send, r_recv) = refs
     me = {name: lax.axis_index(name) for name in axis_names}
 
@@ -162,6 +162,16 @@
         for step in range(1, group_size(stage)):
             other = lax.rem(own + step, group_size(stage))
             pl.semaphore_signal(barrier, 1, device_id=device(other), device_id_type=MESH)
+
+    d = d_ref[...]
+    chroma = chroma_ref[...]
+    channels, count, modes = d.shape
+    beam = beam_ref[...]
+    low = (chroma * d).astype(jnp.bfloat16).reshape(channels * count, modes)
+    seen = lax.dot_general(low, beam, (((1,), (1,)), ((), ())), preferred_element_type=jnp.float32)
+    heard = (weight_ref[...] * seen.reshape(channels, count, -1)).astype(jnp.bfloat16)
+    back = jnp.dot(heard.reshape(channels * count, -1), beam, preferred_element_type=jnp.float32)
+    cb = chroma * back.reshape(channels, count, modes)
     pl.semaphore_wait(barrier, sum(group_size(stage) - 1 for stage in stages))
 
     def exchange_start(stage, src, recv, base, send_sems, recv_sems):
@@ -214,8 +224,6 @@
             value = exchange_finish(row_stage(stage, next_row(value)))
         return value
 
-    d = d_ref[...]
-    cb = cb_ref[...]
     diag = diag_ref[...]
     pm = pm_ref[...]
     count = d.shape[1]
@@ -254,7 +262,7 @@
             copy_to(lax.rem(own + step, size), own).wait_send()
 
 
-def cg_step(first, axis_names, stages, d, cb, diag, pm, *extra):
+def cg_step(first, axis_names, stages, d, beam, chroma, weight, diag, pm, *extra):
     reductions = 2 if first else 1
     slots = reductions * sum(group_size(stage) for stage in stages)
     rounds = reductions * len(stages)
@@ -267,7 +275,7 @@
     return pl.pallas_call(
         functools.partial(cg_kernel, first, axis_names, stages),
         out_shape=out_shape,
-        in_specs=[vmem] * (4 + len(extra)),
+        in_specs=[vmem] * (6 + len(extra)),
         out_specs=(vmem, vmem, vmem) if first else vmem,
         scratch_shapes=[
             pltpu.VMEM(part_shape, jnp.bfloat16),
@@ -282,7 +290,7 @@
         compiler_params=pltpu.CompilerParams(
             collective_id=1 if first else 2, has_side_effects=True
         ),
-    )(d, cb, diag, pm, *extra)
+    )(d, beam, chroma, weight, diag, pm, *extra)
 
 
 def make_shards(mesh):
@@ -373,12 +381,10 @@
             return (chroma * back)[:, 0]
 
         direction = rhs[:, 0]
-        estimate, direction, norm_row = cg_step(
-            True, axis_names, cg_stages, direction, beam_back(direction[:, None]), diag_rows, mode_rows4
-        )
+        operands = (beam_transfer[0], chromatic_gain[:, None, :], noise_weight, diag_rows, mode_rows4)
+        estimate, direction, norm_row = cg_step(True, axis_names, cg_stages, direction, *operands)
         estimate = cg_step(
-            False, axis_names, cg_stages, direction, beam_back(direction[:, None]), diag_rows, mode_rows4,
-            estimate, norm_row,
+            False, axis_names, cg_stages, direction, *operands, estimate, norm_row
         )
         estimate = estimate[:, None]
         return estimate

time: 122 us -> 114 us (0.934)
  matrix products: 14.7 us -> 4.28 us
  Pallas kernels: 62.4 us -> 64.5 us
    dot_general x2 -> x0, matrix products: 11.1 us -> none  [beam_back(): jnp.einsum('fmkb,mbs->fmks', heard, beam_transfer, preferred_element_type...]
    pallas_call x2, Pallas kernels: 62.4 us -> 64.5 us  [cg_step(): pl.pallas_call(functools.partial(cg_kernel, first, axis_names, stages), o...]
  transfers between devices with their start and end apart: 2 -> 2, of which waited for: 2 -> 2; matrix products, arithmetic and copies ran while one was open for 1% -> 2% of each run, Pallas kernels for 0% -> 0%
where the time goes in v8:
time: 114 us
  Pallas kernels  64.5 us (57%)
  waiting for transfers between devices  20.4 us (18%)
  starting transfers between devices  17.7 us (16%)
  local copies, waits for them, and re-layouts  6.49 us (6%)
  matrix products  4.28 us (4%)
    pallas_call x2, Pallas kernels, cg_step(): pl.pallas_call(functools.partial(cg_kernel, first, axis_names, stages), o...  64.5 us
    all_to_all x1, waiting for transfers between devices, shards(): received = lax.all_to_all(send, 'ma', 0, 0, tiled=True)  12 us
    all_to_all x1, starting transfers between devices, shards(): received = lax.all_to_all(send, 'ma', 0, 0, tiled=True)  11.6 us
    all_to_all x1, waiting for transfers between devices, shards(): back_rows = lax.all_to_all(mode_rows, 'ma', 0, 0, tiled=True)  8.42 us
    all_to_all x1, starting transfers between devices, shards(): back_rows = lax.all_to_all(mode_rows, 'ma', 0, 0, tiled=True)  6.03 us
    dot_general x1, matrix products, shards(): jnp.einsum('fmkb,mbs->fmks', weighted, beam_transfer, preferred_element_t...  3.33 us
  transfers between devices with their start and end apart: 2, of which 2 were waited for; matrix products, arithmetic and copies ran while one was open for 2% of the time, Pallas kernels for 0%

profile of v8, /device:TPU:1, one launch (start us, length us, event | category | flops | bytes accessed | tf_op | source)
XLA Modules:
  0.0 113.6 jit_solution(10727638703855688452)
XLA Ops:
  0.0 0.0 copy-start.2
  0.0 0.0 copy-start.1
  0.0 0.0 copy-start.3
  0.0 0.0 copy-start
  0.0 1.2 %reshape.138 = bf16[4,2,8,8,2,128]{5,4,3,2,1,0:T(2,128)(2,1)S(1)} reshape(bf16[4,2,8,2048]{3,2,1,0:T(8,128)(2,1)} %param.6) | data formatting | bytes 524288 | tf_op jit(solution)/shard_map/reshape | solution.py:328
  1.2 0.9 copy.19
  2.1 11.6 %all-to-all-start = ((bf16[64,16,128]{2,1,0:T(8,128)(2,1)}), bf16[64,16,128]{2,1,0:T(8,128)(2,1)S(1)}, u32[]{:S(2)}, u32[]{:S(2)}) async-start(bf16[64,16,128]{2,1,0:T(8,128)(2,1)} %copy.19), calls=%async_computation | async-start | bytes 524288 | tf_op jit(solution)/shard_map/all_to_all | solution.py:332
  13.8 12.0 %all-to-all-done = bf16[64,16,128]{2,1,0:T(8,128)(2,1)S(1)} async-done(((bf16[64,16,128]{2,1,0:T(8,128)(2,1)}), bf16[64,16,128]{2,1,0:T(8,128)(2,1)S(1)}, u32[]{:S(2)}, u32[]{:S(2)}) %all-to-all-start) | async-done | bytes 262176 | tf_op jit(solution)/shard_map/all_to_all | solution.py:332
  25.7 0.2 reshape.140
  25.9 0.5 convolution_bitcast_fusion
  26.4 0.5 fusion.3
  26.9 0.8 copy.22
  27.6 6.0 %all-to-all-start.1 = ((bf16[64,4,256]{2,1,0:T(4,128)(2,1)}), bf16[64,4,256]{2,1,0:T(4,128)(2,1)S(1)}, u32[]{:S(2)}, u32[]{:S(2)}) async-start(bf16[64,4,256]{2,1,0:T(4,128)(2,1)} %copy.22), calls=%async_computation.1 | async-start | bytes 262144 | tf_op jit(solution)/shard_map/all_to_all | solution.py:345
  33.7 0.0 copy-done.2
  33.7 0.6 broadcast_in_dim.18.refs_5_
  34.3 0.0 copy-done.1
  34.3 0.6 broadcast_in_dim.16.refs_2_
  34.9 0.0 copy-done.3
  34.9 0.6 broadcast_in_dim.17.refs_4_
  35.5 0.0 copy-done
  35.5 0.1 reduce
  35.6 8.4 %all-to-all-done.1 = bf16[64,4,256]{2,1,0:T(4,128)(2,1)S(1)} async-done(((bf16[64,4,256]{2,1,0:T(4,128)(2,1)}), bf16[64,4,256]{2,1,0:T(4,128)(2,1)S(1)}, u32[]{:S(2)}, u32[]{:S(2)}) %all-to-all-start.1) | async-done | bytes 131104 | tf_op jit(solution)/shard_map/all_to_all | solution.py:345
  44.0 0.1 fusion.14
  44.1 0.1 copy.23
  44.2 3.3 %fusion.10.refs_0_ = f32[4,8,896]{2,1,0:T(8,128)} fusion(bf16[4,8,2048]{2,1,0:T(8,128)(2,1)S(1)} %bitcast.62, bf16[1,2048,896]{2,1,0:T(8,128)(2,1)} %param.7, f32[4,896]{1,0:T(4,128)S(1)} %copy-done.1), kind=kOutput, calls=%fused_computation.8 | convolution fusion | flops 117469184 | bytes 3930112 | tf_op jit(solution)/shard_map/fmkb,mbs->fmks/dot_general | solution.py:358
  47.5 41.6 %shard_map.64 = (f32[4,8,896]{2,1,0:T(8,128)}, f32[4,8,896]{2,1,0:T(8,128)}, f32[1,128]{1,0:T(1,128)}) custom-call(f32[4,8,896]{2,1,0:T(8,128)} %fusion.10.refs_0_, bf16[2048,896]{1,0:T(8,128)(2,1)} %bitcast.58, f32[4,1,896]{2,1,0:T(1,128)} %broadcast_in_dim.16.refs_2_, f32[4,1,2048]{2,1,0:T(1,128)} %refs_3_.3, f32[4,1,896]{2,1,0:T(1,128)} %broadcast_in_dim.17.refs_4_, ...), custom_call_target="tpu_custom_call" | custom-call | tf_op jit(solution)/shard_map/pallas_call | solution.py:275
  89.1 22.9 %shard_map.65 = f32[4,8,896]{2,1,0:T(8,128)} custom-call(f32[4,8,896]{2,1,0:T(8,128)} %get-tuple-element.8.refs_0_, bf16[2048,896]{1,0:T(8,128)(2,1)} %bitcast.59, f32[4,1,896]{2,1,0:T(1,128)} %broadcast_in_dim.16.refs_2_, f32[4,1,2048]{2,1,0:T(1,128)} %refs_3_.3, f32[4,1,896]{2,1,0:T(1,128)} %broadcast_in_dim.17.refs_4_, ...), custom_call_target="tpu_custom_call" | custom-call | tf_op jit(solution)/shard_map/pallas_call | solution.py:275
  112.1 1.6 %copy.32 = f32[4,1,8,896]{3,2,1,0:T(8,128)} copy(f32[4,1,8,896]{3,2,1,0:T(8,128)} %bitcast.64) | data formatting | bytes 229376
  (2 shorter events, 0.1 us)
Async XLA Ops:
  0.0 33.7 %copy-start.2 = (f32[4,2,896]{2,1,0:T(2,128)S(1)}, f32[4,2,896]{2,1,0:T(2,128)}, u32[]{:S(2)}) copy-start(f32[4,2,896]{2,1,0:T(2,128)} %param.11) | copy-start | bytes 86020
  0.0 34.3 %copy-start.1 = (f32[4,896]{1,0:T(4,128)S(1)}, f32[4,896]{1,0:T(4,128)}, u32[]{:S(2)}) copy-start(f32[4,896]{1,0:T(4,128)} %param.8) | copy-start | bytes 43012
  0.0 34.9 %copy-start.3 = (f32[4,896]{1,0:T(4,128)S(1)}, f32[4,896]{1,0:T(4,128)}, u32[]{:S(2)}) copy-start(f32[4,896]{1,0:T(4,128)} %param.10) | copy-start | bytes 43012
  0.0 35.5 %copy-start = (f32[4,1,2048]{2,1,0:T(1,128)S(1)}, f32[4,1,2048]{2,1,0:T(1,128)}, u32[]{:S(2)}) copy-start(f32[4,1,2048]{2,1,0:T(1,128)} %refs_3_.3) | copy-start | bytes 98308
  2.1 23.6 %all-to-all-start = ((bf16[64,16,128]{2,1,0:T(8,128)(2,1)}), bf16[64,16,128]{2,1,0:T(8,128)(2,1)S(1)}, u32[]{:S(2)}, u32[]{:S(2)}) async-start(bf16[64,16,128]{2,1,0:T(8,128)(2,1)} %copy.19), calls=%async_computation | async-start | bytes 524288 | tf_op jit(solution)/shard_map/all_to_all | solution.py:332
  27.6 16.4 %all-to-all-start.1 = ((bf16[64,4,256]{2,1,0:T(4,128)(2,1)}), bf16[64,4,256]{2,1,0:T(4,128)(2,1)S(1)}, u32[]{:S(2)}, u32[]{:S(2)}) async-start(bf16[64,4,256]{2,1,0:T(4,128)(2,1)} %copy.22), calls=%async_computation.1 | async-start | bytes 262144 | tf_op jit(solution)/shard_map/all_to_all | solution.py:345

commit v9 on v8

--- a/solution.py
+++ b/solution.py
@@ -126,13 +126,8 @@
     return size
 
 
-def cg_kernel(first, axis_names, stages, *refs):
-    if first:
-        (d_ref, beam_ref, chroma_ref, weight_ref, diag_ref, pm_ref, est_ref, next_ref, norm_ref,
-         part, rows, recv_p, recv_rows, p_send, p_recv, r_send, r_recv) = refs
-    else:
-        (d_ref, beam_ref, chroma_ref, weight_ref, diag_ref, pm_ref, est_in_ref, norm_in_ref, est_ref,
-         part, rows, recv_p, recv_rows, p_send, p_recv, r_send, r_recv) = refs
+def cg_kernel(axis_names, stages, d_ref, beam_ref, chroma_ref, weight_ref, diag_ref, pm_ref,
+              est_ref, next_ref, step_ref, parts, rows, recv_p, recv_rows, p_send, p_recv, r_send, r_recv):
     me = {name: lax.axis_index(name) for name in axis_names}
 
     def place(stage):
@@ -163,15 +158,22 @@
             other = lax.rem(own + step, group_size(stage))
             pl.semaphore_signal(barrier, 1, device_id=device(other), device_id_type=MESH)
 
+    chroma = chroma_ref[...]
+    weight = weight_ref[...]
+    diag = diag_ref[...]
+    pm = pm_ref[...]
     d = d_ref[...]
-    chroma = chroma_ref[...]
     channels, count, modes = d.shape
-    beam = beam_ref[...]
-    low = (chroma * d).astype(jnp.bfloat16).reshape(channels * count, modes)
-    seen = lax.dot_general(low, beam, (((1,), (1,)), ((), ())), preferred_element_type=jnp.float32)
-    heard = (weight_ref[...] * seen.reshape(channels, count, -1)).astype(jnp.bfloat16)
-    back = jnp.dot(heard.reshape(channels * count, -1), beam, preferred_element_type=jnp.float32)
-    cb = chroma * back.reshape(channels, count, modes)
+
+    def beam_part(vector):
+        beam = beam_ref[...]
+        low = (chroma * vector).astype(jnp.bfloat16).reshape(channels * count, modes)
+        seen = lax.dot_general(low, beam, (((1,), (1,)), ((), ())), preferred_element_type=jnp.float32)
+        heard = (weight * seen.reshape(channels, count, -1)).astype(jnp.bfloat16)
+        back = jnp.dot(heard.reshape(channels * count, -1), beam, preferred_element_type=jnp.float32)
+        return chroma * back.reshape(channels, count, modes)
+
+    cb = beam_part(d)
     pl.semaphore_wait(barrier, sum(group_size(stage) - 1 for stage in stages))
 
     def exchange_start(stage, src, recv, base, send_sems, recv_sems):
@@ -206,7 +208,7 @@
             total = total + recv[base + slot].astype(jnp.float32)
         return total
 
-    counter = {"row": 0, "slot": 0}
+    counter = {"row": 0, "slot": 0, "part": 0}
 
     def next_row(value):
         index = counter["row"]
@@ -224,73 +226,74 @@
             value = exchange_finish(row_stage(stage, next_row(value)))
         return value
 
-    diag = diag_ref[...]
-    pm = pm_ref[...]
-    count = d.shape[1]
-    for rank in range(pm.shape[1]):
-        part[rank] = jnp.sum(pm[:, rank] * d, axis=0).astype(part.dtype)
-    if first:
-        row = to_row([column_sum(d * (cb + diag * d)), column_sum(d * d)])
-    else:
-        row = to_row([column_sum(d * (cb + diag * d))])
-    p_state = exchange_start(stages[0], part, recv_p, 0, p_send, p_recv)
-    z_state = row_stage(stages[0], next_row(row))
-    projection = exchange_finish(p_state)
-    zrow = exchange_finish(z_state)
-    total = reduce_rest(zrow + to_row([column_sum(projection * projection)]))
+    def curve_sum(vector, image_part, extra):
+        index = counter["part"]
+        counter["part"] += 1
+        for rank in range(pm.shape[1]):
+            parts[index, rank] = jnp.sum(pm[:, rank] * vector, axis=0).astype(parts.dtype)
+        row = to_row([column_sum(vector * image_part)] + extra)
+        nz = group_size(stages[0])
+        p_state = exchange_start(stages[0], parts.at[index], recv_p, index * nz, p_send, p_recv)
+        z_state = row_stage(stages[0], next_row(row))
+        projection = exchange_finish(p_state)
+        zrow = exchange_finish(z_state)
+        total = reduce_rest(zrow + to_row([column_sum(projection * projection)]))
+        return projection, total
+
+    projection, total = curve_sum(d, cb + diag * d, [column_sum(d * d)])
     curve = from_row(total, 0, count)
-    if first:
-        norm_now = from_row(total, 1, count)
-        step_size = (norm_now / curve)[None]
-        est_ref[...] = step_size * d
-        spread = pm[:, 0] * projection[0][None]
-        for rank in range(1, pm.shape[1]):
-            spread = spread + pm[:, rank] * projection[rank][None]
-        image = cb + diag * d + spread
-        residual = d - step_size * image
-        row = to_row([column_sum(residual * residual)])
-        zrow = exchange_finish(row_stage(stages[0], next_row(row)))
-        total = reduce_rest(zrow)
-        norm_next = from_row(total, 0, count)
-        next_ref[...] = residual + (norm_next / norm_now)[None] * d
-        norm_ref[...] = total
-    else:
-        norm_now = from_row(norm_in_ref[...], 0, count)
-        est_ref[...] = est_in_ref[...] + (norm_now / curve)[None] * d
+    norm_now = from_row(total, 1, count)
+    step_size = (norm_now / curve)[None]
+    estimate = step_size * d
+    spread = pm[:, 0] * projection[0][None]
+    for rank in range(1, pm.shape[1]):
+        spread = spread + pm[:, rank] * projection[rank][None]
+    residual = d - step_size * (cb + diag * d + spread)
+    z_state = row_stage(stages[0], next_row(to_row([column_sum(residual * residual)])))
+    cb_residual = beam_part(residual)
+    total = reduce_rest(exchange_finish(z_state))
+    norm_next = from_row(total, 0, count)
+    ratio = (norm_next / norm_now)[None]
+    direction = residual + ratio * d
+    cb_direction = cb_residual + ratio * cb
+    projection, total = curve_sum(direction, cb_direction + diag * direction, [])
+    curve = from_row(total, 0, count)
+    est_ref[...] = estimate
+    next_ref[...] = direction
+    step_ref[...] = to_row([norm_next / curve])
     for own, size, _, _, copy_to in sent:
         for step in range(1, size):
             copy_to(lax.rem(own + step, size), own).wait_send()
 
 
-def cg_step(first, axis_names, stages, d, beam, chroma, weight, diag, pm, *extra):
-    reductions = 2 if first else 1
+def cg_solve(axis_names, stages, d, beam, chroma, weight, diag, pm):
+    reductions = 3
     slots = reductions * sum(group_size(stage) for stage in stages)
     rounds = reductions * len(stages)
     nz = group_size(stages[0])
     vector = jax.ShapeDtypeStruct(d.shape, jnp.float32)
     row = jax.ShapeDtypeStruct((1, 128), jnp.float32)
-    out_shape = (vector, vector, row) if first else vector
     vmem = pl.BlockSpec(memory_space=pltpu.VMEM)
     part_shape = (pm.shape[1],) + d.shape[1:]
-    return pl.pallas_call(
-        functools.partial(cg_kernel, first, axis_names, stages),
-        out_shape=out_shape,
-        in_specs=[vmem] * (6 + len(extra)),
-        out_specs=(vmem, vmem, vmem) if first else vmem,
+    estimate, direction, step_row = pl.pallas_call(
+        functools.partial(cg_kernel, axis_names, stages),
+        out_shape=(vector, vector, row),
+        in_specs=[vmem] * 6,
+        out_specs=(vmem, vmem, vmem),
         scratch_shapes=[
-            pltpu.VMEM(part_shape, jnp.bfloat16),
+            pltpu.VMEM((2,) + part_shape, jnp.bfloat16),
             pltpu.VMEM((rounds, 1, 128), jnp.float32),
-            pltpu.VMEM((nz,) + part_shape, jnp.bfloat16),
+            pltpu.VMEM((2 * nz,) + part_shape, jnp.bfloat16),
             pltpu.VMEM((slots, 1, 128), jnp.float32),
-            pltpu.SemaphoreType.DMA((nz,)),
-            pltpu.SemaphoreType.DMA((nz,)),
+            pltpu.SemaphoreType.DMA((2 * nz,)),
+            pltpu.SemaphoreType.DMA((2 * nz,)),
             pltpu.SemaphoreType.DMA((slots,)),
             pltpu.SemaphoreType.DMA((slots,)),
         ],
-        compiler_params=pltpu.CompilerParams(
-            collective_id=1 if first else 2, has_side_effects=True
-        ),
-    )(d, beam, chroma, weight, diag, pm, *extra)
+        compiler_params=pltpu.CompilerParams(collective_id=1, has_side_effects=True),
+    )(d, beam, chroma, weight, diag, pm)
+    step_size = step_row[0, : d.shape[1]]
+    return estimate + step_size[None, :, None] * direction
 
 
 def make_shards(mesh):
@@ -382,10 +385,7 @@
 
         direction = rhs[:, 0]
         operands = (beam_transfer[0], chromatic_gain[:, None, :], noise_weight, diag_rows, mode_rows4)
-        estimate, direction, norm_row = cg_step(True, axis_names, cg_stages, direction, *operands)
-        estimate = cg_step(
-            False, axis_names, cg_stages, direction, *operands, estimate, norm_row
-        )
+        estimate = cg_solve(axis_names, cg_stages, direction, *operands)
         estimate = estimate[:, None]
         return estimate
 

time: 114 us -> 108 us (0.947)
  Pallas kernels: 64.5 us -> 58.2 us
  other arithmetic: 0.15 us -> 1.82 us
    pallas_call x2 -> x1, Pallas kernels: 64.5 us -> 58.2 us  [cg_solve(): pl.pallas_call(functools.partial(cg_kernel, axis_names, stages), out_shap...]
    broadcast_in_dim x0 -> x1, other arithmetic: none -> 1.68 us  [shards(): estimate = estimate[:, None]]
    unnamed x9 -> x8, local copies, waits for them, and re-layouts: 1.57 us -> 0.02 us
where the time goes in v9:
time: 108 us
  Pallas kernels  58.2 us (54%)
  waiting for transfers between devices  20.4 us (19%)
  starting transfers between devices  17.7 us (16%)
  local copies, waits for them, and re-layouts  5.56 us (5%)
  matrix products  4.28 us (4%)
  other arithmetic  1.82 us (2%)
    pallas_call x1, Pallas kernels, cg_solve(): pl.pallas_call(functools.partial(cg_kernel, axis_names, stages), out_shap...  58.2 us
    all_to_all x1, waiting for transfers between devices, shards(): received = lax.all_to_all(send, 'ma', 0, 0, tiled=True)  12 us
    all_to_all x1, starting transfers between devices, shards(): received = lax.all_to_all(send, 'ma', 0, 0, tiled=True)  11.6 us
    all_to_all x1, waiting for transfers between devices, shards(): back_rows = lax.all_to_all(mode_rows, 'ma', 0, 0, tiled=True)  8.41 us
    all_to_all x1, starting transfers between devices, shards(): back_rows = lax.all_to_all(mode_rows, 'ma', 0, 0, tiled=True)  6.03 us
    dot_general x1, matrix products, shards(): jnp.einsum('fmkb,mbs->fmks', weighted, beam_transfer, preferred_element_t...  3.33 us
  transfers between devices with their start and end apart: 2, of which 2 were waited for; matrix products, arithmetic and copies ran while one was open for 2% of the time, Pallas kernels for 0%

profile of v9, /device:TPU:1, one launch (start us, length us, event | category | flops | bytes accessed | tf_op | source)
XLA Modules:
  0.0 108.0 jit_solution(2618012608022065888)
XLA Ops:
  0.0 0.0 copy-start.2
  0.0 0.0 copy-start.1
  0.0 0.0 copy-start.3
  0.0 0.0 copy-start
  0.0 1.2 %reshape.139 = bf16[4,2,8,8,2,128]{5,4,3,2,1,0:T(2,128)(2,1)S(1)} reshape(bf16[4,2,8,2048]{3,2,1,0:T(8,128)(2,1)} %param.6) | data formatting | bytes 524288 | tf_op jit(solution)/shard_map/reshape | solution.py:331
  1.2 0.9 copy.19
  2.1 11.6 %all-to-all-start = ((bf16[64,16,128]{2,1,0:T(8,128)(2,1)}), bf16[64,16,128]{2,1,0:T(8,128)(2,1)S(1)}, u32[]{:S(2)}, u32[]{:S(2)}) async-start(bf16[64,16,128]{2,1,0:T(8,128)(2,1)} %copy.19), calls=%async_computation | async-start | bytes 524288 | tf_op jit(solution)/shard_map/all_to_all | solution.py:335
  13.8 12.0 %all-to-all-done = bf16[64,16,128]{2,1,0:T(8,128)(2,1)S(1)} async-done(((bf16[64,16,128]{2,1,0:T(8,128)(2,1)}), bf16[64,16,128]{2,1,0:T(8,128)(2,1)S(1)}, u32[]{:S(2)}, u32[]{:S(2)}) %all-to-all-start) | async-done | bytes 262176 | tf_op jit(solution)/shard_map/all_to_all | solution.py:335
  25.7 0.2 reshape.141
  25.9 0.5 convolution_bitcast_fusion
  26.4 0.5 fusion.3
  26.9 0.8 copy.22
  27.6 6.0 %all-to-all-start.1 = ((bf16[64,4,256]{2,1,0:T(4,128)(2,1)}), bf16[64,4,256]{2,1,0:T(4,128)(2,1)S(1)}, u32[]{:S(2)}, u32[]{:S(2)}) async-start(bf16[64,4,256]{2,1,0:T(4,128)(2,1)} %copy.22), calls=%async_computation.1 | async-start | bytes 262144 | tf_op jit(solution)/shard_map/all_to_all | solution.py:348
  33.7 0.0 copy-done.2
  33.7 0.6 broadcast_in_dim.18.pm_ref
  34.3 0.0 copy-done.1
  34.3 0.6 broadcast_in_dim.16.chroma_ref
  34.9 0.0 copy-done.3
  34.9 0.6 broadcast_in_dim.17.diag_ref
  35.5 0.0 copy-done
  35.5 0.1 reduce
  35.6 8.4 %all-to-all-done.1 = bf16[64,4,256]{2,1,0:T(4,128)(2,1)S(1)} async-done(((bf16[64,4,256]{2,1,0:T(4,128)(2,1)}), bf16[64,4,256]{2,1,0:T(4,128)(2,1)S(1)}, u32[]{:S(2)}, u32[]{:S(2)}) %all-to-all-start.1) | async-done | bytes 131104 | tf_op jit(solution)/shard_map/all_to_all | solution.py:348
  44.0 0.1 fusion.14
  44.1 0.1 copy.23
  44.2 3.3 %fusion.10.d_ref = f32[4,8,896]{2,1,0:T(8,128)} fusion(bf16[4,8,2048]{2,1,0:T(8,128)(2,1)S(1)} %bitcast.64, bf16[1,2048,896]{2,1,0:T(8,128)(2,1)} %param.7, f32[4,896]{1,0:T(4,128)S(1)} %copy-done.1), kind=kOutput, calls=%fused_computation.8 | convolution fusion | flops 117469184 | bytes 3930112 | tf_op jit(solution)/shard_map/fmkb,mbs->fmks/dot_general | solution.py:361
  47.5 58.2 %shard_map.64 = (f32[4,8,896]{2,1,0:T(8,128)}, f32[4,8,896]{2,1,0:T(8,128)}, f32[1,128]{1,0:T(1,128)}) custom-call(f32[4,8,896]{2,1,0:T(8,128)} %fusion.10.d_ref, bf16[2048,896]{1,0:T(8,128)(2,1)} %bitcast.61, f32[4,1,896]{2,1,0:T(1,128)} %broadcast_in_dim.16.chroma_ref, f32[4,1,2048]{2,1,0:T(1,128)} %weight_ref.1, f32[4,1,896]{2,1,0:T(1,128)} %broadcast_in_dim.17.diag_ref, ...), custom_call_target="tpu_custom_call" | custom-call | tf_op jit(solution)/shard_map/pallas_call | solution.py:278
  105.7 0.6 slice_bitcast_fusion
  106.4 1.7 %add_bitcast_fusion = f32[4,1,8,896]{3,2,1,0:T(8,128)} fusion(f32[4,8,896]{2,1,0:T(8,128)} %get-tuple-element.8, f32[4,8,896]{2,1,0:T(8,128)} %get-tuple-element.10, f32[8]{0:T(128)S(1)} %slice_bitcast_fusion), kind=kLoop, calls=%fused_computation.14 | loop fusion | flops 57344 | bytes 344096 | tf_op jit(solution)/shard_map/broadcast_in_dim | solution.py:389
  (2 shorter events, 0.1 us)
Async XLA Ops:
  0.0 33.7 %copy-start.2 = (f32[4,2,896]{2,1,0:T(2,128)S(1)}, f32[4,2,896]{2,1,0:T(2,128)}, u32[]{:S(2)}) copy-start(f32[4,2,896]{2,1,0:T(2,128)} %param.11) | copy-start | bytes 86020
  0.0 34.3 %copy-start.1 = (f32[4,896]{1,0:T(4,128)S(1)}, f32[4,896]{1,0:T(4,128)}, u32[]{:S(2)}) copy-start(f32[4,896]{1,0:T(4,128)} %param.8) | copy-start | bytes 43012
  0.0 34.9 %copy-start.3 = (f32[4,896]{1,0:T(4,128)S(1)}, f32[4,896]{1,0:T(4,128)}, u32[]{:S(2)}) copy-start(f32[4,896]{1,0:T(4,128)} %param.10) | copy-start | bytes 43012
  0.0 35.5 %copy-start = (f32[4,1,2048]{2,1,0:T(1,128)S(1)}, f32[4,1,2048]{2,1,0:T(1,128)}, u32[]{:S(2)}) copy-start(f32[4,1,2048]{2,1,0:T(1,128)} %weight_ref.1) | copy-start | bytes 98308
  2.1 23.6 %all-to-all-start = ((bf16[64,16,128]{2,1,0:T(8,128)(2,1)}), bf16[64,16,128]{2,1,0:T(8,128)(2,1)S(1)}, u32[]{:S(2)}, u32[]{:S(2)}) async-start(bf16[64,16,128]{2,1,0:T(8,128)(2,1)} %copy.19), calls=%async_computation | async-start | bytes 524288 | tf_op jit(solution)/shard_map/all_to_all | solution.py:335
  27.6 16.4 %all-to-all-start.1 = ((bf16[64,4,256]{2,1,0:T(4,128)(2,1)}), bf16[64,4,256]{2,1,0:T(4,128)(2,1)S(1)}, u32[]{:S(2)}, u32[]{:S(2)}) async-start(bf16[64,4,256]{2,1,0:T(4,128)(2,1)} %copy.22), calls=%async_computation.1 | async-start | bytes 262144 | tf_op jit(solution)/shard_map/all_to_all | solution.py:348

commit v10 on v9

--- a/solution.py
+++ b/solution.py
@@ -165,15 +165,18 @@
     d = d_ref[...]
     channels, count, modes = d.shape
 
-    def beam_part(vector):
-        beam = beam_ref[...]
+    def beam_forward(vector):
         low = (chroma * vector).astype(jnp.bfloat16).reshape(channels * count, modes)
-        seen = lax.dot_general(low, beam, (((1,), (1,)), ((), ())), preferred_element_type=jnp.float32)
-        heard = (weight * seen.reshape(channels, count, -1)).astype(jnp.bfloat16)
-        back = jnp.dot(heard.reshape(channels * count, -1), beam, preferred_element_type=jnp.float32)
+        seen = lax.dot_general(
+            low, beam_ref[...], (((1,), (1,)), ((), ())), preferred_element_type=jnp.float32
+        )
+        return (weight * seen.reshape(channels, count, -1)).astype(jnp.bfloat16)
+
+    def beam_backward(heard):
+        back = jnp.dot(heard.reshape(channels * count, -1), beam_ref[...], preferred_element_type=jnp.float32)
         return chroma * back.reshape(channels, count, modes)
 
-    cb = beam_part(d)
+    heard = beam_forward(d)
     pl.semaphore_wait(barrier, sum(group_size(stage) - 1 for stage in stages))
 
     def exchange_start(stage, src, recv, base, send_sems, recv_sems):
@@ -226,21 +229,20 @@
             value = exchange_finish(row_stage(stage, next_row(value)))
         return value
 
-    def curve_sum(vector, image_part, extra):
+    def projection_start(vector):
         index = counter["part"]
         counter["part"] += 1
         for rank in range(pm.shape[1]):
             parts[index, rank] = jnp.sum(pm[:, rank] * vector, axis=0).astype(parts.dtype)
-        row = to_row([column_sum(vector * image_part)] + extra)
         nz = group_size(stages[0])
-        p_state = exchange_start(stages[0], parts.at[index], recv_p, index * nz, p_send, p_recv)
-        z_state = row_stage(stages[0], next_row(row))
-        projection = exchange_finish(p_state)
-        zrow = exchange_finish(z_state)
-        total = reduce_rest(zrow + to_row([column_sum(projection * projection)]))
-        return projection, total
-
-    projection, total = curve_sum(d, cb + diag * d, [column_sum(d * d)])
+        return exchange_start(stages[0], parts.at[index], recv_p, index * nz, p_send, p_recv)
+
+    p_state = projection_start(d)
+    cb = beam_backward(heard)
+    z_state = row_stage(stages[0], next_row(to_row([column_sum(d * (cb + diag * d)), column_sum(d * d)])))
+    projection = exchange_finish(p_state)
+    zrow = exchange_finish(z_state)
+    total = reduce_rest(zrow + to_row([column_sum(projection * projection)]))
     curve = from_row(total, 0, count)
     norm_now = from_row(total, 1, count)
     step_size = (norm_now / curve)[None]
@@ -250,13 +252,19 @@
         spread = spread + pm[:, rank] * projection[rank][None]
     residual = d - step_size * (cb + diag * d + spread)
     z_state = row_stage(stages[0], next_row(to_row([column_sum(residual * residual)])))
-    cb_residual = beam_part(residual)
+    p_state = projection_start(residual)
+    cb_residual = beam_backward(beam_forward(residual))
     total = reduce_rest(exchange_finish(z_state))
+    projection_residual = exchange_finish(p_state)
     norm_next = from_row(total, 0, count)
     ratio = (norm_next / norm_now)[None]
     direction = residual + ratio * d
     cb_direction = cb_residual + ratio * cb
-    projection, total = curve_sum(direction, cb_direction + diag * direction, [])
+    projection = projection_residual + ratio * projection
+    zrow = exchange_finish(
+        row_stage(stages[0], next_row(to_row([column_sum(direction * (cb_direction + diag * direction))])))
+    )
+    total = reduce_rest(zrow + to_row([column_sum(projection * projection)]))
     curve = from_row(total, 0, count)
     est_ref[...] = estimate
     next_ref[...] = direction

time: 108 us -> 105 us (0.972)
  Pallas kernels: 58.2 us -> 55.3 us
    pallas_call x1, Pallas kernels: 58.2 us -> 55.3 us  [cg_solve(): pl.pallas_call(functools.partial(cg_kernel, axis_names, stages), out_shap...]
where the time goes in v10:
time: 105 us
  Pallas kernels  55.3 us (53%)
  waiting for transfers between devices  20.4 us (19%)
  starting transfers between devices  17.7 us (17%)
  local copies, waits for them, and re-layouts  5.56 us (5%)
  matrix products  4.28 us (4%)
  other arithmetic  1.82 us (2%)
    pallas_call x1, Pallas kernels, cg_solve(): pl.pallas_call(functools.partial(cg_kernel, axis_names, stages), out_shap...  55.3 us
    all_to_all x1, waiting for transfers between devices, shards(): received = lax.all_to_all(send, 'ma', 0, 0, tiled=True)  12 us
    all_to_all x1, starting transfers between devices, shards(): received = lax.all_to_all(send, 'ma', 0, 0, tiled=True)  11.6 us
    all_to_all x1, waiting for transfers between devices, shards(): back_rows = lax.all_to_all(mode_rows, 'ma', 0, 0, tiled=True)  8.41 us
    all_to_all x1, starting transfers between devices, shards(): back_rows = lax.all_to_all(mode_rows, 'ma', 0, 0, tiled=True)  6.03 us
    dot_general x1, matrix products, shards(): jnp.einsum('fmkb,mbs->fmks', weighted, beam_transfer, preferred_element_t...  3.33 us
  transfers between devices with their start and end apart: 2, of which 2 were waited for; matrix products, arithmetic and copies ran while one was open for 2% of the time, Pallas kernels for 0%

profile of v10, /device:TPU:1, one launch (start us, length us, event | category | flops | bytes accessed | tf_op | source)
XLA Modules:
  0.0 105.1 jit_solution(5614665738481248376)
XLA Ops:
  0.0 0.0 copy-start.2
  0.0 0.0 copy-start.1
  0.0 0.0 copy-start.3
  0.0 0.0 copy-start
  0.0 1.2 %reshape.139 = bf16[4,2,8,8,2,128]{5,4,3,2,1,0:T(2,128)(2,1)S(1)} reshape(bf16[4,2,8,2048]{3,2,1,0:T(8,128)(2,1)} %param.6) | data formatting | bytes 524288 | tf_op jit(solution)/shard_map/reshape | solution.py:339
  1.2 0.9 copy.19
  2.1 11.6 %all-to-all-start = ((bf16[64,16,128]{2,1,0:T(8,128)(2,1)}), bf16[64,16,128]{2,1,0:T(8,128)(2,1)S(1)}, u32[]{:S(2)}, u32[]{:S(2)}) async-start(bf16[64,16,128]{2,1,0:T(8,128)(2,1)} %copy.19), calls=%async_computation | async-start | bytes 524288 | tf_op jit(solution)/shard_map/all_to_all | solution.py:343
  13.8 12.0 %all-to-all-done = bf16[64,16,128]{2,1,0:T(8,128)(2,1)S(1)} async-done(((bf16[64,16,128]{2,1,0:T(8,128)(2,1)}), bf16[64,16,128]{2,1,0:T(8,128)(2,1)S(1)}, u32[]{:S(2)}, u32[]{:S(2)}) %all-to-all-start) | async-done | bytes 262176 | tf_op jit(solution)/shard_map/all_to_all | solution.py:343
  25.7 0.2 reshape.141
  25.9 0.5 convolution_bitcast_fusion
  26.4 0.5 fusion.3
  26.9 0.8 copy.22
  27.6 6.0 %all-to-all-start.1 = ((bf16[64,4,256]{2,1,0:T(4,128)(2,1)}), bf16[64,4,256]{2,1,0:T(4,128)(2,1)S(1)}, u32[]{:S(2)}, u32[]{:S(2)}) async-start(bf16[64,4,256]{2,1,0:T(4,128)(2,1)} %copy.22), calls=%async_computation.1 | async-start | bytes 262144 | tf_op jit(solution)/shard_map/all_to_all | solution.py:356
  33.7 0.0 copy-done.2
  33.7 0.6 broadcast_in_dim.18.pm_ref
  34.3 0.0 copy-done.1
  34.3 0.6 broadcast_in_dim.16.chroma_ref
  34.9 0.0 copy-done.3
  34.9 0.6 broadcast_in_dim.17.diag_ref
  35.5 0.0 copy-done
  35.5 0.1 reduce
  35.6 8.4 %all-to-all-done.1 = bf16[64,4,256]{2,1,0:T(4,128)(2,1)S(1)} async-done(((bf16[64,4,256]{2,1,0:T(4,128)(2,1)}), bf16[64,4,256]{2,1,0:T(4,128)(2,1)S(1)}, u32[]{:S(2)}, u32[]{:S(2)}) %all-to-all-start.1) | async-done | bytes 131104 | tf_op jit(solution)/shard_map/all_to_all | solution.py:356
  44.0 0.1 fusion.14
  44.1 0.1 copy.23
  44.2 3.3 %fusion.10.d_ref = f32[4,8,896]{2,1,0:T(8,128)} fusion(bf16[4,8,2048]{2,1,0:T(8,128)(2,1)S(1)} %bitcast.64, bf16[1,2048,896]{2,1,0:T(8,128)(2,1)} %param.7, f32[4,896]{1,0:T(4,128)S(1)} %copy-done.1), kind=kOutput, calls=%fused_computation.8 | convolution fusion | flops 117469184 | bytes 3930112 | tf_op jit(solution)/shard_map/fmkb,mbs->fmks/dot_general | solution.py:369
  47.5 55.3 %shard_map.64 = (f32[4,8,896]{2,1,0:T(8,128)}, f32[4,8,896]{2,1,0:T(8,128)}, f32[1,128]{1,0:T(1,128)}) custom-call(f32[4,8,896]{2,1,0:T(8,128)} %fusion.10.d_ref, bf16[2048,896]{1,0:T(8,128)(2,1)} %bitcast.61, f32[4,1,896]{2,1,0:T(1,128)} %broadcast_in_dim.16.chroma_ref, f32[4,1,2048]{2,1,0:T(1,128)} %weight_ref.1, f32[4,1,896]{2,1,0:T(1,128)} %broadcast_in_dim.17.diag_ref, ...), custom_call_target="tpu_custom_call" | custom-call | tf_op jit(solution)/shard_map/pallas_call | solution.py:286
  102.9 0.6 slice_bitcast_fusion
  103.5 1.7 %add_bitcast_fusion = f32[4,1,8,896]{3,2,1,0:T(8,128)} fusion(f32[4,8,896]{2,1,0:T(8,128)} %get-tuple-element.8, f32[4,8,896]{2,1,0:T(8,128)} %get-tuple-element.10, f32[8]{0:T(128)S(1)} %slice_bitcast_fusion), kind=kLoop, calls=%fused_computation.14 | loop fusion | flops 57344 | bytes 344096 | tf_op jit(solution)/shard_map/broadcast_in_dim | solution.py:397
  (2 shorter events, 0.1 us)
Async XLA Ops:
  0.0 33.7 %copy-start.2 = (f32[4,2,896]{2,1,0:T(2,128)S(1)}, f32[4,2,896]{2,1,0:T(2,128)}, u32[]{:S(2)}) copy-start(f32[4,2,896]{2,1,0:T(2,128)} %param.11) | copy-start | bytes 86020
  0.0 34.3 %copy-start.1 = (f32[4,896]{1,0:T(4,128)S(1)}, f32[4,896]{1,0:T(4,128)}, u32[]{:S(2)}) copy-start(f32[4,896]{1,0:T(4,128)} %param.8) | copy-start | bytes 43012
  0.0 34.9 %copy-start.3 = (f32[4,896]{1,0:T(4,128)S(1)}, f32[4,896]{1,0:T(4,128)}, u32[]{:S(2)}) copy-start(f32[4,896]{1,0:T(4,128)} %param.10) | copy-start | bytes 43012
  0.0 35.5 %copy-start = (f32[4,1,2048]{2,1,0:T(1,128)S(1)}, f32[4,1,2048]{2,1,0:T(1,128)}, u32[]{:S(2)}) copy-start(f32[4,1,2048]{2,1,0:T(1,128)} %weight_ref.1) | copy-start | bytes 98308
  2.1 23.6 %all-to-all-start = ((bf16[64,16,128]{2,1,0:T(8,128)(2,1)}), bf16[64,16,128]{2,1,0:T(8,128)(2,1)S(1)}, u32[]{:S(2)}, u32[]{:S(2)}) async-start(bf16[64,16,128]{2,1,0:T(8,128)(2,1)} %copy.19), calls=%async_computation | async-start | bytes 524288 | tf_op jit(solution)/shard_map/all_to_all | solution.py:343
  27.6 16.4 %all-to-all-start.1 = ((bf16[64,4,256]{2,1,0:T(4,128)(2,1)}), bf16[64,4,256]{2,1,0:T(4,128)(2,1)S(1)}, u32[]{:S(2)}, u32[]{:S(2)}) async-start(bf16[64,4,256]{2,1,0:T(4,128)(2,1)} %copy.22), calls=%async_computation.1 | async-start | bytes 262144 | tf_op jit(solution)/shard_map/all_to_all | solution.py:356

commit v11 on v10

--- a/solution.py
+++ b/solution.py
@@ -162,8 +162,8 @@
     weight = weight_ref[...]
     diag = diag_ref[...]
     pm = pm_ref[...]
-    d = d_ref[...]
-    channels, count, modes = d.shape
+    channels, count = d_ref.shape[:2]
+    modes = beam_ref.shape[1]
 
     def beam_forward(vector):
         low = (chroma * vector).astype(jnp.bfloat16).reshape(channels * count, modes)
@@ -176,6 +176,7 @@
         back = jnp.dot(heard.reshape(channels * count, -1), beam_ref[...], preferred_element_type=jnp.float32)
         return chroma * back.reshape(channels, count, modes)
 
+    d = beam_backward(d_ref[...])
     heard = beam_forward(d)
     pl.semaphore_wait(barrier, sum(group_size(stage) - 1 for stage in stages))
 
@@ -279,10 +280,10 @@
     slots = reductions * sum(group_size(stage) for stage in stages)
     rounds = reductions * len(stages)
     nz = group_size(stages[0])
-    vector = jax.ShapeDtypeStruct(d.shape, jnp.float32)
+    vector = jax.ShapeDtypeStruct(d.shape[:2] + beam.shape[1:], jnp.float32)
     row = jax.ShapeDtypeStruct((1, 128), jnp.float32)
     vmem = pl.BlockSpec(memory_space=pltpu.VMEM)
-    part_shape = (pm.shape[1],) + d.shape[1:]
+    part_shape = (pm.shape[1],) + vector.shape[1:]
     estimate, direction, step_row = pl.pallas_call(
         functools.partial(cg_kernel, axis_names, stages),
         out_shape=(vector, vector, row),
@@ -366,9 +367,6 @@
         weighted = (noise_weight[:, :, None, :] * measured_visibility.astype(jnp.float32)).astype(
             jnp.bfloat16
         )
-        rhs = chroma * jnp.einsum(
-            "fmkb,mbs->fmks", weighted, beam_transfer, preferred_element_type=jnp.float32
-        )
 
         assert resident_modes == 1
         if mode_devices % 16 == 0:
@@ -391,7 +389,7 @@
             )
             return (chroma * back)[:, 0]
 
-        direction = rhs[:, 0]
+        direction = weighted[:, 0]
         operands = (beam_transfer[0], chromatic_gain[:, None, :], noise_weight, diag_rows, mode_rows4)
         estimate = cg_solve(axis_names, cg_stages, direction, *operands)
         estimate = estimate[:, None]

time: 105 us -> 103 us (0.981)
  matrix products: 4.28 us -> 0.95 us
    dot_general x1 -> x0, matrix products: 3.33 us -> none  [shards(): jnp.einsum('fmkb,mbs->fmks', weighted, beam_transfer, preferred_element_t...]
where the time goes in v11:
time: 103 us; the launch traced here: 102 us
  Pallas kernels  55.4 us (54%)
  waiting for transfers between devices  20.5 us (20%)
  starting transfers between devices  17.7 us (17%)
  local copies, waits for them, and re-layouts  5.56 us (5%)
  other arithmetic  2.37 us (2%)
    pallas_call x1, Pallas kernels, cg_solve(): pl.pallas_call(functools.partial(cg_kernel, axis_names, stages), out_shap...  55.4 us
    all_to_all x1, waiting for transfers between devices, shards(): received = lax.all_to_all(send, 'ma', 0, 0, tiled=True)  12 us
    all_to_all x1, starting transfers between devices, shards(): received = lax.all_to_all(send, 'ma', 0, 0, tiled=True)  11.6 us
    all_to_all x1, waiting for transfers between devices, shards(): back_rows = lax.all_to_all(mode_rows, 'ma', 0, 0, tiled=True)  8.47 us
    all_to_all x1, starting transfers between devices, shards(): back_rows = lax.all_to_all(mode_rows, 'ma', 0, 0, tiled=True)  6.03 us
  transfers between devices with their start and end apart: 2, of which 2 were waited for; matrix products, arithmetic and copies ran while one was open for 2% of the time, Pallas kernels for 0%

profile of v11, /device:TPU:1, one launch (start us, length us, event | category | flops | bytes accessed | tf_op | source)
XLA Modules:
  0.0 102.4 jit_solution(8659019997126509177)
XLA Ops:
  0.0 0.0 copy-start
  0.0 0.0 copy-start.1
  0.0 0.0 copy-start.2
  0.0 0.0 copy-start.3
  0.0 1.2 %reshape.130 = bf16[4,2,8,8,2,128]{5,4,3,2,1,0:T(2,128)(2,1)S(1)} reshape(bf16[4,2,8,2048]{3,2,1,0:T(8,128)(2,1)} %param.6) | data formatting | bytes 524288 | tf_op jit(solution)/shard_map/reshape | solution.py:340
  1.2 0.9 copy.21
  2.1 11.6 %all-to-all-start = ((bf16[64,16,128]{2,1,0:T(8,128)(2,1)}), bf16[64,16,128]{2,1,0:T(8,128)(2,1)S(1)}, u32[]{:S(2)}, u32[]{:S(2)}) async-start(bf16[64,16,128]{2,1,0:T(8,128)(2,1)} %copy.21), calls=%async_computation | async-start | bytes 524288 | tf_op jit(solution)/shard_map/all_to_all | solution.py:344
  13.7 12.0 %all-to-all-done = bf16[64,16,128]{2,1,0:T(8,128)(2,1)S(1)} async-done(((bf16[64,16,128]{2,1,0:T(8,128)(2,1)}), bf16[64,16,128]{2,1,0:T(8,128)(2,1)S(1)}, u32[]{:S(2)}, u32[]{:S(2)}) %all-to-all-start) | async-done | bytes 262176 | tf_op jit(solution)/shard_map/all_to_all | solution.py:344
  25.7 0.2 reshape.132
  25.9 0.5 convolution_bitcast_fusion
  26.4 0.5 fusion.1
  26.9 0.8 copy.24
  27.6 6.0 %all-to-all-start.1 = ((bf16[64,4,256]{2,1,0:T(4,128)(2,1)}), bf16[64,4,256]{2,1,0:T(4,128)(2,1)S(1)}, u32[]{:S(2)}, u32[]{:S(2)}) async-start(bf16[64,4,256]{2,1,0:T(4,128)(2,1)} %copy.24), calls=%async_computation.1 | async-start | bytes 262144 | tf_op jit(solution)/shard_map/all_to_all | solution.py:357
  33.7 0.0 copy-done
  33.7 0.0 copy-done.1
  33.7 0.6 broadcast_in_dim.17.pm_ref
  34.3 0.0 copy-done.2
  34.3 0.6 broadcast_in_dim.15.chroma_ref
  34.9 0.0 copy-done.3
  34.9 0.6 broadcast_in_dim.16.diag_ref
  35.5 8.5 %all-to-all-done.1 = bf16[64,4,256]{2,1,0:T(4,128)(2,1)S(1)} async-done(((bf16[64,4,256]{2,1,0:T(4,128)(2,1)}), bf16[64,4,256]{2,1,0:T(4,128)(2,1)S(1)}, u32[]{:S(2)}, u32[]{:S(2)}) %all-to-all-start.1) | async-done | bytes 131104 | tf_op jit(solution)/shard_map/all_to_all | solution.py:357
  44.0 0.1 copy.25
  44.1 0.7 multiply_convert_fusion.d_ref
  44.8 55.4 %shard_map.64 = (f32[4,8,896]{2,1,0:T(8,128)}, f32[4,8,896]{2,1,0:T(8,128)}, f32[1,128]{1,0:T(1,128)}) custom-call(bf16[4,8,2048]{2,1,0:T(8,128)(2,1)} %multiply_convert_fusion.d_ref, bf16[2048,896]{1,0:T(8,128)(2,1)} %bitcast.37, f32[4,1,896]{2,1,0:T(1,128)} %broadcast_in_dim.15.chroma_ref, f32[4,1,2048]{2,1,0:T(1,128)} %weight_ref.1, ...), custom_call_target="tpu_custom_call" | custom-call | tf_op jit(solution)/shard_map/pallas_call | solution.py:287
  100.2 0.6 slice_bitcast_fusion
  100.8 1.7 %add_bitcast_fusion = f32[4,1,8,896]{3,2,1,0:T(8,128)} fusion(f32[4,8,896]{2,1,0:T(8,128)} %get-tuple-element.8, f32[4,8,896]{2,1,0:T(8,128)} %get-tuple-element.10, f32[8]{0:T(128)S(1)} %slice_bitcast_fusion), kind=kLoop, calls=%fused_computation.7 | loop fusion | flops 57344 | bytes 344096 | tf_op jit(solution)/shard_map/broadcast_in_dim | solution.py:395
  (3 shorter events, 0.1 us)
Async XLA Ops:
  0.0 33.7 %copy-start = (f32[4,1,2048]{2,1,0:T(1,128)S(1)}, f32[4,1,2048]{2,1,0:T(1,128)}, u32[]{:S(2)}) copy-start(f32[4,1,2048]{2,1,0:T(1,128)} %weight_ref.1) | copy-start | bytes 98308
  0.0 33.7 %copy-start.1 = (f32[4,2,896]{2,1,0:T(2,128)S(1)}, f32[4,2,896]{2,1,0:T(2,128)}, u32[]{:S(2)}) copy-start(f32[4,2,896]{2,1,0:T(2,128)} %param.11) | copy-start | bytes 86020
  0.0 34.3 %copy-start.2 = (f32[4,896]{1,0:T(4,128)S(1)}, f32[4,896]{1,0:T(4,128)}, u32[]{:S(2)}) copy-start(f32[4,896]{1,0:T(4,128)} %param.8) | copy-start | bytes 43012
  0.0 34.9 %copy-start.3 = (f32[4,896]{1,0:T(4,128)S(1)}, f32[4,896]{1,0:T(4,128)}, u32[]{:S(2)}) copy-start(f32[4,896]{1,0:T(4,128)} %param.10) | copy-start | bytes 43012
  2.1 23.6 %all-to-all-start = ((bf16[64,16,128]{2,1,0:T(8,128)(2,1)}), bf16[64,16,128]{2,1,0:T(8,128)(2,1)S(1)}, u32[]{:S(2)}, u32[]{:S(2)}) async-start(bf16[64,16,128]{2,1,0:T(8,128)(2,1)} %copy.21), calls=%async_computation | async-start | bytes 524288 | tf_op jit(solution)/shard_map/all_to_all | solution.py:344
  27.6 16.4 %all-to-all-start.1 = ((bf16[64,4,256]{2,1,0:T(4,128)(2,1)}), bf16[64,4,256]{2,1,0:T(4,128)(2,1)S(1)}, u32[]{:S(2)}, u32[]{:S(2)}) async-start(bf16[64,4,256]{2,1,0:T(4,128)(2,1)} %copy.24), calls=%async_computation.1 | async-start | bytes 262144 | tf_op jit(solution)/shard_map/all_to_all | solution.py:357

commit v12 on v11

--- a/solution.py
+++ b/solution.py
@@ -176,9 +176,6 @@
         back = jnp.dot(heard.reshape(channels * count, -1), beam_ref[...], preferred_element_type=jnp.float32)
         return chroma * back.reshape(channels, count, modes)
 
-    d = beam_backward(d_ref[...])
-    heard = beam_forward(d)
-    pl.semaphore_wait(barrier, sum(group_size(stage) - 1 for stage in stages))
 
     def exchange_start(stage, src, recv, base, send_sems, recv_sems):
         own, device = place(stage)
@@ -238,8 +235,10 @@
         nz = group_size(stages[0])
         return exchange_start(stages[0], parts.at[index], recv_p, index * nz, p_send, p_recv)
 
+    d = beam_backward(d_ref[...])
+    pl.semaphore_wait(barrier, sum(group_size(stage) - 1 for stage in stages))
     p_state = projection_start(d)
-    cb = beam_backward(heard)
+    cb = beam_backward(beam_forward(d))
     z_state = row_stage(stages[0], next_row(to_row([column_sum(d * (cb + diag * d)), column_sum(d * d)])))
     projection = exchange_finish(p_state)
     zrow = exchange_finish(z_state)

time: 103 us -> 103 us (level)
  no operation moved by 1% of the time
where the time goes in v12:
time: 103 us; the launch traced here: 102 us
  Pallas kernels  55.4 us (54%)
  waiting for transfers between devices  20.5 us (20%)
  starting transfers between devices  17.7 us (17%)
  local copies, waits for them, and re-layouts  5.56 us (5%)
  other arithmetic  2.37 us (2%)
    pallas_call x1, Pallas kernels, cg_solve(): pl.pallas_call(functools.partial(cg_kernel, axis_names, stages), out_shap...  55.4 us
    all_to_all x1, waiting for transfers between devices, shards(): received = lax.all_to_all(send, 'ma', 0, 0, tiled=True)  12 us
    all_to_all x1, starting transfers between devices, shards(): received = lax.all_to_all(send, 'ma', 0, 0, tiled=True)  11.6 us
    all_to_all x1, waiting for transfers between devices, shards(): back_rows = lax.all_to_all(mode_rows, 'ma', 0, 0, tiled=True)  8.47 us
    all_to_all x1, starting transfers between devices, shards(): back_rows = lax.all_to_all(mode_rows, 'ma', 0, 0, tiled=True)  6.03 us
  transfers between devices with their start and end apart: 2, of which 2 were waited for; matrix products, arithmetic and copies ran while one was open for 2% of the time, Pallas kernels for 0%

profile of v12, /device:TPU:1, one launch (start us, length us, event | category | flops | bytes accessed | tf_op | source)
XLA Modules:
  0.0 102.4 jit_solution(14805018105813134769)
XLA Ops:
  0.0 0.0 copy-start
  0.0 0.0 copy-start.1
  0.0 0.0 copy-start.2
  0.0 0.0 copy-start.3
  0.0 1.2 %reshape.130 = bf16[4,2,8,8,2,128]{5,4,3,2,1,0:T(2,128)(2,1)S(1)} reshape(bf16[4,2,8,2048]{3,2,1,0:T(8,128)(2,1)} %param.6) | data formatting | bytes 524288 | tf_op jit(solution)/shard_map/reshape | solution.py:339
  1.2 0.9 copy.21
  2.1 11.6 %all-to-all-start = ((bf16[64,16,128]{2,1,0:T(8,128)(2,1)}), bf16[64,16,128]{2,1,0:T(8,128)(2,1)S(1)}, u32[]{:S(2)}, u32[]{:S(2)}) async-start(bf16[64,16,128]{2,1,0:T(8,128)(2,1)} %copy.21), calls=%async_computation | async-start | bytes 524288 | tf_op jit(solution)/shard_map/all_to_all | solution.py:343
  13.7 12.0 %all-to-all-done = bf16[64,16,128]{2,1,0:T(8,128)(2,1)S(1)} async-done(((bf16[64,16,128]{2,1,0:T(8,128)(2,1)}), bf16[64,16,128]{2,1,0:T(8,128)(2,1)S(1)}, u32[]{:S(2)}, u32[]{:S(2)}) %all-to-all-start) | async-done | bytes 262176 | tf_op jit(solution)/shard_map/all_to_all | solution.py:343
  25.7 0.2 reshape.132
  25.9 0.5 convolution_bitcast_fusion
  26.4 0.5 fusion.1
  26.9 0.8 copy.24
  27.6 6.0 %all-to-all-start.1 = ((bf16[64,4,256]{2,1,0:T(4,128)(2,1)}), bf16[64,4,256]{2,1,0:T(4,128)(2,1)S(1)}, u32[]{:S(2)}, u32[]{:S(2)}) async-start(bf16[64,4,256]{2,1,0:T(4,128)(2,1)} %copy.24), calls=%async_computation.1 | async-start | bytes 262144 | tf_op jit(solution)/shard_map/all_to_all | solution.py:356
  33.7 0.0 copy-done
  33.7 0.0 copy-done.1
  33.7 0.6 broadcast_in_dim.17.pm_ref
  34.3 0.0 copy-done.2
  34.3 0.6 broadcast_in_dim.15.chroma_ref
  34.9 0.0 copy-done.3
  34.9 0.6 broadcast_in_dim.16.diag_ref
  35.5 8.5 %all-to-all-done.1 = bf16[64,4,256]{2,1,0:T(4,128)(2,1)S(1)} async-done(((bf16[64,4,256]{2,1,0:T(4,128)(2,1)}), bf16[64,4,256]{2,1,0:T(4,128)(2,1)S(1)}, u32[]{:S(2)}, u32[]{:S(2)}) %all-to-all-start.1) | async-done | bytes 131104 | tf_op jit(solution)/shard_map/all_to_all | solution.py:356
  44.0 0.1 copy.25
  44.1 0.7 multiply_convert_fusion.d_ref
  44.8 55.4 %shard_map.64 = (f32[4,8,896]{2,1,0:T(8,128)}, f32[4,8,896]{2,1,0:T(8,128)}, f32[1,128]{1,0:T(1,128)}) custom-call(bf16[4,8,2048]{2,1,0:T(8,128)(2,1)} %multiply_convert_fusion.d_ref, bf16[2048,896]{1,0:T(8,128)(2,1)} %bitcast.37, f32[4,1,896]{2,1,0:T(1,128)} %broadcast_in_dim.15.chroma_ref, f32[4,1,2048]{2,1,0:T(1,128)} %weight_ref.1, ...), custom_call_target="tpu_custom_call" | custom-call | tf_op jit(solution)/shard_map/pallas_call | solution.py:286
  100.2 0.6 slice_bitcast_fusion
  100.8 1.7 %add_bitcast_fusion = f32[4,1,8,896]{3,2,1,0:T(8,128)} fusion(f32[4,8,896]{2,1,0:T(8,128)} %get-tuple-element.8, f32[4,8,896]{2,1,0:T(8,128)} %get-tuple-element.10, f32[8]{0:T(128)S(1)} %slice_bitcast_fusion), kind=kLoop, calls=%fused_computation.7 | loop fusion | flops 57344 | bytes 344096 | tf_op jit(solution)/shard_map/broadcast_in_dim | solution.py:394
  (3 shorter events, 0.1 us)
Async XLA Ops:
  0.0 33.7 %copy-start = (f32[4,1,2048]{2,1,0:T(1,128)S(1)}, f32[4,1,2048]{2,1,0:T(1,128)}, u32[]{:S(2)}) copy-start(f32[4,1,2048]{2,1,0:T(1,128)} %weight_ref.1) | copy-start | bytes 98308
  0.0 33.7 %copy-start.1 = (f32[4,2,896]{2,1,0:T(2,128)S(1)}, f32[4,2,896]{2,1,0:T(2,128)}, u32[]{:S(2)}) copy-start(f32[4,2,896]{2,1,0:T(2,128)} %param.11) | copy-start | bytes 86020
  0.0 34.3 %copy-start.2 = (f32[4,896]{1,0:T(4,128)S(1)}, f32[4,896]{1,0:T(4,128)}, u32[]{:S(2)}) copy-start(f32[4,896]{1,0:T(4,128)} %param.8) | copy-start | bytes 43012
  0.0 34.9 %copy-start.3 = (f32[4,896]{1,0:T(4,128)S(1)}, f32[4,896]{1,0:T(4,128)}, u32[]{:S(2)}) copy-start(f32[4,896]{1,0:T(4,128)} %param.10) | copy-start | bytes 43012
  2.1 23.6 %all-to-all-start = ((bf16[64,16,128]{2,1,0:T(8,128)(2,1)}), bf16[64,16,128]{2,1,0:T(8,128)(2,1)S(1)}, u32[]{:S(2)}, u32[]{:S(2)}) async-start(bf16[64,16,128]{2,1,0:T(8,128)(2,1)} %copy.21), calls=%async_computation | async-start | bytes 524288 | tf_op jit(solution)/shard_map/all_to_all | solution.py:343
  27.6 16.4 %all-to-all-start.1 = ((bf16[64,4,256]{2,1,0:T(4,128)(2,1)}), bf16[64,4,256]{2,1,0:T(4,128)(2,1)S(1)}, u32[]{:S(2)}, u32[]{:S(2)}) async-start(bf16[64,4,256]{2,1,0:T(4,128)(2,1)} %copy.24), calls=%async_computation.1 | async-start | bytes 262144 | tf_op jit(solution)/shard_map/all_to_all | solution.py:356

commit v13 on v12

--- a/solution.py
+++ b/solution.py
@@ -165,12 +165,15 @@
     channels, count = d_ref.shape[:2]
     modes = beam_ref.shape[1]
 
-    def beam_forward(vector):
+    def beam_seen(vector):
         low = (chroma * vector).astype(jnp.bfloat16).reshape(channels * count, modes)
         seen = lax.dot_general(
             low, beam_ref[...], (((1,), (1,)), ((), ())), preferred_element_type=jnp.float32
         )
-        return (weight * seen.reshape(channels, count, -1)).astype(jnp.bfloat16)
+        return seen.reshape(channels, count, -1)
+
+    def beam_forward(vector):
+        return (weight * beam_seen(vector)).astype(jnp.bfloat16)
 
     def beam_backward(heard):
         back = jnp.dot(heard.reshape(channels * count, -1), beam_ref[...], preferred_element_type=jnp.float32)
@@ -238,8 +241,11 @@
     d = beam_backward(d_ref[...])
     pl.semaphore_wait(barrier, sum(group_size(stage) - 1 for stage in stages))
     p_state = projection_start(d)
-    cb = beam_backward(beam_forward(d))
-    z_state = row_stage(stages[0], next_row(to_row([column_sum(d * (cb + diag * d)), column_sum(d * d)])))
+    seen = beam_seen(d)
+    heard = (weight * seen).astype(jnp.bfloat16)
+    quadratic = column_sum(seen * heard.astype(jnp.float32)) + column_sum(d * (diag * d))
+    z_state = row_stage(stages[0], next_row(to_row([quadratic, column_sum(d * d)])))
+    cb = beam_backward(heard)
     projection = exchange_finish(p_state)
     zrow = exchange_finish(z_state)
     total = reduce_rest(zrow + to_row([column_sum(projection * projection)]))

time: 103 us -> 103 us (level)
  no operation moved by 1% of the time
where the time goes in v13:
time: 103 us; the launch traced here: 102 us
  Pallas kernels  55.4 us (54%)
  waiting for transfers between devices  20.5 us (20%)
  starting transfers between devices  17.7 us (17%)
  local copies, waits for them, and re-layouts  5.56 us (5%)
  other arithmetic  2.37 us (2%)
    pallas_call x1, Pallas kernels, cg_solve(): pl.pallas_call(functools.partial(cg_kernel, axis_names, stages), out_shap...  55.4 us
    all_to_all x1, waiting for transfers between devices, shards(): received = lax.all_to_all(send, 'ma', 0, 0, tiled=True)  12 us
    all_to_all x1, starting transfers between devices, shards(): received = lax.all_to_all(send, 'ma', 0, 0, tiled=True)  11.6 us
    all_to_all x1, waiting for transfers between devices, shards(): back_rows = lax.all_to_all(mode_rows, 'ma', 0, 0, tiled=True)  8.47 us
    all_to_all x1, starting transfers between devices, shards(): back_rows = lax.all_to_all(mode_rows, 'ma', 0, 0, tiled=True)  6.03 us
  transfers between devices with their start and end apart: 2, of which 2 were waited for; matrix products, arithmetic and copies ran while one was open for 2% of the time, Pallas kernels for 0%

profile of v13, /device:TPU:1, one launch (start us, length us, event | category | flops | bytes accessed | tf_op | source)
XLA Modules:
  0.0 102.4 jit_solution(9897147519287308593)
XLA Ops:
  0.0 0.0 copy-start
  0.0 0.0 copy-start.1
  0.0 0.0 copy-start.2
  0.0 0.0 copy-start.3
  0.0 1.2 %reshape.130 = bf16[4,2,8,8,2,128]{5,4,3,2,1,0:T(2,128)(2,1)S(1)} reshape(bf16[4,2,8,2048]{3,2,1,0:T(8,128)(2,1)} %param.6) | data formatting | bytes 524288 | tf_op jit(solution)/shard_map/reshape | solution.py:345
  1.2 0.9 copy.21
  2.1 11.6 %all-to-all-start = ((bf16[64,16,128]{2,1,0:T(8,128)(2,1)}), bf16[64,16,128]{2,1,0:T(8,128)(2,1)S(1)}, u32[]{:S(2)}, u32[]{:S(2)}) async-start(bf16[64,16,128]{2,1,0:T(8,128)(2,1)} %copy.21), calls=%async_computation | async-start | bytes 524288 | tf_op jit(solution)/shard_map/all_to_all | solution.py:349
  13.7 12.0 %all-to-all-done = bf16[64,16,128]{2,1,0:T(8,128)(2,1)S(1)} async-done(((bf16[64,16,128]{2,1,0:T(8,128)(2,1)}), bf16[64,16,128]{2,1,0:T(8,128)(2,1)S(1)}, u32[]{:S(2)}, u32[]{:S(2)}) %all-to-all-start) | async-done | bytes 262176 | tf_op jit(solution)/shard_map/all_to_all | solution.py:349
  25.7 0.2 reshape.132
  25.9 0.5 convolution_bitcast_fusion
  26.4 0.5 fusion.1
  26.9 0.8 copy.24
  27.6 6.0 %all-to-all-start.1 = ((bf16[64,4,256]{2,1,0:T(4,128)(2,1)}), bf16[64,4,256]{2,1,0:T(4,128)(2,1)S(1)}, u32[]{:S(2)}, u32[]{:S(2)}) async-start(bf16[64,4,256]{2,1,0:T(4,128)(2,1)} %copy.24), calls=%async_computation.1 | async-start | bytes 262144 | tf_op jit(solution)/shard_map/all_to_all | solution.py:362
  33.7 0.0 copy-done
  33.7 0.0 copy-done.1
  33.7 0.6 broadcast_in_dim.17.pm_ref
  34.3 0.0 copy-done.2
  34.3 0.6 broadcast_in_dim.15.chroma_ref
  34.9 0.0 copy-done.3
  34.9 0.6 broadcast_in_dim.16.diag_ref
  35.5 8.5 %all-to-all-done.1 = bf16[64,4,256]{2,1,0:T(4,128)(2,1)S(1)} async-done(((bf16[64,4,256]{2,1,0:T(4,128)(2,1)}), bf16[64,4,256]{2,1,0:T(4,128)(2,1)S(1)}, u32[]{:S(2)}, u32[]{:S(2)}) %all-to-all-start.1) | async-done | bytes 131104 | tf_op jit(solution)/shard_map/all_to_all | solution.py:362
  44.0 0.1 copy.25
  44.1 0.7 multiply_convert_fusion.d_ref
  44.8 55.4 %shard_map.64 = (f32[4,8,896]{2,1,0:T(8,128)}, f32[4,8,896]{2,1,0:T(8,128)}, f32[1,128]{1,0:T(1,128)}) custom-call(bf16[4,8,2048]{2,1,0:T(8,128)(2,1)} %multiply_convert_fusion.d_ref, bf16[2048,896]{1,0:T(8,128)(2,1)} %bitcast.37, f32[4,1,896]{2,1,0:T(1,128)} %broadcast_in_dim.15.chroma_ref, f32[4,1,2048]{2,1,0:T(1,128)} %weight_ref.1, ...), custom_call_target="tpu_custom_call" | custom-call | tf_op jit(solution)/shard_map/pallas_call | solution.py:292
  100.2 0.6 slice_bitcast_fusion
  100.8 1.7 %add_bitcast_fusion = f32[4,1,8,896]{3,2,1,0:T(8,128)} fusion(f32[4,8,896]{2,1,0:T(8,128)} %get-tuple-element.8, f32[4,8,896]{2,1,0:T(8,128)} %get-tuple-element.10, f32[8]{0:T(128)S(1)} %slice_bitcast_fusion), kind=kLoop, calls=%fused_computation.7 | loop fusion | flops 57344 | bytes 344096 | tf_op jit(solution)/shard_map/broadcast_in_dim | solution.py:400
  (3 shorter events, 0.1 us)
Async XLA Ops:
  0.0 33.7 %copy-start = (f32[4,1,2048]{2,1,0:T(1,128)S(1)}, f32[4,1,2048]{2,1,0:T(1,128)}, u32[]{:S(2)}) copy-start(f32[4,1,2048]{2,1,0:T(1,128)} %weight_ref.1) | copy-start | bytes 98308
  0.0 33.7 %copy-start.1 = (f32[4,2,896]{2,1,0:T(2,128)S(1)}, f32[4,2,896]{2,1,0:T(2,128)}, u32[]{:S(2)}) copy-start(f32[4,2,896]{2,1,0:T(2,128)} %param.11) | copy-start | bytes 86020
  0.0 34.3 %copy-start.2 = (f32[4,896]{1,0:T(4,128)S(1)}, f32[4,896]{1,0:T(4,128)}, u32[]{:S(2)}) copy-start(f32[4,896]{1,0:T(4,128)} %param.8) | copy-start | bytes 43012
  0.0 34.9 %copy-start.3 = (f32[4,896]{1,0:T(4,128)S(1)}, f32[4,896]{1,0:T(4,128)}, u32[]{:S(2)}) copy-start(f32[4,896]{1,0:T(4,128)} %param.10) | copy-start | bytes 43012
  2.1 23.6 %all-to-all-start = ((bf16[64,16,128]{2,1,0:T(8,128)(2,1)}), bf16[64,16,128]{2,1,0:T(8,128)(2,1)S(1)}, u32[]{:S(2)}, u32[]{:S(2)}) async-start(bf16[64,16,128]{2,1,0:T(8,128)(2,1)} %copy.21), calls=%async_computation | async-start | bytes 524288 | tf_op jit(solution)/shard_map/all_to_all | solution.py:349
  27.6 16.4 %all-to-all-start.1 = ((bf16[64,4,256]{2,1,0:T(4,128)(2,1)}), bf16[64,4,256]{2,1,0:T(4,128)(2,1)S(1)}, u32[]{:S(2)}, u32[]{:S(2)}) async-start(bf16[64,4,256]{2,1,0:T(4,128)(2,1)} %copy.24), calls=%async_computation.1 | async-start | bytes 262144 | tf_op jit(solution)/shard_map/all_to_all | solution.py:362

commit v14 on v12

--- a/solution.py
+++ b/solution.py
@@ -127,7 +127,7 @@
 
 
 def cg_kernel(axis_names, stages, d_ref, beam_ref, chroma_ref, weight_ref, diag_ref, pm_ref,
-              est_ref, next_ref, step_ref, parts, rows, recv_p, recv_rows, p_send, p_recv, r_send, r_recv):
+              est_ref, parts, rows, recv_p, recv_rows, p_send, p_recv, r_send, r_recv):
     me = {name: lax.axis_index(name) for name in axis_names}
 
     def place(stage):
@@ -266,9 +266,7 @@
     )
     total = reduce_rest(zrow + to_row([column_sum(projection * projection)]))
     curve = from_row(total, 0, count)
-    est_ref[...] = estimate
-    next_ref[...] = direction
-    step_ref[...] = to_row([norm_next / curve])
+    est_ref[...] = estimate + (norm_next / curve)[None] * direction
     for own, size, _, _, copy_to in sent:
         for step in range(1, size):
             copy_to(lax.rem(own + step, size), own).wait_send()
@@ -283,11 +281,11 @@
     row = jax.ShapeDtypeStruct((1, 128), jnp.float32)
     vmem = pl.BlockSpec(memory_space=pltpu.VMEM)
     part_shape = (pm.shape[1],) + vector.shape[1:]
-    estimate, direction, step_row = pl.pallas_call(
+    return pl.pallas_call(
         functools.partial(cg_kernel, axis_names, stages),
-        out_shape=(vector, vector, row),
+        out_shape=vector,
         in_specs=[vmem] * 6,
-        out_specs=(vmem, vmem, vmem),
+        out_specs=vmem,
         scratch_shapes=[
             pltpu.VMEM((2,) + part_shape, jnp.bfloat16),
             pltpu.VMEM((rounds, 1, 128), jnp.float32),
@@ -300,8 +298,6 @@
         ],
         compiler_params=pltpu.CompilerParams(collective_id=1, has_side_effects=True),
     )(d, beam, chroma, weight, diag, pm)
-    step_size = step_row[0, : d.shape[1]]
-    return estimate + step_size[None, :, None] * direction
 
 
 def make_shards(mesh):

time: 103 us -> 102 us (level)
  other arithmetic: 2.37 us -> 0.69 us
    broadcast_in_dim x1 -> x0, other arithmetic: 1.68 us -> none  [shards(): estimate = estimate[:, None]]
    unnamed x9 -> x10, local copies, waits for them, and re-layouts: 0.03 us -> 1.58 us
where the time goes in v14:
time: 102 us
  Pallas kernels  55.3 us (54%)
  waiting for transfers between devices  20.5 us (20%)
  starting transfers between devices  17.6 us (17%)
  local copies, waits for them, and re-layouts  6.52 us (6%)
    pallas_call x1, Pallas kernels, cg_solve(): pl.pallas_call(functools.partial(cg_kernel, axis_names, stages), out_shap...  55.3 us
    all_to_all x1, waiting for transfers between devices, shards(): received = lax.all_to_all(send, 'ma', 0, 0, tiled=True)  12 us
    all_to_all x1, starting transfers between devices, shards(): received = lax.all_to_all(send, 'ma', 0, 0, tiled=True)  11.6 us
    all_to_all x1, waiting for transfers between devices, shards(): back_rows = lax.all_to_all(mode_rows, 'ma', 0, 0, tiled=True)  8.47 us
    all_to_all x1, starting transfers between devices, shards(): back_rows = lax.all_to_all(mode_rows, 'ma', 0, 0, tiled=True)  6.03 us
  transfers between devices with their start and end apart: 2, of which 2 were waited for; matrix products, arithmetic and copies ran while one was open for 2% of the time, Pallas kernels for 0%

profile of v14, /device:TPU:1, one launch (start us, length us, event | category | flops | bytes accessed | tf_op | source)
XLA Modules:
  0.0 101.6 jit_solution(14325060185720975819)
XLA Ops:
  0.0 0.0 copy-start
  0.0 0.0 copy-start.1
  0.0 0.0 copy-start.2
  0.0 0.0 copy-start.3
  0.0 1.2 %reshape.129 = bf16[4,2,8,8,2,128]{5,4,3,2,1,0:T(2,128)(2,1)S(1)} reshape(bf16[4,2,8,2048]{3,2,1,0:T(8,128)(2,1)} %param.6) | data formatting | bytes 524288 | tf_op jit(solution)/shard_map/reshape | solution.py:335
  1.2 0.9 copy.21
  2.1 11.6 %all-to-all-start = ((bf16[64,16,128]{2,1,0:T(8,128)(2,1)}), bf16[64,16,128]{2,1,0:T(8,128)(2,1)S(1)}, u32[]{:S(2)}, u32[]{:S(2)}) async-start(bf16[64,16,128]{2,1,0:T(8,128)(2,1)} %copy.21), calls=%async_computation | async-start | bytes 524288 | tf_op jit(solution)/shard_map/all_to_all | solution.py:339
  13.7 12.0 %all-to-all-done = bf16[64,16,128]{2,1,0:T(8,128)(2,1)S(1)} async-done(((bf16[64,16,128]{2,1,0:T(8,128)(2,1)}), bf16[64,16,128]{2,1,0:T(8,128)(2,1)S(1)}, u32[]{:S(2)}, u32[]{:S(2)}) %all-to-all-start) | async-done | bytes 262176 | tf_op jit(solution)/shard_map/all_to_all | solution.py:339
  25.7 0.2 reshape.131
  25.9 0.5 convolution_bitcast_fusion
  26.4 0.5 fusion.1
  26.9 0.8 copy.24
  27.6 6.0 %all-to-all-start.1 = ((bf16[64,4,256]{2,1,0:T(4,128)(2,1)}), bf16[64,4,256]{2,1,0:T(4,128)(2,1)S(1)}, u32[]{:S(2)}, u32[]{:S(2)}) async-start(bf16[64,4,256]{2,1,0:T(4,128)(2,1)} %copy.24), calls=%async_computation.1 | async-start | bytes 262144 | tf_op jit(solution)/shard_map/all_to_all | solution.py:352
  33.7 0.0 copy-done
  33.7 0.0 copy-done.1
  33.7 0.6 broadcast_in_dim.17.pm_ref
  34.3 0.0 copy-done.2
  34.3 0.6 broadcast_in_dim.15.chroma_ref
  34.9 0.0 copy-done.3
  34.9 0.6 broadcast_in_dim.16.diag_ref
  35.5 8.5 %all-to-all-done.1 = bf16[64,4,256]{2,1,0:T(4,128)(2,1)S(1)} async-done(((bf16[64,4,256]{2,1,0:T(4,128)(2,1)}), bf16[64,4,256]{2,1,0:T(4,128)(2,1)S(1)}, u32[]{:S(2)}, u32[]{:S(2)}) %all-to-all-start.1) | async-done | bytes 131104 | tf_op jit(solution)/shard_map/all_to_all | solution.py:352
  44.0 0.1 copy.25
  44.1 0.7 multiply_convert_fusion.d_ref
  44.8 55.3 %shard_map.64 = f32[4,8,896]{2,1,0:T(8,128)} custom-call(bf16[4,8,2048]{2,1,0:T(8,128)(2,1)} %multiply_convert_fusion.d_ref, bf16[2048,896]{1,0:T(8,128)(2,1)} %bitcast.34, f32[4,1,896]{2,1,0:T(1,128)} %broadcast_in_dim.15.chroma_ref, f32[4,1,2048]{2,1,0:T(1,128)} %weight_ref.1, f32[4,1,896]{2,1,0:T(1,128)} %broadcast_in_dim.16.diag_ref, ...), custom_call_target="tpu_custom_call" | custom-call | tf_op jit(solution)/shard_map/pallas_call | solution.py:284
  100.1 1.6 %copy.37 = f32[4,1,8,896]{3,2,1,0:T(8,128)} copy(f32[4,1,8,896]{3,2,1,0:T(8,128)} %bitcast.39) | data formatting | bytes 229376
  (3 shorter events, 0.1 us)
Async XLA Ops:
  0.0 33.7 %copy-start = (f32[4,1,2048]{2,1,0:T(1,128)S(1)}, f32[4,1,2048]{2,1,0:T(1,128)}, u32[]{:S(2)}) copy-start(f32[4,1,2048]{2,1,0:T(1,128)} %weight_ref.1) | copy-start | bytes 98308
  0.0 33.7 %copy-start.1 = (f32[4,2,896]{2,1,0:T(2,128)S(1)}, f32[4,2,896]{2,1,0:T(2,128)}, u32[]{:S(2)}) copy-start(f32[4,2,896]{2,1,0:T(2,128)} %param.11) | copy-start | bytes 86020
  0.0 34.3 %copy-start.2 = (f32[4,896]{1,0:T(4,128)S(1)}, f32[4,896]{1,0:T(4,128)}, u32[]{:S(2)}) copy-start(f32[4,896]{1,0:T(4,128)} %param.8) | copy-start | bytes 43012
  0.0 34.9 %copy-start.3 = (f32[4,896]{1,0:T(4,128)S(1)}, f32[4,896]{1,0:T(4,128)}, u32[]{:S(2)}) copy-start(f32[4,896]{1,0:T(4,128)} %param.10) | copy-start | bytes 43012
  2.1 23.6 %all-to-all-start = ((bf16[64,16,128]{2,1,0:T(8,128)(2,1)}), bf16[64,16,128]{2,1,0:T(8,128)(2,1)S(1)}, u32[]{:S(2)}, u32[]{:S(2)}) async-start(bf16[64,16,128]{2,1,0:T(8,128)(2,1)} %copy.21), calls=%async_computation | async-start | bytes 524288 | tf_op jit(solution)/shard_map/all_to_all | solution.py:339
  27.6 16.4 %all-to-all-start.1 = ((bf16[64,4,256]{2,1,0:T(4,128)(2,1)}), bf16[64,4,256]{2,1,0:T(4,128)(2,1)S(1)}, u32[]{:S(2)}, u32[]{:S(2)}) async-start(bf16[64,4,256]{2,1,0:T(4,128)(2,1)} %copy.24), calls=%async_computation.1 | async-start | bytes 262144 | tf_op jit(solution)/shard_map/all_to_all | solution.py:352

commit v15 on v14

--- a/solution.py
+++ b/solution.py
@@ -126,8 +126,8 @@
     return size
 
 
-def cg_kernel(axis_names, stages, d_ref, beam_ref, chroma_ref, weight_ref, diag_ref, pm_ref,
-              est_ref, parts, rows, recv_p, recv_rows, p_send, p_recv, r_send, r_recv):
+def cg_kernel(axis_names, stages, d_ref, beam_hbm, chroma_ref, weight_ref, diag_ref, pm_ref,
+              est_ref, beam_ref, beam_sems, parts, rows, recv_p, recv_rows, p_send, p_recv, r_send, r_recv):
     me = {name: lax.axis_index(name) for name in axis_names}
 
     def place(stage):
@@ -158,6 +158,15 @@
             other = lax.rem(own + step, group_size(stage))
             pl.semaphore_signal(barrier, 1, device_id=device(other), device_id_type=MESH)
 
+    chunks = beam_sems.shape[0]
+    rows_per = beam_ref.shape[0] // chunks
+    beam_copies = []
+    for chunk in range(chunks):
+        window = pl.ds(chunk * rows_per, rows_per)
+        beam_copy = pltpu.make_async_copy(beam_hbm.at[window], beam_ref.at[window], beam_sems.at[chunk])
+        beam_copy.start()
+        beam_copies.append(beam_copy)
+
     chroma = chroma_ref[...]
     weight = weight_ref[...]
     diag = diag_ref[...]
@@ -235,7 +244,16 @@
         nz = group_size(stages[0])
         return exchange_start(stages[0], parts.at[index], recv_p, index * nz, p_send, p_recv)
 
-    d = beam_backward(d_ref[...])
+    weighted = d_ref[...].reshape(channels * count, -1)
+    back = None
+    for chunk, beam_copy in enumerate(beam_copies):
+        beam_copy.wait()
+        window = slice(chunk * rows_per, (chunk + 1) * rows_per)
+        term = jnp.dot(
+            weighted[:, window], beam_ref[window, :], preferred_element_type=jnp.float32
+        )
+        back = term if back is None else back + term
+    d = chroma * back.reshape(channels, count, modes)
     pl.semaphore_wait(barrier, sum(group_size(stage) - 1 for stage in stages))
     p_state = projection_start(d)
     cb = beam_backward(beam_forward(d))
@@ -284,9 +302,11 @@
     return pl.pallas_call(
         functools.partial(cg_kernel, axis_names, stages),
         out_shape=vector,
-        in_specs=[vmem] * 6,
+        in_specs=[vmem, pl.BlockSpec(memory_space=pl.ANY)] + [vmem] * 4,
         out_specs=vmem,
         scratch_shapes=[
+            pltpu.VMEM(beam.shape, beam.dtype),
+            pltpu.SemaphoreType.DMA((4,)),
             pltpu.VMEM((2,) + part_shape, jnp.bfloat16),
             pltpu.VMEM((rounds, 1, 128), jnp.float32),
             pltpu.VMEM((2 * nz,) + part_shape, jnp.bfloat16),

time: 102 us -> 101 us (level)
  Pallas kernels: 55.3 us -> 54.2 us
    pallas_call x1, Pallas kernels: 55.3 us -> 54.2 us  [cg_solve(): pl.pallas_call(functools.partial(cg_kernel, axis_names, stages), out_shap...]
where the time goes in v15:
time: 101 us
  Pallas kernels  54.2 us (54%)
  waiting for transfers between devices  20.5 us (20%)
  starting transfers between devices  17.6 us (17%)
  local copies, waits for them, and re-layouts  6.52 us (6%)
    pallas_call x1, Pallas kernels, cg_solve(): pl.pallas_call(functools.partial(cg_kernel, axis_names, stages), out_shap...  54.2 us
    all_to_all x1, waiting for transfers between devices, shards(): received = lax.all_to_all(send, 'ma', 0, 0, tiled=True)  12 us
    all_to_all x1, starting transfers between devices, shards(): received = lax.all_to_all(send, 'ma', 0, 0, tiled=True)  11.6 us
    all_to_all x1, waiting for transfers between devices, shards(): back_rows = lax.all_to_all(mode_rows, 'ma', 0, 0, tiled=True)  8.47 us
    all_to_all x1, starting transfers between devices, shards(): back_rows = lax.all_to_all(mode_rows, 'ma', 0, 0, tiled=True)  6.03 us
  transfers between devices with their start and end apart: 2, of which 2 were waited for; matrix products, arithmetic and copies ran while one was open for 2% of the time, Pallas kernels for 0%

profile of v15, /device:TPU:1, one launch (start us, length us, event | category | flops | bytes accessed | tf_op | source)
XLA Modules:
  0.0 100.6 jit_solution(4835775526896079120)
XLA Ops:
  0.0 0.0 copy-start
  0.0 0.0 copy-start.1
  0.0 0.0 copy-start.2
  0.0 0.0 copy-start.3
  0.0 1.2 %reshape.129 = bf16[4,2,8,8,2,128]{5,4,3,2,1,0:T(2,128)(2,1)S(1)} reshape(bf16[4,2,8,2048]{3,2,1,0:T(8,128)(2,1)} %param.6) | data formatting | bytes 524288 | tf_op jit(solution)/shard_map/reshape | solution.py:355
  1.2 0.9 copy.21
  2.1 11.6 %all-to-all-start = ((bf16[64,16,128]{2,1,0:T(8,128)(2,1)}), bf16[64,16,128]{2,1,0:T(8,128)(2,1)S(1)}, u32[]{:S(2)}, u32[]{:S(2)}) async-start(bf16[64,16,128]{2,1,0:T(8,128)(2,1)} %copy.21), calls=%async_computation | async-start | bytes 524288 | tf_op jit(solution)/shard_map/all_to_all | solution.py:359
  13.7 12.0 %all-to-all-done = bf16[64,16,128]{2,1,0:T(8,128)(2,1)S(1)} async-done(((bf16[64,16,128]{2,1,0:T(8,128)(2,1)}), bf16[64,16,128]{2,1,0:T(8,128)(2,1)S(1)}, u32[]{:S(2)}, u32[]{:S(2)}) %all-to-all-start) | async-done | bytes 262176 | tf_op jit(solution)/shard_map/all_to_all | solution.py:359
  25.7 0.2 reshape.131
  25.9 0.5 convolution_bitcast_fusion
  26.4 0.5 fusion.1
  26.9 0.8 copy.24
  27.6 6.0 %all-to-all-start.1 = ((bf16[64,4,256]{2,1,0:T(4,128)(2,1)}), bf16[64,4,256]{2,1,0:T(4,128)(2,1)S(1)}, u32[]{:S(2)}, u32[]{:S(2)}) async-start(bf16[64,4,256]{2,1,0:T(4,128)(2,1)} %copy.24), calls=%async_computation.1 | async-start | bytes 262144 | tf_op jit(solution)/shard_map/all_to_all | solution.py:372
  33.7 0.0 copy-done
  33.7 0.0 copy-done.1
  33.7 0.6 broadcast_in_dim.17.pm_ref
  34.3 0.0 copy-done.2
  34.3 0.6 broadcast_in_dim.15.chroma_ref
  34.9 0.0 copy-done.3
  34.9 0.6 broadcast_in_dim.16.diag_ref
  35.5 8.5 %all-to-all-done.1 = bf16[64,4,256]{2,1,0:T(4,128)(2,1)S(1)} async-done(((bf16[64,4,256]{2,1,0:T(4,128)(2,1)}), bf16[64,4,256]{2,1,0:T(4,128)(2,1)S(1)}, u32[]{:S(2)}, u32[]{:S(2)}) %all-to-all-start.1) | async-done | bytes 131104 | tf_op jit(solution)/shard_map/all_to_all | solution.py:372
  44.0 0.1 copy.25
  44.1 0.7 multiply_convert_fusion.d_ref
  44.8 54.2 %shard_map.64 = f32[4,8,896]{2,1,0:T(8,128)} custom-call(bf16[4,8,2048]{2,1,0:T(8,128)(2,1)} %multiply_convert_fusion.d_ref, bf16[2048,896]{1,0:T(8,128)(2,1)} %bitcast.34, f32[4,1,896]{2,1,0:T(1,128)} %broadcast_in_dim.15.chroma_ref, f32[4,1,2048]{2,1,0:T(1,128)} %weight_ref.1, f32[4,1,896]{2,1,0:T(1,128)} %broadcast_in_dim.16.diag_ref, ...), custom_call_target="tpu_custom_call" | custom-call | tf_op jit(solution)/shard_map/pallas_call | solution.py:302
  99.0 1.6 %copy.37 = f32[4,1,8,896]{3,2,1,0:T(8,128)} copy(f32[4,1,8,896]{3,2,1,0:T(8,128)} %bitcast.39) | data formatting | bytes 229376
  (3 shorter events, 0.1 us)
Async XLA Ops:
  0.0 33.7 %copy-start = (f32[4,1,2048]{2,1,0:T(1,128)S(1)}, f32[4,1,2048]{2,1,0:T(1,128)}, u32[]{:S(2)}) copy-start(f32[4,1,2048]{2,1,0:T(1,128)} %weight_ref.1) | copy-start | bytes 98308
  0.0 33.7 %copy-start.1 = (f32[4,2,896]{2,1,0:T(2,128)S(1)}, f32[4,2,896]{2,1,0:T(2,128)}, u32[]{:S(2)}) copy-start(f32[4,2,896]{2,1,0:T(2,128)} %param.11) | copy-start | bytes 86020
  0.0 34.3 %copy-start.2 = (f32[4,896]{1,0:T(4,128)S(1)}, f32[4,896]{1,0:T(4,128)}, u32[]{:S(2)}) copy-start(f32[4,896]{1,0:T(4,128)} %param.8) | copy-start | bytes 43012
  0.0 34.9 %copy-start.3 = (f32[4,896]{1,0:T(4,128)S(1)}, f32[4,896]{1,0:T(4,128)}, u32[]{:S(2)}) copy-start(f32[4,896]{1,0:T(4,128)} %param.10) | copy-start | bytes 43012
  2.1 23.6 %all-to-all-start = ((bf16[64,16,128]{2,1,0:T(8,128)(2,1)}), bf16[64,16,128]{2,1,0:T(8,128)(2,1)S(1)}, u32[]{:S(2)}, u32[]{:S(2)}) async-start(bf16[64,16,128]{2,1,0:T(8,128)(2,1)} %copy.21), calls=%async_computation | async-start | bytes 524288 | tf_op jit(solution)/shard_map/all_to_all | solution.py:359
  27.6 16.4 %all-to-all-start.1 = ((bf16[64,4,256]{2,1,0:T(4,128)(2,1)}), bf16[64,4,256]{2,1,0:T(4,128)(2,1)S(1)}, u32[]{:S(2)}, u32[]{:S(2)}) async-start(bf16[64,4,256]{2,1,0:T(4,128)(2,1)} %copy.24), calls=%async_computation.1 | async-start | bytes 262144 | tf_op jit(solution)/shard_map/all_to_all | solution.py:372

commit v16 on v15

--- a/solution.py
+++ b/solution.py
@@ -174,12 +174,15 @@
     channels, count = d_ref.shape[:2]
     modes = beam_ref.shape[1]
 
-    def beam_forward(vector):
+    def beam_seen(vector):
         low = (chroma * vector).astype(jnp.bfloat16).reshape(channels * count, modes)
         seen = lax.dot_general(
             low, beam_ref[...], (((1,), (1,)), ((), ())), preferred_element_type=jnp.float32
         )
-        return (weight * seen.reshape(channels, count, -1)).astype(jnp.bfloat16)
+        return seen.reshape(channels, count, -1)
+
+    def beam_forward(vector):
+        return (weight * beam_seen(vector)).astype(jnp.bfloat16)
 
     def beam_backward(heard):
         back = jnp.dot(heard.reshape(channels * count, -1), beam_ref[...], preferred_element_type=jnp.float32)
@@ -256,8 +259,11 @@
     d = chroma * back.reshape(channels, count, modes)
     pl.semaphore_wait(barrier, sum(group_size(stage) - 1 for stage in stages))
     p_state = projection_start(d)
-    cb = beam_backward(beam_forward(d))
-    z_state = row_stage(stages[0], next_row(to_row([column_sum(d * (cb + diag * d)), column_sum(d * d)])))
+    seen = beam_seen(d)
+    heard = (weight * seen).astype(jnp.bfloat16)
+    quadratic = column_sum(seen * heard.astype(jnp.float32)) + column_sum(d * (diag * d))
+    z_state = row_stage(stages[0], next_row(to_row([quadratic, column_sum(d * d)])))
+    cb = beam_backward(heard)
     projection = exchange_finish(p_state)
     zrow = exchange_finish(z_state)
     total = reduce_rest(zrow + to_row([column_sum(projection * projection)]))

time: 101 us -> 101 us (level)
  no operation moved by 1% of the time
where the time goes in v16:
time: 101 us
  Pallas kernels  54.2 us (54%)
  waiting for transfers between devices  20.5 us (20%)
  starting transfers between devices  17.6 us (17%)
  local copies, waits for them, and re-layouts  6.52 us (6%)
    pallas_call x1, Pallas kernels, cg_solve(): pl.pallas_call(functools.partial(cg_kernel, axis_names, stages), out_shap...  54.2 us
    all_to_all x1, waiting for transfers between devices, shards(): received = lax.all_to_all(send, 'ma', 0, 0, tiled=True)  12 us
    all_to_all x1, starting transfers between devices, shards(): received = lax.all_to_all(send, 'ma', 0, 0, tiled=True)  11.6 us
    all_to_all x1, waiting for transfers between devices, shards(): back_rows = lax.all_to_all(mode_rows, 'ma', 0, 0, tiled=True)  8.47 us
    all_to_all x1, starting transfers between devices, shards(): back_rows = lax.all_to_all(mode_rows, 'ma', 0, 0, tiled=True)  6.03 us
  transfers between devices with their start and end apart: 2, of which 2 were waited for; matrix products, arithmetic and copies ran while one was open for 2% of the time, Pallas kernels for 0%

profile of v16, /device:TPU:1, one launch (start us, length us, event | category | flops | bytes accessed | tf_op | source)
XLA Modules:
  0.0 100.6 jit_solution(13437297779019627046)
XLA Ops:
  0.0 0.0 copy-start
  0.0 0.0 copy-start.1
  0.0 0.0 copy-start.2
  0.0 0.0 copy-start.3
  0.0 1.2 %reshape.129 = bf16[4,2,8,8,2,128]{5,4,3,2,1,0:T(2,128)(2,1)S(1)} reshape(bf16[4,2,8,2048]{3,2,1,0:T(8,128)(2,1)} %param.6) | data formatting | bytes 524288 | tf_op jit(solution)/shard_map/reshape | solution.py:361
  1.2 0.9 copy.21
  2.1 11.6 %all-to-all-start = ((bf16[64,16,128]{2,1,0:T(8,128)(2,1)}), bf16[64,16,128]{2,1,0:T(8,128)(2,1)S(1)}, u32[]{:S(2)}, u32[]{:S(2)}) async-start(bf16[64,16,128]{2,1,0:T(8,128)(2,1)} %copy.21), calls=%async_computation | async-start | bytes 524288 | tf_op jit(solution)/shard_map/all_to_all | solution.py:365
  13.7 12.0 %all-to-all-done = bf16[64,16,128]{2,1,0:T(8,128)(2,1)S(1)} async-done(((bf16[64,16,128]{2,1,0:T(8,128)(2,1)}), bf16[64,16,128]{2,1,0:T(8,128)(2,1)S(1)}, u32[]{:S(2)}, u32[]{:S(2)}) %all-to-all-start) | async-done | bytes 262176 | tf_op jit(solution)/shard_map/all_to_all | solution.py:365
  25.7 0.2 reshape.131
  25.9 0.5 convolution_bitcast_fusion
  26.4 0.5 fusion.1
  26.9 0.8 copy.24
  27.6 6.0 %all-to-all-start.1 = ((bf16[64,4,256]{2,1,0:T(4,128)(2,1)}), bf16[64,4,256]{2,1,0:T(4,128)(2,1)S(1)}, u32[]{:S(2)}, u32[]{:S(2)}) async-start(bf16[64,4,256]{2,1,0:T(4,128)(2,1)} %copy.24), calls=%async_computation.1 | async-start | bytes 262144 | tf_op jit(solution)/shard_map/all_to_all | solution.py:378
  33.7 0.0 copy-done
  33.7 0.0 copy-done.1
  33.7 0.6 broadcast_in_dim.17.pm_ref
  34.3 0.0 copy-done.2
  34.3 0.6 broadcast_in_dim.15.chroma_ref
  34.9 0.0 copy-done.3
  34.9 0.6 broadcast_in_dim.16.diag_ref
  35.5 8.5 %all-to-all-done.1 = bf16[64,4,256]{2,1,0:T(4,128)(2,1)S(1)} async-done(((bf16[64,4,256]{2,1,0:T(4,128)(2,1)}), bf16[64,4,256]{2,1,0:T(4,128)(2,1)S(1)}, u32[]{:S(2)}, u32[]{:S(2)}) %all-to-all-start.1) | async-done | bytes 131104 | tf_op jit(solution)/shard_map/all_to_all | solution.py:378
  44.0 0.1 copy.25
  44.1 0.7 multiply_convert_fusion.d_ref
  44.8 54.2 %shard_map.64 = f32[4,8,896]{2,1,0:T(8,128)} custom-call(bf16[4,8,2048]{2,1,0:T(8,128)(2,1)} %multiply_convert_fusion.d_ref, bf16[2048,896]{1,0:T(8,128)(2,1)} %bitcast.34, f32[4,1,896]{2,1,0:T(1,128)} %broadcast_in_dim.15.chroma_ref, f32[4,1,2048]{2,1,0:T(1,128)} %weight_ref.1, f32[4,1,896]{2,1,0:T(1,128)} %broadcast_in_dim.16.diag_ref, ...), custom_call_target="tpu_custom_call" | custom-call | tf_op jit(solution)/shard_map/pallas_call | solution.py:308
  99.0 1.6 %copy.37 = f32[4,1,8,896]{3,2,1,0:T(8,128)} copy(f32[4,1,8,896]{3,2,1,0:T(8,128)} %bitcast.39) | data formatting | bytes 229376
  (3 shorter events, 0.1 us)
Async XLA Ops:
  0.0 33.7 %copy-start = (f32[4,1,2048]{2,1,0:T(1,128)S(1)}, f32[4,1,2048]{2,1,0:T(1,128)}, u32[]{:S(2)}) copy-start(f32[4,1,2048]{2,1,0:T(1,128)} %weight_ref.1) | copy-start | bytes 98308
  0.0 33.7 %copy-start.1 = (f32[4,2,896]{2,1,0:T(2,128)S(1)}, f32[4,2,896]{2,1,0:T(2,128)}, u32[]{:S(2)}) copy-start(f32[4,2,896]{2,1,0:T(2,128)} %param.11) | copy-start | bytes 86020
  0.0 34.3 %copy-start.2 = (f32[4,896]{1,0:T(4,128)S(1)}, f32[4,896]{1,0:T(4,128)}, u32[]{:S(2)}) copy-start(f32[4,896]{1,0:T(4,128)} %param.8) | copy-start | bytes 43012
  0.0 34.9 %copy-start.3 = (f32[4,896]{1,0:T(4,128)S(1)}, f32[4,896]{1,0:T(4,128)}, u32[]{:S(2)}) copy-start(f32[4,896]{1,0:T(4,128)} %param.10) | copy-start | bytes 43012
  2.1 23.6 %all-to-all-start = ((bf16[64,16,128]{2,1,0:T(8,128)(2,1)}), bf16[64,16,128]{2,1,0:T(8,128)(2,1)S(1)}, u32[]{:S(2)}, u32[]{:S(2)}) async-start(bf16[64,16,128]{2,1,0:T(8,128)(2,1)} %copy.21), calls=%async_computation | async-start | bytes 524288 | tf_op jit(solution)/shard_map/all_to_all | solution.py:365
  27.6 16.4 %all-to-all-start.1 = ((bf16[64,4,256]{2,1,0:T(4,128)(2,1)}), bf16[64,4,256]{2,1,0:T(4,128)(2,1)S(1)}, u32[]{:S(2)}, u32[]{:S(2)}) async-start(bf16[64,4,256]{2,1,0:T(4,128)(2,1)} %copy.24), calls=%async_computation.1 | async-start | bytes 262144 | tf_op jit(solution)/shard_map/all_to_all | solution.py:378

commit v17 on v16

--- a/solution.py
+++ b/solution.py
@@ -276,9 +276,10 @@
         spread = spread + pm[:, rank] * projection[rank][None]
     residual = d - step_size * (cb + diag * d + spread)
     z_state = row_stage(stages[0], next_row(to_row([column_sum(residual * residual)])))
+    cb_residual = beam_backward(beam_forward(residual))
+    zrow = exchange_finish(z_state)
     p_state = projection_start(residual)
-    cb_residual = beam_backward(beam_forward(residual))
-    total = reduce_rest(exchange_finish(z_state))
+    total = reduce_rest(zrow)
     projection_residual = exchange_finish(p_state)
     norm_next = from_row(total, 0, count)
     ratio = (norm_next / norm_now)[None]

time: 101 us -> 101 us (level)
  no operation moved by 1% of the time
where the time goes in v17:
time: 101 us; the launch traced here: 100 us
  Pallas kernels  54.1 us (54%)
  waiting for transfers between devices  20.5 us (20%)
  starting transfers between devices  17.6 us (17%)
  local copies, waits for them, and re-layouts  6.52 us (6%)
    pallas_call x1, Pallas kernels, cg_solve(): pl.pallas_call(functools.partial(cg_kernel, axis_names, stages), out_shap...  54.1 us
    all_to_all x1, waiting for transfers between devices, shards(): received = lax.all_to_all(send, 'ma', 0, 0, tiled=True)  12 us
    all_to_all x1, starting transfers between devices, shards(): received = lax.all_to_all(send, 'ma', 0, 0, tiled=True)  11.6 us
    all_to_all x1, waiting for transfers between devices, shards(): back_rows = lax.all_to_all(mode_rows, 'ma', 0, 0, tiled=True)  8.47 us
    all_to_all x1, starting transfers between devices, shards(): back_rows = lax.all_to_all(mode_rows, 'ma', 0, 0, tiled=True)  6.03 us
  transfers between devices with their start and end apart: 2, of which 2 were waited for; matrix products, arithmetic and copies ran while one was open for 2% of the time, Pallas kernels for 0%

profile of v17, /device:TPU:1, one launch (start us, length us, event | category | flops | bytes accessed | tf_op | source)
XLA Modules:
  0.0 100.5 jit_solution(18024869992694828336)
XLA Ops:
  0.0 0.0 copy-start
  0.0 0.0 copy-start.1
  0.0 0.0 copy-start.2
  0.0 0.0 copy-start.3
  0.0 1.2 %reshape.129 = bf16[4,2,8,8,2,128]{5,4,3,2,1,0:T(2,128)(2,1)S(1)} reshape(bf16[4,2,8,2048]{3,2,1,0:T(8,128)(2,1)} %param.6) | data formatting | bytes 524288 | tf_op jit(solution)/shard_map/reshape | solution.py:362
  1.2 0.9 copy.21
  2.1 11.6 %all-to-all-start = ((bf16[64,16,128]{2,1,0:T(8,128)(2,1)}), bf16[64,16,128]{2,1,0:T(8,128)(2,1)S(1)}, u32[]{:S(2)}, u32[]{:S(2)}) async-start(bf16[64,16,128]{2,1,0:T(8,128)(2,1)} %copy.21), calls=%async_computation | async-start | bytes 524288 | tf_op jit(solution)/shard_map/all_to_all | solution.py:366
  13.7 12.0 %all-to-all-done = bf16[64,16,128]{2,1,0:T(8,128)(2,1)S(1)} async-done(((bf16[64,16,128]{2,1,0:T(8,128)(2,1)}), bf16[64,16,128]{2,1,0:T(8,128)(2,1)S(1)}, u32[]{:S(2)}, u32[]{:S(2)}) %all-to-all-start) | async-done | bytes 262176 | tf_op jit(solution)/shard_map/all_to_all | solution.py:366
  25.7 0.2 reshape.131
  25.9 0.5 convolution_bitcast_fusion
  26.4 0.5 fusion.1
  26.9 0.8 copy.24
  27.6 6.0 %all-to-all-start.1 = ((bf16[64,4,256]{2,1,0:T(4,128)(2,1)}), bf16[64,4,256]{2,1,0:T(4,128)(2,1)S(1)}, u32[]{:S(2)}, u32[]{:S(2)}) async-start(bf16[64,4,256]{2,1,0:T(4,128)(2,1)} %copy.24), calls=%async_computation.1 | async-start | bytes 262144 | tf_op jit(solution)/shard_map/all_to_all | solution.py:379
  33.7 0.0 copy-done
  33.7 0.0 copy-done.1
  33.7 0.6 broadcast_in_dim.17.pm_ref
  34.3 0.0 copy-done.2
  34.3 0.6 broadcast_in_dim.15.chroma_ref
  34.9 0.0 copy-done.3
  34.9 0.6 broadcast_in_dim.16.diag_ref
  35.5 8.5 %all-to-all-done.1 = bf16[64,4,256]{2,1,0:T(4,128)(2,1)S(1)} async-done(((bf16[64,4,256]{2,1,0:T(4,128)(2,1)}), bf16[64,4,256]{2,1,0:T(4,128)(2,1)S(1)}, u32[]{:S(2)}, u32[]{:S(2)}) %all-to-all-start.1) | async-done | bytes 131104 | tf_op jit(solution)/shard_map/all_to_all | solution.py:379
  44.0 0.1 copy.25
  44.1 0.7 multiply_convert_fusion.d_ref
  44.8 54.1 %shard_map.64 = f32[4,8,896]{2,1,0:T(8,128)} custom-call(bf16[4,8,2048]{2,1,0:T(8,128)(2,1)} %multiply_convert_fusion.d_ref, bf16[2048,896]{1,0:T(8,128)(2,1)} %bitcast.34, f32[4,1,896]{2,1,0:T(1,128)} %broadcast_in_dim.15.chroma_ref, f32[4,1,2048]{2,1,0:T(1,128)} %weight_ref.1, f32[4,1,896]{2,1,0:T(1,128)} %broadcast_in_dim.16.diag_ref, ...), custom_call_target="tpu_custom_call" | custom-call | tf_op jit(solution)/shard_map/pallas_call | solution.py:309
  98.9 1.6 %copy.37 = f32[4,1,8,896]{3,2,1,0:T(8,128)} copy(f32[4,1,8,896]{3,2,1,0:T(8,128)} %bitcast.39) | data formatting | bytes 229376
  (3 shorter events, 0.1 us)
Async XLA Ops:
  0.0 33.7 %copy-start = (f32[4,1,2048]{2,1,0:T(1,128)S(1)}, f32[4,1,2048]{2,1,0:T(1,128)}, u32[]{:S(2)}) copy-start(f32[4,1,2048]{2,1,0:T(1,128)} %weight_ref.1) | copy-start | bytes 98308
  0.0 33.7 %copy-start.1 = (f32[4,2,896]{2,1,0:T(2,128)S(1)}, f32[4,2,896]{2,1,0:T(2,128)}, u32[]{:S(2)}) copy-start(f32[4,2,896]{2,1,0:T(2,128)} %param.11) | copy-start | bytes 86020
  0.0 34.3 %copy-start.2 = (f32[4,896]{1,0:T(4,128)S(1)}, f32[4,896]{1,0:T(4,128)}, u32[]{:S(2)}) copy-start(f32[4,896]{1,0:T(4,128)} %param.8) | copy-start | bytes 43012
  0.0 34.9 %copy-start.3 = (f32[4,896]{1,0:T(4,128)S(1)}, f32[4,896]{1,0:T(4,128)}, u32[]{:S(2)}) copy-start(f32[4,896]{1,0:T(4,128)} %param.10) | copy-start | bytes 43012
  2.1 23.6 %all-to-all-start = ((bf16[64,16,128]{2,1,0:T(8,128)(2,1)}), bf16[64,16,128]{2,1,0:T(8,128)(2,1)S(1)}, u32[]{:S(2)}, u32[]{:S(2)}) async-start(bf16[64,16,128]{2,1,0:T(8,128)(2,1)} %copy.21), calls=%async_computation | async-start | bytes 524288 | tf_op jit(solution)/shard_map/all_to_all | solution.py:366
  27.6 16.4 %all-to-all-start.1 = ((bf16[64,4,256]{2,1,0:T(4,128)(2,1)}), bf16[64,4,256]{2,1,0:T(4,128)(2,1)S(1)}, u32[]{:S(2)}, u32[]{:S(2)}) async-start(bf16[64,4,256]{2,1,0:T(4,128)(2,1)} %copy.24), calls=%async_computation.1 | async-start | bytes 262144 | tf_op jit(solution)/shard_map/all_to_all | solution.py:379

commit v18 on v16

--- a/solution.py
+++ b/solution.py
@@ -127,7 +127,7 @@
 
 
 def cg_kernel(axis_names, stages, d_ref, beam_hbm, chroma_ref, weight_ref, diag_ref, pm_ref,
-              est_ref, beam_ref, beam_sems, parts, rows, recv_p, recv_rows, p_send, p_recv, r_send, r_recv):
+              est_ref, next_ref, step_ref, beam_ref, beam_sems, parts, rows, recv_p, recv_rows, p_send, p_recv, r_send, r_recv):
     me = {name: lax.axis_index(name) for name in axis_names}
 
     def place(stage):
@@ -290,7 +290,9 @@
     )
     total = reduce_rest(zrow + to_row([column_sum(projection * projection)]))
     curve = from_row(total, 0, count)
-    est_ref[...] = estimate + (norm_next / curve)[None] * direction
+    est_ref[...] = estimate
+    next_ref[...] = direction
+    step_ref[...] = to_row([norm_next / curve])
     for own, size, _, _, copy_to in sent:
         for step in range(1, size):
             copy_to(lax.rem(own + step, size), own).wait_send()
@@ -305,11 +307,11 @@
     row = jax.ShapeDtypeStruct((1, 128), jnp.float32)
     vmem = pl.BlockSpec(memory_space=pltpu.VMEM)
     part_shape = (pm.shape[1],) + vector.shape[1:]
-    return pl.pallas_call(
+    estimate, direction, step_row = pl.pallas_call(
         functools.partial(cg_kernel, axis_names, stages),
-        out_shape=vector,
+        out_shape=(vector, vector, row),
         in_specs=[vmem, pl.BlockSpec(memory_space=pl.ANY)] + [vmem] * 4,
-        out_specs=vmem,
+        out_specs=(vmem, vmem, vmem),
         scratch_shapes=[
             pltpu.VMEM(beam.shape, beam.dtype),
             pltpu.SemaphoreType.DMA((4,)),
@@ -324,6 +326,18 @@
         ],
         compiler_params=pltpu.CompilerParams(collective_id=1, has_side_effects=True),
     )(d, beam, chroma, weight, diag, pm)
+    return pl.pallas_call(
+        finish_kernel,
+        out_shape=vector,
+        in_specs=[vmem] * 3,
+        out_specs=vmem,
+    )(estimate, direction, step_row)
+
+
+def finish_kernel(est_ref, direction_ref, step_ref, out_ref):
+    count = direction_ref.shape[1]
+    step_size = from_row(step_ref[...], 0, count)
+    out_ref[...] = est_ref[...] + step_size[None] * direction_ref[...]
 
 
 def make_shards(mesh):

time: 101 us -> 101 us (level)
  Pallas kernels: 54.2 us -> 56 us
  local copies, waits for them, and re-layouts: 6.52 us -> 4.96 us
    pallas_call x0 -> x1, Pallas kernels: none -> 1.69 us  [cg_solve(): pl.pallas_call(finish_kernel, out_shape=vector, in_specs=[vmem] * 3, out_...]
    unnamed x10 -> x9, local copies, waits for them, and re-layouts: 1.58 us -> 0.03 us
where the time goes in v18:
time: 101 us
  Pallas kernels  56 us (55%)
  waiting for transfers between devices  20.5 us (20%)
  starting transfers between devices  17.7 us (18%)
  local copies, waits for them, and re-layouts  4.96 us (5%)
    pallas_call x1, Pallas kernels, cg_solve(): pl.pallas_call(functools.partial(cg_kernel, axis_names, stages), out_shap...  54.3 us
    all_to_all x1, waiting for transfers between devices, shards(): received = lax.all_to_all(send, 'ma', 0, 0, tiled=True)  12 us
    all_to_all x1, starting transfers between devices, shards(): received = lax.all_to_all(send, 'ma', 0, 0, tiled=True)  11.6 us
    all_to_all x1, waiting for transfers between devices, shards(): back_rows = lax.all_to_all(mode_rows, 'ma', 0, 0, tiled=True)  8.47 us
    all_to_all x1, starting transfers between devices, shards(): back_rows = lax.all_to_all(mode_rows, 'ma', 0, 0, tiled=True)  6.03 us
  transfers between devices with their start and end apart: 2, of which 2 were waited for; matrix products, arithmetic and copies ran while one was open for 2% of the time, Pallas kernels for 0%

profile of v18, /device:TPU:1, one launch (start us, length us, event | category | flops | bytes accessed | tf_op | source)
XLA Modules:
  0.0 100.8 jit_solution(6444059541000976142)
XLA Ops:
  0.0 0.0 copy-start
  0.0 0.0 copy-start.1
  0.0 0.0 copy-start.2
  0.0 0.0 copy-start.3
  0.0 1.2 %reshape.129 = bf16[4,2,8,8,2,128]{5,4,3,2,1,0:T(2,128)(2,1)S(1)} reshape(bf16[4,2,8,2048]{3,2,1,0:T(8,128)(2,1)} %param.6) | data formatting | bytes 524288 | tf_op jit(solution)/shard_map/reshape | solution.py:375
  1.2 0.9 copy.21
  2.1 11.6 %all-to-all-start = ((bf16[64,16,128]{2,1,0:T(8,128)(2,1)}), bf16[64,16,128]{2,1,0:T(8,128)(2,1)S(1)}, u32[]{:S(2)}, u32[]{:S(2)}) async-start(bf16[64,16,128]{2,1,0:T(8,128)(2,1)} %copy.21), calls=%async_computation | async-start | bytes 524288 | tf_op jit(solution)/shard_map/all_to_all | solution.py:379
  13.7 12.0 %all-to-all-done = bf16[64,16,128]{2,1,0:T(8,128)(2,1)S(1)} async-done(((bf16[64,16,128]{2,1,0:T(8,128)(2,1)}), bf16[64,16,128]{2,1,0:T(8,128)(2,1)S(1)}, u32[]{:S(2)}, u32[]{:S(2)}) %all-to-all-start) | async-done | bytes 262176 | tf_op jit(solution)/shard_map/all_to_all | solution.py:379
  25.7 0.2 reshape.131
  25.9 0.5 convolution_bitcast_fusion
  26.4 0.5 fusion.1
  26.9 0.8 copy.24
  27.6 6.0 %all-to-all-start.1 = ((bf16[64,4,256]{2,1,0:T(4,128)(2,1)}), bf16[64,4,256]{2,1,0:T(4,128)(2,1)S(1)}, u32[]{:S(2)}, u32[]{:S(2)}) async-start(bf16[64,4,256]{2,1,0:T(4,128)(2,1)} %copy.24), calls=%async_computation.1 | async-start | bytes 262144 | tf_op jit(solution)/shard_map/all_to_all | solution.py:392
  33.7 0.0 copy-done
  33.7 0.0 copy-done.1
  33.7 0.6 broadcast_in_dim.17.pm_ref
  34.3 0.0 copy-done.2
  34.3 0.6 broadcast_in_dim.15.chroma_ref
  34.9 0.0 copy-done.3
  34.9 0.6 broadcast_in_dim.16.diag_ref
  35.5 8.5 %all-to-all-done.1 = bf16[64,4,256]{2,1,0:T(4,128)(2,1)S(1)} async-done(((bf16[64,4,256]{2,1,0:T(4,128)(2,1)}), bf16[64,4,256]{2,1,0:T(4,128)(2,1)S(1)}, u32[]{:S(2)}, u32[]{:S(2)}) %all-to-all-start.1) | async-done | bytes 131104 | tf_op jit(solution)/shard_map/all_to_all | solution.py:392
  44.0 0.1 copy.25
  44.1 0.7 multiply_convert_fusion.d_ref
  44.8 54.3 %shard_map.64 = (f32[4,8,896]{2,1,0:T(8,128)}, f32[4,8,896]{2,1,0:T(8,128)}, f32[1,128]{1,0:T(1,128)}) custom-call(bf16[4,8,2048]{2,1,0:T(8,128)(2,1)} %multiply_convert_fusion.d_ref, bf16[2048,896]{1,0:T(8,128)(2,1)} %bitcast.34, f32[4,1,896]{2,1,0:T(1,128)} %broadcast_in_dim.15.chroma_ref, f32[4,1,2048]{2,1,0:T(1,128)} %weight_ref.1, ...), custom_call_target="tpu_custom_call" | custom-call | tf_op jit(solution)/shard_map/pallas_call | solution.py:310
  99.1 1.7 %shard_map.65 = f32[4,8,896]{2,1,0:T(8,128)} custom-call(f32[4,8,896]{2,1,0:T(8,128)} %get-tuple-element.8.est_ref, f32[4,8,896]{2,1,0:T(8,128)} %get-tuple-element.9.direction_ref, f32[1,128]{1,0:T(1,128)} %get-tuple-element.10.step_ref), custom_call_target="tpu_custom_call" | custom-call | tf_op jit(solution)/shard_map/pallas_call | solution.py:329
  (3 shorter events, 0.1 us)
Async XLA Ops:
  0.0 33.7 %copy-start = (f32[4,1,2048]{2,1,0:T(1,128)S(1)}, f32[4,1,2048]{2,1,0:T(1,128)}, u32[]{:S(2)}) copy-start(f32[4,1,2048]{2,1,0:T(1,128)} %weight_ref.1) | copy-start | bytes 98308
  0.0 33.7 %copy-start.1 = (f32[4,2,896]{2,1,0:T(2,128)S(1)}, f32[4,2,896]{2,1,0:T(2,128)}, u32[]{:S(2)}) copy-start(f32[4,2,896]{2,1,0:T(2,128)} %param.11) | copy-start | bytes 86020
  0.0 34.3 %copy-start.2 = (f32[4,896]{1,0:T(4,128)S(1)}, f32[4,896]{1,0:T(4,128)}, u32[]{:S(2)}) copy-start(f32[4,896]{1,0:T(4,128)} %param.8) | copy-start | bytes 43012
  0.0 34.9 %copy-start.3 = (f32[4,896]{1,0:T(4,128)S(1)}, f32[4,896]{1,0:T(4,128)}, u32[]{:S(2)}) copy-start(f32[4,896]{1,0:T(4,128)} %param.10) | copy-start | bytes 43012
  2.1 23.6 %all-to-all-start = ((bf16[64,16,128]{2,1,0:T(8,128)(2,1)}), bf16[64,16,128]{2,1,0:T(8,128)(2,1)S(1)}, u32[]{:S(2)}, u32[]{:S(2)}) async-start(bf16[64,16,128]{2,1,0:T(8,128)(2,1)} %copy.21), calls=%async_computation | async-start | bytes 524288 | tf_op jit(solution)/shard_map/all_to_all | solution.py:379
  27.6 16.4 %all-to-all-start.1 = ((bf16[64,4,256]{2,1,0:T(4,128)(2,1)}), bf16[64,4,256]{2,1,0:T(4,128)(2,1)S(1)}, u32[]{:S(2)}, u32[]{:S(2)}) async-start(bf16[64,4,256]{2,1,0:T(4,128)(2,1)} %copy.24), calls=%async_computation.1 | async-start | bytes 262144 | tf_op jit(solution)/shard_map/all_to_all | solution.py:392

commit v19 on v16

--- a/solution.py
+++ b/solution.py
@@ -312,7 +312,7 @@
         out_specs=vmem,
         scratch_shapes=[
             pltpu.VMEM(beam.shape, beam.dtype),
-            pltpu.SemaphoreType.DMA((4,)),
+            pltpu.SemaphoreType.DMA((8,)),
             pltpu.VMEM((2,) + part_shape, jnp.bfloat16),
             pltpu.VMEM((rounds, 1, 128), jnp.float32),
             pltpu.VMEM((2 * nz,) + part_shape, jnp.bfloat16),

time: 101 us -> 101 us (level)
  no operation moved by 1% of the time
where the time goes in v19:
time: 101 us
  Pallas kernels  54.3 us (54%)
  waiting for transfers between devices  20.5 us (20%)
  starting transfers between devices  17.6 us (17%)
  local copies, waits for them, and re-layouts  6.52 us (6%)
    pallas_call x1, Pallas kernels, cg_solve(): pl.pallas_call(functools.partial(cg_kernel, axis_names, stages), out_shap...  54.3 us
    all_to_all x1, waiting for transfers between devices, shards(): received = lax.all_to_all(send, 'ma', 0, 0, tiled=True)  12 us
    all_to_all x1, starting transfers between devices, shards(): received = lax.all_to_all(send, 'ma', 0, 0, tiled=True)  11.6 us
    all_to_all x1, waiting for transfers between devices, shards(): back_rows = lax.all_to_all(mode_rows, 'ma', 0, 0, tiled=True)  8.47 us
    all_to_all x1, starting transfers between devices, shards(): back_rows = lax.all_to_all(mode_rows, 'ma', 0, 0, tiled=True)  6.03 us
  transfers between devices with their start and end apart: 2, of which 2 were waited for; matrix products, arithmetic and copies ran while one was open for 2% of the time, Pallas kernels for 0%

profile of v19, /device:TPU:1, one launch (start us, length us, event | category | flops | bytes accessed | tf_op | source)
XLA Modules:
  0.0 100.6 jit_solution(7492289696442729403)
XLA Ops:
  0.0 0.0 copy-start
  0.0 0.0 copy-start.1
  0.0 0.0 copy-start.2
  0.0 0.0 copy-start.3
  0.0 1.2 %reshape.129 = bf16[4,2,8,8,2,128]{5,4,3,2,1,0:T(2,128)(2,1)S(1)} reshape(bf16[4,2,8,2048]{3,2,1,0:T(8,128)(2,1)} %param.6) | data formatting | bytes 524288 | tf_op jit(solution)/shard_map/reshape | solution.py:361
  1.2 0.9 copy.21
  2.1 11.6 %all-to-all-start = ((bf16[64,16,128]{2,1,0:T(8,128)(2,1)}), bf16[64,16,128]{2,1,0:T(8,128)(2,1)S(1)}, u32[]{:S(2)}, u32[]{:S(2)}) async-start(bf16[64,16,128]{2,1,0:T(8,128)(2,1)} %copy.21), calls=%async_computation | async-start | bytes 524288 | tf_op jit(solution)/shard_map/all_to_all | solution.py:365
  13.7 12.0 %all-to-all-done = bf16[64,16,128]{2,1,0:T(8,128)(2,1)S(1)} async-done(((bf16[64,16,128]{2,1,0:T(8,128)(2,1)}), bf16[64,16,128]{2,1,0:T(8,128)(2,1)S(1)}, u32[]{:S(2)}, u32[]{:S(2)}) %all-to-all-start) | async-done | bytes 262176 | tf_op jit(solution)/shard_map/all_to_all | solution.py:365
  25.7 0.2 reshape.131
  25.9 0.5 convolution_bitcast_fusion
  26.4 0.5 fusion.1
  26.9 0.8 copy.24
  27.6 6.0 %all-to-all-start.1 = ((bf16[64,4,256]{2,1,0:T(4,128)(2,1)}), bf16[64,4,256]{2,1,0:T(4,128)(2,1)S(1)}, u32[]{:S(2)}, u32[]{:S(2)}) async-start(bf16[64,4,256]{2,1,0:T(4,128)(2,1)} %copy.24), calls=%async_computation.1 | async-start | bytes 262144 | tf_op jit(solution)/shard_map/all_to_all | solution.py:378
  33.7 0.0 copy-done
  33.7 0.0 copy-done.1
  33.7 0.6 broadcast_in_dim.17.pm_ref
  34.3 0.0 copy-done.2
  34.3 0.6 broadcast_in_dim.15.chroma_ref
  34.9 0.0 copy-done.3
  34.9 0.6 broadcast_in_dim.16.diag_ref
  35.5 8.5 %all-to-all-done.1 = bf16[64,4,256]{2,1,0:T(4,128)(2,1)S(1)} async-done(((bf16[64,4,256]{2,1,0:T(4,128)(2,1)}), bf16[64,4,256]{2,1,0:T(4,128)(2,1)S(1)}, u32[]{:S(2)}, u32[]{:S(2)}) %all-to-all-start.1) | async-done | bytes 131104 | tf_op jit(solution)/shard_map/all_to_all | solution.py:378
  44.0 0.1 copy.25
  44.1 0.7 multiply_convert_fusion.d_ref
  44.8 54.3 %shard_map.64 = f32[4,8,896]{2,1,0:T(8,128)} custom-call(bf16[4,8,2048]{2,1,0:T(8,128)(2,1)} %multiply_convert_fusion.d_ref, bf16[2048,896]{1,0:T(8,128)(2,1)} %bitcast.34, f32[4,1,896]{2,1,0:T(1,128)} %broadcast_in_dim.15.chroma_ref, f32[4,1,2048]{2,1,0:T(1,128)} %weight_ref.1, f32[4,1,896]{2,1,0:T(1,128)} %broadcast_in_dim.16.diag_ref, ...), custom_call_target="tpu_custom_call" | custom-call | tf_op jit(solution)/shard_map/pallas_call | solution.py:308
  99.1 1.6 %copy.37 = f32[4,1,8,896]{3,2,1,0:T(8,128)} copy(f32[4,1,8,896]{3,2,1,0:T(8,128)} %bitcast.39) | data formatting | bytes 229376
  (3 shorter events, 0.1 us)
Async XLA Ops:
  0.0 33.7 %copy-start = (f32[4,1,2048]{2,1,0:T(1,128)S(1)}, f32[4,1,2048]{2,1,0:T(1,128)}, u32[]{:S(2)}) copy-start(f32[4,1,2048]{2,1,0:T(1,128)} %weight_ref.1) | copy-start | bytes 98308
  0.0 33.7 %copy-start.1 = (f32[4,2,896]{2,1,0:T(2,128)S(1)}, f32[4,2,896]{2,1,0:T(2,128)}, u32[]{:S(2)}) copy-start(f32[4,2,896]{2,1,0:T(2,128)} %param.11) | copy-start | bytes 86020
  0.0 34.3 %copy-start.2 = (f32[4,896]{1,0:T(4,128)S(1)}, f32[4,896]{1,0:T(4,128)}, u32[]{:S(2)}) copy-start(f32[4,896]{1,0:T(4,128)} %param.8) | copy-start | bytes 43012
  0.0 34.9 %copy-start.3 = (f32[4,896]{1,0:T(4,128)S(1)}, f32[4,896]{1,0:T(4,128)}, u32[]{:S(2)}) copy-start(f32[4,896]{1,0:T(4,128)} %param.10) | copy-start | bytes 43012
  2.1 23.6 %all-to-all-start = ((bf16[64,16,128]{2,1,0:T(8,128)(2,1)}), bf16[64,16,128]{2,1,0:T(8,128)(2,1)S(1)}, u32[]{:S(2)}, u32[]{:S(2)}) async-start(bf16[64,16,128]{2,1,0:T(8,128)(2,1)} %copy.21), calls=%async_computation | async-start | bytes 524288 | tf_op jit(solution)/shard_map/all_to_all | solution.py:365
  27.6 16.4 %all-to-all-start.1 = ((bf16[64,4,256]{2,1,0:T(4,128)(2,1)}), bf16[64,4,256]{2,1,0:T(4,128)(2,1)S(1)}, u32[]{:S(2)}, u32[]{:S(2)}) async-start(bf16[64,4,256]{2,1,0:T(4,128)(2,1)} %copy.24), calls=%async_computation.1 | async-start | bytes 262144 | tf_op jit(solution)/shard_map/all_to_all | solution.py:378

commit v20 on v16

--- a/solution.py
+++ b/solution.py
@@ -393,8 +393,8 @@
         if mode_devices % 16 == 0:
             cg_stages = [
                 ("freq", [(1, freq_devices)]),
+                ("ma", [(2, 8)]),
                 ("ma", [(1, 2), (16, mode_devices // 16)]),
-                ("ma", [(2, 8)]),
             ]
         else:
             cg_stages = [("freq", [(1, freq_devices)]), ("ma", [(1, mode_devices)])]

time: 101 us -> 102 us (level)
  no operation moved by 1% of the time
where the time goes in v20:
time: 102 us; the launch traced here: 101 us
  Pallas kernels  54.8 us (54%)
  waiting for transfers between devices  20.5 us (20%)
  starting transfers between devices  17.6 us (17%)
  local copies, waits for them, and re-layouts  6.52 us (6%)
    pallas_call x1, Pallas kernels, cg_solve(): pl.pallas_call(functools.partial(cg_kernel, axis_names, stages), out_shap...  54.8 us
    all_to_all x1, waiting for transfers between devices, shards(): received = lax.all_to_all(send, 'ma', 0, 0, tiled=True)  12 us
    all_to_all x1, starting transfers between devices, shards(): received = lax.all_to_all(send, 'ma', 0, 0, tiled=True)  11.6 us
    all_to_all x1, waiting for transfers between devices, shards(): back_rows = lax.all_to_all(mode_rows, 'ma', 0, 0, tiled=True)  8.47 us
    all_to_all x1, starting transfers between devices, shards(): back_rows = lax.all_to_all(mode_rows, 'ma', 0, 0, tiled=True)  6.03 us
  transfers between devices with their start and end apart: 2, of which 2 were waited for; matrix products, arithmetic and copies ran while one was open for 2% of the time, Pallas kernels for 0%

profile of v20, /device:TPU:1, one launch (start us, length us, event | category | flops | bytes accessed | tf_op | source)
XLA Modules:
  0.0 101.2 jit_solution(17178849344249727642)
XLA Ops:
  0.0 0.0 copy-start
  0.0 0.0 copy-start.1
  0.0 0.0 copy-start.2
  0.0 0.0 copy-start.3
  0.0 1.2 %reshape.129 = bf16[4,2,8,8,2,128]{5,4,3,2,1,0:T(2,128)(2,1)S(1)} reshape(bf16[4,2,8,2048]{3,2,1,0:T(8,128)(2,1)} %param.6) | data formatting | bytes 524288 | tf_op jit(solution)/shard_map/reshape | solution.py:361
  1.2 0.9 copy.21
  2.1 11.6 %all-to-all-start = ((bf16[64,16,128]{2,1,0:T(8,128)(2,1)}), bf16[64,16,128]{2,1,0:T(8,128)(2,1)S(1)}, u32[]{:S(2)}, u32[]{:S(2)}) async-start(bf16[64,16,128]{2,1,0:T(8,128)(2,1)} %copy.21), calls=%async_computation | async-start | bytes 524288 | tf_op jit(solution)/shard_map/all_to_all | solution.py:365
  13.7 12.0 %all-to-all-done = bf16[64,16,128]{2,1,0:T(8,128)(2,1)S(1)} async-done(((bf16[64,16,128]{2,1,0:T(8,128)(2,1)}), bf16[64,16,128]{2,1,0:T(8,128)(2,1)S(1)}, u32[]{:S(2)}, u32[]{:S(2)}) %all-to-all-start) | async-done | bytes 262176 | tf_op jit(solution)/shard_map/all_to_all | solution.py:365
  25.7 0.2 reshape.131
  25.9 0.5 convolution_bitcast_fusion
  26.4 0.5 fusion.1
  26.9 0.8 copy.24
  27.6 6.0 %all-to-all-start.1 = ((bf16[64,4,256]{2,1,0:T(4,128)(2,1)}), bf16[64,4,256]{2,1,0:T(4,128)(2,1)S(1)}, u32[]{:S(2)}, u32[]{:S(2)}) async-start(bf16[64,4,256]{2,1,0:T(4,128)(2,1)} %copy.24), calls=%async_computation.1 | async-start | bytes 262144 | tf_op jit(solution)/shard_map/all_to_all | solution.py:378
  33.7 0.0 copy-done
  33.7 0.0 copy-done.1
  33.7 0.6 broadcast_in_dim.17.pm_ref
  34.3 0.0 copy-done.2
  34.3 0.6 broadcast_in_dim.15.chroma_ref
  34.9 0.0 copy-done.3
  34.9 0.6 broadcast_in_dim.16.diag_ref
  35.5 8.5 %all-to-all-done.1 = bf16[64,4,256]{2,1,0:T(4,128)(2,1)S(1)} async-done(((bf16[64,4,256]{2,1,0:T(4,128)(2,1)}), bf16[64,4,256]{2,1,0:T(4,128)(2,1)S(1)}, u32[]{:S(2)}, u32[]{:S(2)}) %all-to-all-start.1) | async-done | bytes 131104 | tf_op jit(solution)/shard_map/all_to_all | solution.py:378
  44.0 0.1 copy.25
  44.1 0.7 multiply_convert_fusion.d_ref
  44.8 54.8 %shard_map.64 = f32[4,8,896]{2,1,0:T(8,128)} custom-call(bf16[4,8,2048]{2,1,0:T(8,128)(2,1)} %multiply_convert_fusion.d_ref, bf16[2048,896]{1,0:T(8,128)(2,1)} %bitcast.34, f32[4,1,896]{2,1,0:T(1,128)} %broadcast_in_dim.15.chroma_ref, f32[4,1,2048]{2,1,0:T(1,128)} %weight_ref.1, f32[4,1,896]{2,1,0:T(1,128)} %broadcast_in_dim.16.diag_ref, ...), custom_call_target="tpu_custom_call" | custom-call | tf_op jit(solution)/shard_map/pallas_call | solution.py:308
  99.6 1.6 %copy.37 = f32[4,1,8,896]{3,2,1,0:T(8,128)} copy(f32[4,1,8,896]{3,2,1,0:T(8,128)} %bitcast.39) | data formatting | bytes 229376
  (3 shorter events, 0.1 us)
Async XLA Ops:
  0.0 33.7 %copy-start = (f32[4,1,2048]{2,1,0:T(1,128)S(1)}, f32[4,1,2048]{2,1,0:T(1,128)}, u32[]{:S(2)}) copy-start(f32[4,1,2048]{2,1,0:T(1,128)} %weight_ref.1) | copy-start | bytes 98308
  0.0 33.7 %copy-start.1 = (f32[4,2,896]{2,1,0:T(2,128)S(1)}, f32[4,2,896]{2,1,0:T(2,128)}, u32[]{:S(2)}) copy-start(f32[4,2,896]{2,1,0:T(2,128)} %param.11) | copy-start | bytes 86020
  0.0 34.3 %copy-start.2 = (f32[4,896]{1,0:T(4,128)S(1)}, f32[4,896]{1,0:T(4,128)}, u32[]{:S(2)}) copy-start(f32[4,896]{1,0:T(4,128)} %param.8) | copy-start | bytes 43012
  0.0 34.9 %copy-start.3 = (f32[4,896]{1,0:T(4,128)S(1)}, f32[4,896]{1,0:T(4,128)}, u32[]{:S(2)}) copy-start(f32[4,896]{1,0:T(4,128)} %param.10) | copy-start | bytes 43012
  2.1 23.6 %all-to-all-start = ((bf16[64,16,128]{2,1,0:T(8,128)(2,1)}), bf16[64,16,128]{2,1,0:T(8,128)(2,1)S(1)}, u32[]{:S(2)}, u32[]{:S(2)}) async-start(bf16[64,16,128]{2,1,0:T(8,128)(2,1)} %copy.21), calls=%async_computation | async-start | bytes 524288 | tf_op jit(solution)/shard_map/all_to_all | solution.py:365
  27.6 16.4 %all-to-all-start.1 = ((bf16[64,4,256]{2,1,0:T(4,128)(2,1)}), bf16[64,4,256]{2,1,0:T(4,128)(2,1)S(1)}, u32[]{:S(2)}, u32[]{:S(2)}) async-start(bf16[64,4,256]{2,1,0:T(4,128)(2,1)} %copy.24), calls=%async_computation.1 | async-start | bytes 262144 | tf_op jit(solution)/shard_map/all_to_all | solution.py:378

commit v21 on v20

--- a/solution.py
+++ b/solution.py
@@ -393,8 +393,8 @@
         if mode_devices % 16 == 0:
             cg_stages = [
                 ("freq", [(1, freq_devices)]),
-                ("ma", [(2, 8)]),
-                ("ma", [(1, 2), (16, mode_devices // 16)]),
+                ("ma", [(1, 2), (2, 8)]),
+                ("ma", [(16, mode_devices // 16)]),
             ]
         else:
             cg_stages = [("freq", [(1, freq_devices)]), ("ma", [(1, mode_devices)])]

time: 102 us -> 101 us (level)
  no operation moved by 1% of the time
where the time goes in v21:
time: 101 us
  Pallas kernels  54.7 us (54%)
  waiting for transfers between devices  20.5 us (20%)
  starting transfers between devices  17.6 us (17%)
  local copies, waits for them, and re-layouts  6.52 us (6%)
    pallas_call x1, Pallas kernels, cg_solve(): pl.pallas_call(functools.partial(cg_kernel, axis_names, stages), out_shap...  54.7 us
    all_to_all x1, waiting for transfers between devices, shards(): received = lax.all_to_all(send, 'ma', 0, 0, tiled=True)  12 us
    all_to_all x1, starting transfers between devices, shards(): received = lax.all_to_all(send, 'ma', 0, 0, tiled=True)  11.6 us
    all_to_all x1, waiting for transfers between devices, shards(): back_rows = lax.all_to_all(mode_rows, 'ma', 0, 0, tiled=True)  8.47 us
    all_to_all x1, starting transfers between devices, shards(): back_rows = lax.all_to_all(mode_rows, 'ma', 0, 0, tiled=True)  6.03 us
  transfers between devices with their start and end apart: 2, of which 2 were waited for; matrix products, arithmetic and copies ran while one was open for 2% of the time, Pallas kernels for 0%

profile of v21, /device:TPU:1, one launch (start us, length us, event | category | flops | bytes accessed | tf_op | source)
XLA Modules:
  0.0 101.1 jit_solution(6862838788442204795)
XLA Ops:
  0.0 0.0 copy-start
  0.0 0.0 copy-start.1
  0.0 0.0 copy-start.2
  0.0 0.0 copy-start.3
  0.0 1.2 %reshape.129 = bf16[4,2,8,8,2,128]{5,4,3,2,1,0:T(2,128)(2,1)S(1)} reshape(bf16[4,2,8,2048]{3,2,1,0:T(8,128)(2,1)} %param.6) | data formatting | bytes 524288 | tf_op jit(solution)/shard_map/reshape | solution.py:361
  1.2 0.9 copy.21
  2.1 11.6 %all-to-all-start = ((bf16[64,16,128]{2,1,0:T(8,128)(2,1)}), bf16[64,16,128]{2,1,0:T(8,128)(2,1)S(1)}, u32[]{:S(2)}, u32[]{:S(2)}) async-start(bf16[64,16,128]{2,1,0:T(8,128)(2,1)} %copy.21), calls=%async_computation | async-start | bytes 524288 | tf_op jit(solution)/shard_map/all_to_all | solution.py:365
  13.7 12.0 %all-to-all-done = bf16[64,16,128]{2,1,0:T(8,128)(2,1)S(1)} async-done(((bf16[64,16,128]{2,1,0:T(8,128)(2,1)}), bf16[64,16,128]{2,1,0:T(8,128)(2,1)S(1)}, u32[]{:S(2)}, u32[]{:S(2)}) %all-to-all-start) | async-done | bytes 262176 | tf_op jit(solution)/shard_map/all_to_all | solution.py:365
  25.7 0.2 reshape.131
  25.9 0.5 convolution_bitcast_fusion
  26.4 0.5 fusion.1
  26.9 0.8 copy.24
  27.6 6.0 %all-to-all-start.1 = ((bf16[64,4,256]{2,1,0:T(4,128)(2,1)}), bf16[64,4,256]{2,1,0:T(4,128)(2,1)S(1)}, u32[]{:S(2)}, u32[]{:S(2)}) async-start(bf16[64,4,256]{2,1,0:T(4,128)(2,1)} %copy.24), calls=%async_computation.1 | async-start | bytes 262144 | tf_op jit(solution)/shard_map/all_to_all | solution.py:378
  33.7 0.0 copy-done
  33.7 0.0 copy-done.1
  33.7 0.6 broadcast_in_dim.17.pm_ref
  34.3 0.0 copy-done.2
  34.3 0.6 broadcast_in_dim.15.chroma_ref
  34.9 0.0 copy-done.3
  34.9 0.6 broadcast_in_dim.16.diag_ref
  35.5 8.5 %all-to-all-done.1 = bf16[64,4,256]{2,1,0:T(4,128)(2,1)S(1)} async-done(((bf16[64,4,256]{2,1,0:T(4,128)(2,1)}), bf16[64,4,256]{2,1,0:T(4,128)(2,1)S(1)}, u32[]{:S(2)}, u32[]{:S(2)}) %all-to-all-start.1) | async-done | bytes 131104 | tf_op jit(solution)/shard_map/all_to_all | solution.py:378
  44.0 0.1 copy.25
  44.1 0.7 multiply_convert_fusion.d_ref
  44.8 54.7 %shard_map.64 = f32[4,8,896]{2,1,0:T(8,128)} custom-call(bf16[4,8,2048]{2,1,0:T(8,128)(2,1)} %multiply_convert_fusion.d_ref, bf16[2048,896]{1,0:T(8,128)(2,1)} %bitcast.34, f32[4,1,896]{2,1,0:T(1,128)} %broadcast_in_dim.15.chroma_ref, f32[4,1,2048]{2,1,0:T(1,128)} %weight_ref.1, f32[4,1,896]{2,1,0:T(1,128)} %broadcast_in_dim.16.diag_ref, ...), custom_call_target="tpu_custom_call" | custom-call | tf_op jit(solution)/shard_map/pallas_call | solution.py:308
  99.5 1.6 %copy.37 = f32[4,1,8,896]{3,2,1,0:T(8,128)} copy(f32[4,1,8,896]{3,2,1,0:T(8,128)} %bitcast.39) | data formatting | bytes 229376
  (3 shorter events, 0.1 us)
Async XLA Ops:
  0.0 33.7 %copy-start = (f32[4,1,2048]{2,1,0:T(1,128)S(1)}, f32[4,1,2048]{2,1,0:T(1,128)}, u32[]{:S(2)}) copy-start(f32[4,1,2048]{2,1,0:T(1,128)} %weight_ref.1) | copy-start | bytes 98308
  0.0 33.7 %copy-start.1 = (f32[4,2,896]{2,1,0:T(2,128)S(1)}, f32[4,2,896]{2,1,0:T(2,128)}, u32[]{:S(2)}) copy-start(f32[4,2,896]{2,1,0:T(2,128)} %param.11) | copy-start | bytes 86020
  0.0 34.3 %copy-start.2 = (f32[4,896]{1,0:T(4,128)S(1)}, f32[4,896]{1,0:T(4,128)}, u32[]{:S(2)}) copy-start(f32[4,896]{1,0:T(4,128)} %param.8) | copy-start | bytes 43012
  0.0 34.9 %copy-start.3 = (f32[4,896]{1,0:T(4,128)S(1)}, f32[4,896]{1,0:T(4,128)}, u32[]{:S(2)}) copy-start(f32[4,896]{1,0:T(4,128)} %param.10) | copy-start | bytes 43012
  2.1 23.6 %all-to-all-start = ((bf16[64,16,128]{2,1,0:T(8,128)(2,1)}), bf16[64,16,128]{2,1,0:T(8,128)(2,1)S(1)}, u32[]{:S(2)}, u32[]{:S(2)}) async-start(bf16[64,16,128]{2,1,0:T(8,128)(2,1)} %copy.21), calls=%async_computation | async-start | bytes 524288 | tf_op jit(solution)/shard_map/all_to_all | solution.py:365
  27.6 16.4 %all-to-all-start.1 = ((bf16[64,4,256]{2,1,0:T(4,128)(2,1)}), bf16[64,4,256]{2,1,0:T(4,128)(2,1)S(1)}, u32[]{:S(2)}, u32[]{:S(2)}) async-start(bf16[64,4,256]{2,1,0:T(4,128)(2,1)} %copy.24), calls=%async_computation.1 | async-start | bytes 262144 | tf_op jit(solution)/shard_map/all_to_all | solution.py:378
